TPU v7x, 128 devices: a whole 4x4x4 slice. The times are simulated.
128 devices in a mesh: wide: 64 (over y, x, z), narrow: 2 (over core).
Axes of the slice: x: 4, y: 4, z: 4, core: 2. Of those that a mesh axis runs over, the one named last changes fastest.
Arguments:
- hidden_in: bfloat16 [8192, 4096], P('wide'), may hold values from -6 to 6
- readout: bfloat16 [8192, 4096], P('wide'), may hold values from -0.09375 to 0.09375
- route_ids: int32 [8192, 8], P('wide'), may hold values from 0 to 63, all different within a row; in each aligned block of 128 rows (0 to 127, 128 to 255, ...) at most 24 rows name the same one
- route_weights: bfloat16 [8192, 8], P('wide'), may hold values from 0.25 to 1
- forget_mask: int32 [8192], P('wide'), may hold values 0 or 1
- gate_proj: bfloat16 [64, 4096, 1536], P('wide', None, 'narrow'), may hold values from -0.09375 to 0.09375
- up_proj: bfloat16 [64, 4096, 1536], P('wide', None, 'narrow'), may hold values from -0.09375 to 0.09375
- adapter_a: bfloat16 [64, 16, 1536], P('wide', None, 'narrow'), may hold values from -0.15625 to 0.15625
- adapter_b: bfloat16 [64, 16, 4096], P('wide'), may hold values from -1.5 to 1.5
Outputs:
- log_ratio: float32 [8192], P('wide')
- grad_a: float32 [64, 16, 1536], P('wide', None, 'narrow')
- grad_b: float32 [64, 16, 4096], P('wide')
Inputs may be any that keep to these rules, and one draw needn't show every extreme that they name: `route_ids`: each token names 8 different experts. Among the 128 tokens of one index of wide no expert is named by more than 24 tokens, and in some such blocks one expert is named by exactly 24.
All inputs are finite; a program needn't handle non-finite values. No bound on the sum of `forget_mask` on one device may be relied on, other than what follows from the above.
Results may differ from a plain program's by a relative error of at most 0.027.
Values may be sent and summed in bfloat16 or wider, within the bound.
No kernel may reach another device: no remote copies, remote signals or barrier semaphores. Data moves between devices by JAX's collectives and lax.ppermute only.
A program may use at most 192 MiB of HBM per device.

v0:
```python
import jax
import jax.numpy as jnp
from jax import lax
from jax.sharding import PartitionSpec as P


def slot_tables(block_ids, experts, capacity):
    total = block_ids.shape[0]
    matches = (block_ids[:, None] == jnp.arange(experts, dtype=jnp.int32)[None, :]).astype(
        jnp.int32
    )
    earlier = jnp.cumsum(matches, axis=0) - matches
    slot_rank = jnp.sum(earlier * matches, axis=1)
    slot_place = block_ids * capacity + slot_rank
    slot_owner = (
        jnp.full((experts * capacity,), -1, dtype=jnp.int32)
        .at[slot_place]
        .set(jnp.arange(total, dtype=jnp.int32))
    )
    return (slot_place, slot_owner)


def to_experts(payload):
    groups = payload.shape[0]
    half_cap = payload.shape[1]
    trailing = payload.shape[2:]
    pairs = lax.axis_size("narrow")
    doubled = jnp.broadcast_to(payload[:, None], (groups, pairs) + payload.shape[1:]).reshape(
        (groups * pairs,) + payload.shape[1:]
    )
    arrived = lax.all_to_all(doubled, ("wide", "narrow"), split_axis=0, concat_axis=0, tiled=True)
    result = arrived.reshape((groups, pairs * half_cap) + trailing)
    return result


def to_homes(payload, pair_index):
    groups = payload.shape[0]
    pairs = lax.axis_size("narrow")
    half_cap = payload.shape[1] // pairs
    trailing = payload.shape[2:]
    own_half = lax.dynamic_slice_in_dim(payload, pair_index * half_cap, half_cap, 1)
    doubled = jnp.broadcast_to(own_half[:, None], (groups, pairs) + own_half.shape[1:]).reshape(
        (groups * pairs,) + own_half.shape[1:]
    )
    arrived = lax.all_to_all(doubled, ("wide", "narrow"), split_axis=0, concat_axis=0, tiled=True)
    result = arrived.reshape((groups, pairs * half_cap) + trailing)
    return result


def on_device(
    hidden_in,
    readout,
    route_ids,
    route_weights,
    forget_mask,
    gate_proj,
    up_proj,
    adapter_a,
    adapter_b,
):
    groups = lax.axis_size("wide")
    pairs = lax.axis_size("narrow")
    tok_count = route_ids.shape[0]
    picks = route_ids.shape[1]
    features = hidden_in.shape[1]
    capacity = 3 * tok_count * picks // (2 * groups)
    half_cap = capacity // pairs
    pair_index = lax.axis_index("narrow")
    slot_place, slot_owner = slot_tables(route_ids.reshape(-1), groups, capacity)
    own_slots = lax.dynamic_slice_in_dim(
        slot_owner.reshape(groups, capacity), pair_index * half_cap, half_cap, 1
    )
    filled = own_slots >= 0
    safe_slots = jnp.maximum(own_slots, 0)
    token_of = safe_slots // picks
    zero_value = jnp.zeros((), jnp.bfloat16)
    token_rows = jnp.where(filled[..., None], hidden_in[token_of], zero_value)
    expert_rows = to_experts(token_rows).reshape(-1, features)
    pre_gate = jnp.dot(expert_rows, gate_proj[0], preferred_element_type=jnp.float32)
    pre_up = jnp.dot(expert_rows, up_proj[0], preferred_element_type=jnp.float32)
    expert_hidden = (jax.nn.silu(pre_gate) * pre_up).astype(jnp.bfloat16)
    partial_latent = lax.dot_general(
        expert_hidden, adapter_a[0], (((1,), (1,)), ((), ())), preferred_element_type=jnp.float32
    )
    latent = lax.psum(partial_latent.astype(jnp.bfloat16), "narrow")
    deltas = jnp.dot(latent, adapter_b[0], preferred_element_type=jnp.float32).astype(jnp.bfloat16)
    home_deltas = to_homes(deltas.reshape(groups, capacity, features), pair_index)
    picked = home_deltas.reshape(-1, features)[slot_place].reshape(tok_count, picks, features)
    scores = jnp.einsum("tkd,td->tk", picked, readout, preferred_element_type=jnp.float32).astype(
        jnp.bfloat16
    )
    gains = route_weights.astype(jnp.float32)
    log_ratio = jnp.sum(gains * scores.astype(jnp.float32), axis=1)
    coefficient = 2.0 * forget_mask.astype(jnp.float32) * jax.nn.sigmoid(log_ratio)
    slot_weight = (gains * coefficient[:, None]).astype(jnp.bfloat16).reshape(-1)
    own_weight = jnp.where(filled, slot_weight[safe_slots], zero_value)
    cot_rows = (
        own_weight.astype(jnp.float32)[..., None] * readout[token_of].astype(jnp.float32)
    ).astype(jnp.bfloat16)
    slot_cot = to_experts(cot_rows).reshape(-1, features)
    grad_b = lax.dot_general(
        latent, slot_cot, (((0,), (0,)), ((), ())), preferred_element_type=jnp.float32
    )
    back_latent = lax.dot_general(
        slot_cot, adapter_b[0], (((1,), (1,)), ((), ())), preferred_element_type=jnp.float32
    ).astype(jnp.bfloat16)
    grad_a = lax.dot_general(
        back_latent, expert_hidden, (((0,), (0,)), ((), ())), preferred_element_type=jnp.float32
    )
    return (log_ratio, grad_a[None], grad_b[None])


def solution(mesh):
    return jax.shard_map(
        on_device,
        mesh=mesh,
        in_specs=(
            P("wide", None),
            P("wide", None),
            P("wide", None),
            P("wide", None),
            P("wide"),
            P("wide", None, "narrow"),
            P("wide", None, "narrow"),
            P("wide", None, "narrow"),
            P("wide", None, None),
        ),
        out_specs=(P("wide"), P("wide", None, "narrow"), P("wide", None, None)),
        check_vma=False,
    )
```

profile of v0, /device:TPU:1, one launch (start us, length us, event | category | flops | bytes accessed | tf_op | source)
XLA Modules:
  0.0 867.2 jit_solution(14991775274755730724)
XLA Ops:
  0.7 0.9 copy.13
  1.6 0.1 eq.29
  1.7 0.1 eq.25
  1.8 0.7 broadcast_multiply_fusion
  2.5 18.0 %reduce-window.6 = s32[64,8,128]{2,1,0:T(8,128)S(1)} reduce-window(s32[64,8,128]{2,1,0:T(8,128)S(1)} %fusion.14, s32[]{:T(128)} %constant.19.clone.1), window={size=1x1x128 pad=0_0x0_0x127_0}, to_apply=%region_0.0 | reduce-window | flops 8323072 | bytes 524292 | tf_op jit(solution)/shard_map/reduce-window
  20.5 0.1 slice.16
  20.6 0.1 copy.15
  20.8 0.1 copy.16
  20.9 0.1 broadcast_add_fusion
  21.1 0.1 copy.12
  21.2 0.1 mul.64
  21.4 4.3 scatter_custom_fusion
  25.7 0.1 reshape.86
  25.8 0.1 compare_select_fusion
  25.9 0.1 dynamic-slice_compare_fusion
  26.0 0.1 reshape.95
  26.1 5.8 gather_fusion
  31.9 9.8 %reshape.94 = bf16[64,12,4096]{2,1,0:T(8,128)(2,1)} reshape(bf16[768,4096]{1,0:T(8,128)(2,1)} %gather_fusion) | data formatting | bytes 12582912 | tf_op jit(solution)/shard_map/gather | solution.py:77
  41.7 7.2 broadcast_select_fusion
  48.9 6.4 broadcast_in_dim.60
  55.4 201.1 %all_to_all.15 = bf16[128,12,4096]{2,1,0:T(8,128)(2,1)} all-to-all(bf16[128,12,4096]{2,1,0:T(8,128)(2,1)S(1)} %bitcast.63), channel_id=1, replica_groups=mesh['wide'=64,'narrow'=2] {'wide','narrow'}, dimensions={0} | all-to-all | bytes 25165824 | tf_op jit(solution)/shard_map/all_to_all | solution.py:31
  256.5 18.2 %reshape_reshape.9 = bf16[1536,4096]{1,0:T(8,128)(2,1)} reshape(bf16[128,12,4096]{2,1,0:T(8,128)(2,1)} %all_to_all.15) | data formatting | bytes 25165824 | tf_op jit(solution)/shard_map/reshape;reshape | solution.py:78
  274.7 14.0 %fusion.2 = f32[1536,768]{1,0:T(8,128)S(1)} fusion(bf16[1536,4096]{1,0:T(8,128)(2,1)} %reshape_reshape.9, bf16[1,4096,768]{2,1,0:T(8,128)(2,1)} %param.15), kind=kOutput, calls=%fused_computation.10 | convolution fusion | flops 9663676416 | bytes 23592960 | tf_op jit(solution)/shard_map/dot_general | solution.py:80
  288.7 13.0 %multiply_convert_fusion.1 = bf16[1536,768]{1,0:T(8,128)(2,1)S(1)} fusion(f32[1536,768]{1,0:T(8,128)S(1)} %fusion.2, bf16[1536,4096]{1,0:T(8,128)(2,1)S(1)} %copy-done.2, bf16[1,4096,768]{2,1,0:T(8,128)(2,1)} %param.14), kind=kOutput, calls=%fused_computation.14 | convolution fusion | flops 9670754304 | bytes 25952256 | tf_op jit(solution)/shard_map/dot_general | solution.py:79
  301.7 0.7 convolution_convert_fusion.2
  302.4 3.9 psum.7
  306.4 7.3 convolution_convert_fusion
  313.7 11.1 %constant_dynamic-slice_fusion = bf16[64,12,4096]{2,1,0:T(8,128)(2,1)} fusion(bf16[64,24,4096]{2,1,0:T(8,128)(2,1)} %bitcast.65, s32[]{:T(128)S(6)} %select_n.38), kind=kLoop, calls=%fused_computation.53 | loop fusion | bytes 12582916 | tf_op jit(solution)/shard_map/dynamic_slice | solution.py:41
  324.7 10.7 %broadcast_in_dim.61 = bf16[64,2,12,4096]{3,2,1,0:T(8,128)(2,1)} broadcast(bf16[64,12,4096]{2,1,0:T(8,128)(2,1)} %constant_dynamic-slice_fusion), dimensions={0,2,3} | broadcast | bytes 18874368 | tf_op jit(solution)/shard_map/broadcast_in_dim | solution.py:42
  335.4 10.5 %all-to-all-start.1 = ((bf16[128,12,4096]{2,1,0:T(8,128)(2,1)}), bf16[128,12,4096]{2,1,0:T(8,128)(2,1)}, u32[]{:S(2)}, u32[]{:S(2)}) async-start(bf16[128,12,4096]{2,1,0:T(8,128)(2,1)} %bitcast.62), calls=%async_computation.1 | async-start | bytes 33554432 | tf_op jit(solution)/shard_map/all_to_all | solution.py:45
  346.0 0.1 reshape.111
  346.1 5.6 gather_fusion.3
  351.7 10.6 %reshape.139 = f32[64,12,4096]{2,1,0:T(8,128)} reshape(bf16[768,4096]{1,0:T(8,128)(2,1)} %gather_fusion.3) | data formatting | bytes 18874368 | tf_op jit(solution)/shard_map/convert_element_type | solution.py:98
  362.4 207.5 %all-to-all-done.1 = bf16[128,12,4096]{2,1,0:T(8,128)(2,1)} async-done(((bf16[128,12,4096]{2,1,0:T(8,128)(2,1)}), bf16[128,12,4096]{2,1,0:T(8,128)(2,1)}, u32[]{:S(2)}, u32[]{:S(2)}) %all-to-all-start.1) | async-done | bytes 12582944 | tf_op jit(solution)/shard_map/all_to_all | solution.py:45
  569.8 18.1 %reshape_reshape.10 = bf16[1536,4096]{1,0:T(8,128)(2,1)} reshape(bf16[128,12,4096]{2,1,0:T(8,128)(2,1)} %all-to-all-done.1) | data formatting | bytes 25165824 | tf_op jit(solution)/shard_map/reshape;reshape | solution.py:88
  587.9 21.3 %gather_fusion.1 = bf16[1024,4096]{1,0:T(8,128)(2,1)} fusion(bf16[1536,4096]{1,0:T(8,128)(2,1)} %reshape_reshape.10, s32[1024]{0:T(1024)S(1)} %broadcast_clamp_fusion), kind=kCustom, calls=%fused_computation.1 | custom fusion | bytes 16781312 | tf_op jit(solution)/shard_map/gather | solution.py:88
  609.2 8.8 %fusion = bf16[128,1,8]{2,1,0:T(2,128)(2,1)S(1)} fusion(bf16[1024,4096]{1,0:T(8,128)(2,1)} %gather_fusion.1, bf16[128,4096,1]{1,0,2:T(8,128)(2,1)S(1)} %bitcast.61), kind=kOutput, calls=%fused_computation.7 | convolution fusion | flops 8388608 | bytes 9439232 | tf_op jit(solution)/shard_map/tkd,td->tk/dot_general | solution.py:89
  618.1 0.1 copy.17
  618.3 0.1 reshape.91
  618.4 5.0 gather_fusion.2
  623.4 0.1 reshape.110
  623.5 0.1 select_convert_fusion
  623.6 6.8 multiply_convert_fusion
  630.4 2.0 broadcast_in_dim.64
  632.4 201.8 %all_to_all.16 = bf16[128,12,4096]{2,1,0:T(8,128)(2,1)} all-to-all(bf16[128,12,4096]{2,1,0:T(8,128)(2,1)S(1)} %bitcast.64), channel_id=1, replica_groups=mesh['wide'=64,'narrow'=2] {'wide','narrow'}, dimensions={0} | all-to-all | bytes 25165824 | tf_op jit(solution)/shard_map/all_to_all | solution.py:31
  834.2 18.2 %reshape_reshape.11 = bf16[1536,4096]{1,0:T(8,128)(2,1)} reshape(bf16[128,12,4096]{2,1,0:T(8,128)(2,1)} %all_to_all.16) | data formatting | bytes 25165824 | tf_op jit(solution)/shard_map/reshape;reshape | solution.py:100
  852.4 7.0 convolution_bitcast_fusion
  859.4 7.8 fusion.10
  (31 shorter events, 0.3 us)
Async XLA Ops:
  0.6 345.4 %copy-start = (bf16[128,4096]{1,0:T(8,128)(2,1)S(1)}, bf16[128,4096]{1,0:T(8,128)(2,1)}, u32[]{:S(2)}) copy-start(bf16[128,4096]{1,0:T(8,128)(2,1)} %param.10) | copy-start | bytes 3145732
  0.6 25.4 %copy-start.1 = (bf16[128,4096]{1,0:T(8,128)(2,1)S(1)}, bf16[128,4096]{1,0:T(8,128)(2,1)}, u32[]{:S(2)}) copy-start(bf16[128,4096]{1,0:T(8,128)(2,1)} %param.9) | copy-start | bytes 3145732
  25.8 6.1 copy-start.3
  274.7 14.0 %copy-start.2 = (bf16[1536,4096]{1,0:T(8,128)(2,1)S(1)}, bf16[1536,4096]{1,0:T(8,128)(2,1)}, u32[]{:S(2)}) copy-start(bf16[1536,4096]{1,0:T(8,128)(2,1)} %reshape_reshape.9) | copy-start | bytes 37748740
  288.7 13.0 %copy-start.5 = (bf16[1,16,768]{2,1,0:T(8,128)(2,1)S(1)}, bf16[1,16,768]{2,1,0:T(8,128)(2,1)}, u32[]{:S(2)}) copy-start(bf16[1,16,768]{2,1,0:T(8,128)(2,1)} %param.16) | copy-start | bytes 73732
  335.4 234.4 %all-to-all-start.1 = ((bf16[128,12,4096]{2,1,0:T(8,128)(2,1)}), bf16[128,12,4096]{2,1,0:T(8,128)(2,1)}, u32[]{:S(2)}, u32[]{:S(2)}) async-start(bf16[128,12,4096]{2,1,0:T(8,128)(2,1)} %bitcast.62), calls=%async_computation.1 | async-start | bytes 33554432 | tf_op jit(solution)/shard_map/all_to_all | solution.py:45
  609.2 8.9 %copy-start.6 = (bf16[128,8]{0,1:T(8,128)(2,1)S(1)}, bf16[128,8]{0,1:T(8,128)(2,1)}, u32[]{:S(2)}) copy-start(bf16[128,8]{0,1:T(8,128)(2,1)} %param.12) | copy-start | bytes 6148
  609.2 8.9 %copy-start.8 = (s32[128]{0:T(128)S(1)}, s32[128]{0:T(128)}, u32[]{:S(2)}) copy-start(s32[128]{0:T(128)} %param.13) | copy-start | bytes 1540
  618.1 5.3 copy-start.7
  618.4 5.1 copy-start.4
where the time goes:
time: 870 us; the launch traced here: 867 us
  blocking collectives  407 us (47%)
  waiting for transfers between devices  207 us (24%)
  local copies, waits for them, and re-layouts  149 us (17%)
  matrix products  58.7 us (7%)
  other arithmetic  33.3 us (4%)
  starting transfers between devices  10.5 us (1%)
    all_to_all x2, blocking collectives, to_experts(): lax.all_to_all(doubled, ('wide', 'narrow'), split_axis=0, concat_axis=0,...  403 us
    all_to_all x1, waiting for transfers between devices, to_homes(): lax.all_to_all(doubled, ('wide', 'narrow'), split_axis=0, concat_axis=0,...  207 us
    gather x1, local copies, waits for them, and re-layouts, on_device(): home_deltas.reshape(-1, features)[slot_place]  21.3 us
    another operation x3, other arithmetic  18.2 us
    another operation x1, local copies, waits for them, and re-layouts, on_device(): expert_rows = to_experts(token_rows).reshape(-1, features)  18.2 us
    another operation x1, local copies, waits for them, and re-layouts, on_device(): slot_cot = to_experts(cot_rows).reshape(-1, features)  18.2 us
    another operation x1, local copies, waits for them, and re-layouts, on_device(): home_deltas.reshape(-1, features)[slot_place]  18.1 us
  transfers between devices with their start and end apart: 1, of which 1 were waited for; matrix products, arithmetic and copies ran while one was open for 2% of the time, Pallas kernels for 0%

commit v1 on v0

v1 whole, which is shorter than its diff:
```python
import functools

import jax
import jax.numpy as jnp
from jax import lax
from jax.experimental import pallas as pl
from jax.experimental.pallas import tpu as pltpu
from jax.sharding import PartitionSpec as P

F32 = jnp.float32
BF16 = jnp.bfloat16
ROWS = 8
PARTS = (16, 8)


def iota(shape, dim):
    return lax.broadcasted_iota(jnp.int32, shape, dim)


def ones_where(condition, dtype=BF16):
    return jnp.where(condition, 1.0, 0.0).astype(dtype)


def dot(a, b, dims=((1,), (0,)), precision=None):
    return lax.dot_general(a, b, (dims, ((), ())), precision=precision, preferred_element_type=F32)


def transposed(block):
    tokens = block.shape[0]
    eye = ones_where(iota((tokens, tokens), 0) == iota((tokens, tokens), 1))
    return dot(block.astype(BF16), eye, ((0,), (0,)))


def slot_of_token(ids, experts):
    tokens, picks = ids.shape
    ids_t = transposed(ids.astype(F32))
    expert = iota((experts, tokens), 0).astype(F32)
    match = jnp.zeros((experts, tokens), F32)
    for k in range(picks):
        match = match + jnp.where(ids_t[k : k + 1, :] == expert, 1.0, 0.0)
    before = ones_where(iota((tokens, tokens), 0) < iota((tokens, tokens), 1))
    rank = dot(match.astype(BF16), before)
    return jnp.where(match > 0.0, rank, -1.0), ids_t


def spread(groups, slots=ROWS):
    shape = (groups * slots, groups)
    return ones_where(iota(shape, 0) // slots == iota(shape, 1))


def gathered(groups):
    shape = (groups, groups * ROWS)
    return ones_where(iota(shape, 1) // ROWS == iota(shape, 0))


def own_lanes(rows, rank, slots=ROWS):
    shape = (rows, slots * rank)
    return iota(shape, 0) % slots == iota(shape, 1) // rank


def one_hot_slots(slots, first, count=ROWS):
    rows = slots.shape[0] * count
    wide = dot(spread(slots.shape[0], count), slots.astype(BF16))
    wanted = (iota((rows, slots.shape[1]), 0) % count + first).astype(F32)
    return jnp.where(wide == wanted, 1.0, 0.0)


def dispatch_body(experts, first, count, core_ref, ids_ref, rows_ref, out_ref, hot_ref):
    @pl.when(pl.program_id(0) == 0)
    def _():
        slots, _unused = slot_of_token(ids_ref[...], experts)
        hot_ref[...] = one_hot_slots(slots, first, count).astype(BF16)

    out_ref[...] = dot(hot_ref[...], rows_ref[...]).astype(BF16)


def dispatch(core, ids, rows, experts, first, count):
    tokens, features = rows.shape
    half = features // 2
    block = min(512, half)
    steps = half // block
    sent = experts * count
    return pl.pallas_call(
        functools.partial(dispatch_body, experts, first, count),
        grid_spec=pltpu.PrefetchScalarGridSpec(
            num_scalar_prefetch=1,
            grid=(steps,),
            in_specs=[
                pl.BlockSpec(ids.shape, lambda n, c: (0, 0)),
                pl.BlockSpec((tokens, block), lambda n, c: (0, c[0] * steps + n)),
            ],
            out_specs=pl.BlockSpec((sent, block), lambda n, c: (0, n)),
            scratch_shapes=[pltpu.VMEM((sent, tokens), BF16)],
        ),
        out_shape=jax.ShapeDtypeStruct((sent, half), BF16),
        cost_estimate=pl.CostEstimate(
            flops=2 * sent * tokens * half, bytes_accessed=2 * sent * half, transcendentals=0
        ),
        compiler_params=pltpu.CompilerParams(vmem_limit_bytes=24 * 1024 * 1024),
        name="dispatch_rows",
    )(core, ids, rows)


def experts_body(groups, pairs, count, steps, last, core_ref, own_ref, other_ref, go_ref, gx_ref, uo_ref, ux_ref, a_ref, *refs):
    before_refs, (hid_ref, lat_ref, acc_ref) = refs[:-3], refs[-3:]
    n = pl.program_id(0)
    own, other = own_ref[...], other_ref[...]
    gate = dot(own, go_ref[0]) + dot(other, gx_ref[0])
    up = dot(own, uo_ref[0]) + dot(other, ux_ref[0])
    hidden = (gate / (1.0 + jnp.exp(-gate)) * up).astype(BF16)
    hid_ref[...] = hidden
    rank = a_ref.shape[1]
    tiled = jnp.concatenate([a_ref[0]] * count, axis=0)
    part = dot(hidden, tiled, ((1,), (1,)))

    @pl.when(n == 0)
    def _():
        acc_ref[...] = part

    @pl.when(n > 0)
    def _():
        acc_ref[...] = acc_ref[...] + part

    @pl.when(n == steps - 1)
    def _():
        rows = groups * count
        mine = jnp.where(own_lanes(rows, rank, count), acc_ref[...], 0.0).astype(BF16)
        shape = (groups * pairs, rows)
        both = ones_where(iota(shape, 1) // count == iota(shape, 0) // pairs)
        now = dot(both, mine).astype(BF16)
        if last:
            width = ROWS * rank
            pieces = [ref[...] for ref in before_refs] + [now]
            at = 0
            for piece in pieces:
                for c in range(piece.shape[1] // width):
                    lat_ref[:, at, :] = piece[:, c * width : (c + 1) * width]
                    at += 1
            for c in range(at, ROWS):
                lat_ref[:, c, :] = jnp.zeros((groups * pairs, width), BF16)
        else:
            lat_ref[...] = now


def experts_forward(core, own, other, gate, up, adapter_a, before, groups, pairs, last):
    rows, half = own.shape
    count = rows // groups
    hidden_units = gate.shape[2]
    rank = adapter_a.shape[1]
    block = min(256, hidden_units)
    steps = hidden_units // block
    width = count * rank
    mine = pl.BlockSpec((1, half, block), lambda n, c: (0, c[0], n))
    theirs = pl.BlockSpec((1, half, block), lambda n, c: (0, 1 - c[0], n))
    whole = pl.BlockSpec((rows, half), lambda n, c: (0, 0))
    in_specs = [whole, whole, mine, theirs, mine, theirs, pl.BlockSpec((1, rank, block), lambda n, c: (0, 0, n))]
    in_specs += [pl.BlockSpec(x.shape, lambda n, c: (0, 0)) for x in before]
    out = (groups * pairs, ROWS, ROWS * rank) if last else (groups * pairs, width)
    return pl.pallas_call(
        functools.partial(experts_body, groups, pairs, count, steps, last),
        grid_spec=pltpu.PrefetchScalarGridSpec(
            num_scalar_prefetch=1,
            grid=(steps,),
            in_specs=in_specs,
            out_specs=[
                pl.BlockSpec((rows, block), lambda n, c: (0, n)),
                pl.BlockSpec(out, lambda n, c: (0,) * len(out)),
            ],
            scratch_shapes=[pltpu.VMEM((rows, width), F32)],
        ),
        out_shape=[
            jax.ShapeDtypeStruct((rows, hidden_units), BF16),
            jax.ShapeDtypeStruct(out, BF16),
        ],
        cost_estimate=pl.CostEstimate(
            flops=8 * rows * half * hidden_units,
            bytes_accessed=8 * half * hidden_units + 4 * rows * half,
            transcendentals=rows * hidden_units,
        ),
        compiler_params=pltpu.CompilerParams(vmem_limit_bytes=48 * 1024 * 1024),
        name="experts_forward",
    )(core, own, other, gate, gate, up, up, adapter_a, *before)


def project_body(experts, chunks, core_ref, ids_ref, readout_ref, adapters_ref, out_ref):
    rank = adapters_ref.shape[0] // experts
    rows = experts * ROWS
    slots, _unused = slot_of_token(ids_ref[...], experts)
    every = dot(readout_ref[...], adapters_ref[...], ((1,), (1,))).astype(BF16)
    width = experts * rank
    own_expert = iota((rows, width), 0) // ROWS == iota((rows, width), 1) // rank
    fold = ones_where(iota((width, ROWS * rank), 0) % rank == iota((width, ROWS * rank), 1) % rank)
    lanes = own_lanes(rows, rank)
    for c in range(chunks):
        hot = one_hot_slots(slots, c * ROWS).astype(BF16)
        picked = jnp.where(own_expert, dot(hot, every), 0.0).astype(BF16)
        placed = jnp.where(lanes, dot(picked, fold), 0.0).astype(BF16)
        out_ref[:, c * ROWS * rank : (c + 1) * ROWS * rank] = dot(gathered(experts), placed)


def project(core, ids, readout, adapters, experts, chunks):
    tokens, features = readout.shape
    half = features // 2
    rank = adapters.shape[0] // experts
    return pl.pallas_call(
        functools.partial(project_body, experts, chunks),
        grid_spec=pltpu.PrefetchScalarGridSpec(
            num_scalar_prefetch=1,
            grid=(1,),
            in_specs=[
                pl.BlockSpec(ids.shape, lambda n, c: (0, 0)),
                pl.BlockSpec((tokens, half), lambda n, c: (0, c[0])),
                pl.BlockSpec(adapters.shape, lambda n, c: (0, 0)),
            ],
            out_specs=pl.BlockSpec((experts, chunks * ROWS * rank), lambda n, c: (0, 0)),
        ),
        out_shape=jax.ShapeDtypeStruct((experts, chunks * ROWS * rank), F32),
        compiler_params=pltpu.CompilerParams(vmem_limit_bytes=48 * 1024 * 1024),
        name="project_readout",
    )(core, ids, readout, adapters)


def weigh_body(experts, pairs, chunks, core_ref, ids_ref, gains_ref, mask_ref, latent_ref, own_ref, other_ref, readout_ref, log_ref, out_ref, lift_ref):
    tokens, picks = ids_ref.shape
    width = latent_ref.shape[2]
    rank = width // ROWS
    rows = experts * ROWS
    half = readout_ref.shape[1]

    @pl.when(pl.program_id(0) == 0)
    def _():
        slots, ids_t = slot_of_token(ids_ref[...], experts)
        gains_t = transposed(gains_ref[...])
        expert = iota((experts, tokens), 0).astype(F32)
        gains = jnp.zeros((experts, tokens), F32)
        for k in range(picks):
            gains = gains + jnp.where(ids_t[k : k + 1, :] == expert, gains_t[k : k + 1, :], 0.0)
        spread_rows = spread(experts)
        lanes = own_lanes(rows, rank)
        first = iota((rows, width), 1) % rank == 0
        shape = (experts, experts * pairs)
        both = ones_where(iota(shape, 1) // pairs == iota(shape, 0))
        same = ones_where(iota((width, width), 0) // rank == iota((width, width), 1) // rank, F32)
        wide_gains = dot(spread_rows, gains.astype(BF16))
        hots, latents, projections = [], [], []
        total = jnp.zeros((1, tokens), F32)
        for c in range(chunks):
            span = slice(c * width, (c + 1) * width)
            latent = dot(both, latent_ref[:, c, :]).astype(BF16).astype(F32)
            projection = own_ref[:, span] + other_ref[:, span]
            score = dot(latent * projection, same, precision=lax.Precision.HIGHEST).astype(BF16)
            column = jnp.sum(
                jnp.where(lanes & first, dot(spread_rows, score), 0.0), axis=1, keepdims=True
            )
            hot = one_hot_slots(slots, c * ROWS)
            total = total + jnp.sum(hot * wide_gains * column, axis=0, keepdims=True)
            hots.append(hot)
            latents.append(latent)
            projections.append(projection)
        log_ref[...] = total
        coefficient = 2.0 * mask_ref[...].astype(F32) / (1.0 + jnp.exp(-total))
        weight = (gains * coefficient).astype(BF16)
        wide_weight = dot(spread_rows, weight)
        every = experts * rank
        tile = ones_where(iota((width, every), 0) % rank == iota((width, every), 1) % rank)
        own_expert = iota((rows, every), 0) // ROWS == iota((rows, every), 1) // rank
        lift = jnp.zeros((every, tokens), F32)
        out_ref[:, :, half:] = jnp.zeros((experts, rank, width), BF16)
        for c in range(chunks):
            column = jnp.sum(hots[c] * wide_weight, axis=1, keepdims=True)
            placed = jnp.where(lanes, column, 0.0).astype(BF16)
            slot_weight = dot(gathered(experts), placed)
            out_ref[:, c, half:] = (slot_weight * projections[c]).astype(BF16)
            weighted = (slot_weight * latents[c]).astype(BF16)
            weighted = jnp.where(lanes, dot(spread_rows, weighted), 0.0).astype(BF16)
            weighted = jnp.where(own_expert, dot(weighted, tile), 0.0).astype(BF16)
            lift = lift + dot(weighted, hots[c].astype(BF16), ((0,), (0,)))
        lift_ref[...] = lift.astype(BF16)

    block = 512
    for n in range(half // block):
        part = dot(lift_ref[...], readout_ref[:, n * block : (n + 1) * block]).astype(BF16)
        out_ref[:, :, n * block : (n + 1) * block] = part.reshape(experts, rank, block)


def weigh(core, ids, gains, mask, latents, own, other, readout, experts, pairs, chunks):
    tokens = ids.shape[0]
    half = readout.shape[1] // pairs
    width = latents.shape[2]
    rank = width // ROWS
    full = lambda shape: pl.BlockSpec(shape, lambda n, c: (0,) * len(shape))
    out = (experts, rank, half + width)
    return pl.pallas_call(
        functools.partial(weigh_body, experts, pairs, chunks),
        grid_spec=pltpu.PrefetchScalarGridSpec(
            num_scalar_prefetch=1,
            grid=(1,),
            in_specs=[
                full(ids.shape),
                full(gains.shape),
                full(mask.shape),
                full(latents.shape),
                full(own.shape),
                full(other.shape),
                pl.BlockSpec((tokens, half), lambda n, c: (0, c[0])),
            ],
            out_specs=[full((1, tokens)), full(out)],
            scratch_shapes=[pltpu.VMEM((experts * rank, tokens), BF16)],
        ),
        out_shape=[jax.ShapeDtypeStruct((1, tokens), F32), jax.ShapeDtypeStruct(out, BF16)],
        compiler_params=pltpu.CompilerParams(vmem_limit_bytes=40 * 1024 * 1024),
        name="weigh_tokens",
    )(core, ids, gains, mask, latents, own, other, readout)


def gradients_body(groups, packed_ref, *refs):
    hid_refs, (grad_a_ref, grad_b_ref) = refs[:-2], refs[-2:]
    rank, half = grad_b_ref.shape
    block = 256
    for n in range(half // block):
        span = slice(n * block, (n + 1) * block)
        grad_b_ref[:, span] = jnp.sum(packed_ref[:, :, span].astype(F32), axis=0)
    result = jnp.zeros(grad_a_ref.shape, F32)
    at = 0
    for hid_ref in hid_refs:
        rows = hid_ref.shape[0]
        count = rows // groups
        pieces = [packed_ref[:, at + c, half:] for c in range(count // ROWS)]
        at += count // ROWS
        back = dot(spread(groups, count), jnp.concatenate(pieces, axis=1))
        back = jnp.where(own_lanes(rows, rank, count), back, 0.0).astype(BF16)
        total = dot(back, hid_ref[...], ((0,), (0,)))
        for s in range(count):
            result = result + total[s * rank : (s + 1) * rank]
    grad_a_ref[...] = result


def gradients(packed, hidden, rank):
    groups = packed.shape[0]
    half = packed.shape[2] - ROWS * rank
    hidden_units = hidden[0].shape[1]
    return pl.pallas_call(
        functools.partial(gradients_body, groups),
        out_shape=[
            jax.ShapeDtypeStruct((rank, hidden_units), F32),
            jax.ShapeDtypeStruct((rank, half), F32),
        ],
        compiler_params=pltpu.CompilerParams(vmem_limit_bytes=40 * 1024 * 1024),
        name="adapter_gradients",
    )(packed, *hidden)


def swap(payload):
    return lax.ppermute(payload, "narrow", [(0, 1), (1, 0)])


def exchange(payload):
    return lax.all_to_all(payload, "wide", split_axis=0, concat_axis=0, tiled=True)


def on_device(
    hidden_in,
    readout,
    route_ids,
    route_weights,
    forget_mask,
    gate_proj,
    up_proj,
    adapter_a,
    adapter_b,
):
    groups = lax.axis_size("wide")
    pairs = lax.axis_size("narrow")
    tokens, picks = route_ids.shape
    features = hidden_in.shape[1]
    half = features // pairs
    rank = adapter_a.shape[1]
    chunks = sum(PARTS) // ROWS
    side = lax.axis_index("narrow")
    core = side.reshape(1).astype(jnp.int32)

    own_b = lax.dynamic_slice_in_dim(adapter_b[0], side * half, half, 1)
    own_b, route_ids = lax.optimization_barrier((own_b, route_ids))
    adapters = lax.all_gather(own_b, "wide", axis=0, tiled=True)

    own, first = [], 0
    for count in PARTS:
        sent = dispatch(core, route_ids, hidden_in, groups, first, count)
        own.append(exchange(sent.reshape(groups, count, half)).reshape(groups * count, half))
        first += count

    hidden, latents = [], []
    for part, x in enumerate(own):
        if hidden:
            x, hidden[-1] = lax.optimization_barrier((x, hidden[-1]))
        acts, sums = experts_forward(
            core, x, swap(x), gate_proj, up_proj, adapter_a, latents, groups, pairs, part == len(own) - 1
        )
        hidden.append(acts)
        latents.append(sums)
    projections = project(core, route_ids, readout, adapters, groups, chunks)
    home_latents = lax.all_to_all(
        latents[-1], ("wide", "narrow"), split_axis=0, concat_axis=0, tiled=True
    )
    log_ratio, packed = weigh(
        core,
        route_ids,
        route_weights,
        forget_mask.reshape(1, tokens),
        home_latents,
        projections,
        swap(projections),
        readout,
        groups,
        pairs,
        chunks,
    )
    grad_a, part_b = gradients(exchange(packed), hidden, rank)
    other_b = swap(part_b)
    grad_b = jnp.where(
        side == 0,
        jnp.concatenate([part_b, other_b], axis=1),
        jnp.concatenate([other_b, part_b], axis=1),
    )
    return (log_ratio.reshape(tokens), grad_a[None], grad_b[None])


def solution(mesh):
    return jax.shard_map(
        on_device,
        mesh=mesh,
        in_specs=(
            P("wide", None),
            P("wide", None),
            P("wide", None),
            P("wide", None),
            P("wide"),
            P("wide", None, "narrow"),
            P("wide", None, "narrow"),
            P("wide", None, "narrow"),
            P("wide", None, None),
        ),
        out_specs=(P("wide"), P("wide", None, "narrow"), P("wide", None, None)),
        check_vma=False,
    )
```

time: 870 us -> 249 us (0.29)
  blocking collectives: 407 us -> 123 us
  waiting for transfers between devices: 207 us -> 35.1 us
  local copies, waits for them, and re-layouts: 149 us -> 8.58 us
  matrix products: 58.7 us -> 0 us
  Pallas kernels: 0 us -> 49.5 us
  other arithmetic: 33.3 us -> 0.72 us
  between operations: 0.94 us -> 14.2 us
    all_to_all x2, blocking collectives: 403 us -> 123 us  [exchange(): lax.all_to_all(payload, 'wide', split_axis=0, concat_axis=0, tiled=True)]
    all_to_all x1 -> x2, waiting for transfers between devices: 207 us -> 8.15 us  [the longest x1 8.15 us: exchange(): lax.all_to_all(payload, 'wide', split_axis=0, concat_axis=0, tiled=True)]
    dot_general x7 -> x0, matrix products: 58.7 us -> none  [the longest x1 14 us: on_device(): jnp.dot(expert_rows, up_proj[0], preferred_element_type=jnp.float32)]
    another operation x5 -> x0, local copies, waits for them, and re-layouts: 54.5 us -> none  [the longest x1 18.2 us: on_device(): expert_rows = to_experts(token_rows).reshape(-1, features)]
    pallas_call x0 -> x7, Pallas kernels: none -> 49.5 us  [the longest x2 30.8 us: experts_forward(): pl.pallas_call(functools.partial(experts_body, groups, pairs, count, step...]
    gather x6 -> x0, local copies, waits for them, and re-layouts: 47.6 us -> none  [the longest x1 21.3 us: on_device(): home_deltas.reshape(-1, features)[slot_place]]
    all_gather x0 -> x1, waiting for transfers between devices: none -> 21.4 us  [on_device(): adapters = lax.all_gather(own_b, 'wide', axis=0, tiled=True)]
    broadcast_in_dim x5 -> x0, local copies, waits for them, and re-layouts: 19.3 us -> none  [the longest x1 10.7 us: to_homes(): jnp.broadcast_to(own_half[:, None], (groups, pairs) + own_half.shape[1:])]
  transfers between devices with their start and end apart: 1 -> 7, of which waited for: 1 -> 5; matrix products, arithmetic and copies ran while one was open for 2% -> 0% of each run, Pallas kernels for 0% -> 15%
where the time goes in v1:
time: 249 us
  blocking collectives  123 us (49%)
  Pallas kernels  49.5 us (20%)
  waiting for transfers between devices  35.1 us (14%)
  starting transfers between devices  17.5 us (7%)
  between operations  14.2 us (6%)
  local copies, waits for them, and re-layouts  8.58 us (3%)
    all_to_all x2, blocking collectives, exchange(): lax.all_to_all(payload, 'wide', split_axis=0, concat_axis=0, tiled=True)  123 us
    pallas_call x2, Pallas kernels, experts_forward(): pl.pallas_call(functools.partial(experts_body, groups, pairs, count, step...  30.8 us
    all_gather x1, waiting for transfers between devices, on_device(): adapters = lax.all_gather(own_b, 'wide', axis=0, tiled=True)  21.4 us
    all_to_all x1, waiting for transfers between devices, exchange(): lax.all_to_all(payload, 'wide', split_axis=0, concat_axis=0, tiled=True)  8.15 us
    ppermute x4, starting transfers between devices, swap(): return lax.ppermute(payload, 'narrow', [(0, 1), (1, 0)])  7.22 us
    unnamed x27, local copies, waits for them, and re-layouts  7.17 us
    pallas_call x1, Pallas kernels, weigh(): pl.pallas_call(functools.partial(weigh_body, experts, pairs, chunks), gri...  6.16 us
    pallas_call x2, Pallas kernels, dispatch(): pl.pallas_call(functools.partial(dispatch_body, experts, first, count), g...  5.66 us
  transfers between devices with their start and end apart: 7, of which 5 were waited for; matrix products, arithmetic and copies ran while one was open for 0% of the time, Pallas kernels for 15%

profile of v1, /device:TPU:1, one launch (start us, length us, event | category | flops | bytes accessed | tf_op | source)
XLA Modules:
  0.0 248.8 jit_solution(3557578404781123775)
XLA Ops:
  7.2 0.0 copy-start
  7.2 0.0 all-gather.2.cloned.1.call-start
  7.2 0.8 copy-done
  8.1 0.6 dynamic-slice_bitcast_fusion
  8.7 0.8 copy.15.ids_ref
  9.5 0.0 copy-start.2
  9.5 1.2 copy-done.2
  10.7 2.6 %dispatch_rows.3 = bf16[1024,2048]{1,0:T(8,128)(2,1)S(1)} custom-call(s32[1]{0:T(128)} %bitcast.core_ref, s32[128,8]{1,0:T(8,128)S(1)} %copy.15.ids_ref, bf16[128,4096]{1,0:T(8,128)(2,1)S(1)} %copy-done.2), custom_call_target="tpu_custom_call" | custom-call | flops 536870912 | bytes 4194304 | tf_op jit(solution)/shard_map/dispatch_rows/pallas_call | solution.py:83
  13.3 0.0 copy-start.3
  13.3 62.2 %all_to_all.20 = bf16[64,16,2048]{2,1,0:T(8,128)(2,1)} all-to-all(bf16[64,16,2048]{2,1,0:T(8,128)(2,1)S(1)} %bitcast.12), channel_id=1, replica_groups=mesh['wide'=64,'narrow'=2] {'wide'}, dimensions={0} | all-to-all | bytes 8388608 | tf_op jit(solution)/shard_map/all_to_all | solution.py:358
  75.5 2.8 %collective-permute-start = (bf16[1024,2048]{1,0:T(8,128)(2,1)}, bf16[1024,2048]{1,0:T(8,128)(2,1)}, u32[]{:S(2)}, u32[]{:S(2)}) collective-permute-start(bf16[1024,2048]{1,0:T(8,128)(2,1)} %bitcast.6.own_ref), channel_id=1, source_target_pairs={{0,1},{1,0},{2,3},{3,2},{4,5},{5,4},{6,7},{7,6},{8,9},{9,8},{10,11... | collective-permute-start | bytes 12582920 | tf_op jit(solution)/shard_map/ppermute | solution.py:354
  78.4 0.0 all-gather.2.cloned.1.call-update
  78.4 0.0 copy-done.3
  78.4 3.1 %dispatch_rows.2 = bf16[512,2048]{1,0:T(8,128)(2,1)} custom-call(s32[1]{0:T(128)} %bitcast.core_ref, s32[128,8]{1,0:T(8,128)S(1)} %copy.15.ids_ref, bf16[128,4096]{1,0:T(8,128)(2,1)S(1)} %copy-done.3), custom_call_target="tpu_custom_call" | custom-call | flops 268435456 | bytes 2097152 | tf_op jit(solution)/shard_map/dispatch_rows/pallas_call | solution.py:83
  81.5 5.3 %all-to-all-start = ((bf16[64,8,2048]{2,1,0:T(8,128)(2,1)}), bf16[64,8,2048]{2,1,0:T(8,128)(2,1)S(1)}, u32[]{:S(2)}, u32[]{:S(2)}) async-start(bf16[64,8,2048]{2,1,0:T(8,128)(2,1)} %bitcast.3), calls=%async_computation | async-start | bytes 4194304 | tf_op jit(solution)/shard_map/all_to_all | solution.py:358
  86.8 0.0 collective-permute-done.other_ref
  86.8 0.0 copy-done.10
  86.8 19.9 %experts_forward.2 = (bf16[1024,768]{1,0:T(8,128)(2,1)S(1)}, bf16[128,256]{1,0:T(8,128)(2,1)S(1)}) custom-call(s32[1]{0:T(128)} %bitcast.core_ref, bf16[1024,2048]{1,0:T(8,128)(2,1)} %bitcast.6.own_ref, bf16[1024,2048]{1,0:T(8,128)(2,1)} %collective-permute-done.other_ref, bf16[1,4096,768]{2,1,0:T(8,128)(2,1)} %gx_ref.3, bf16[1,4096,768]{2,1,0:T(8,128)(2,1)} %gx_ref.3, ...), custom_call_target="tpu_custom_call" | custom-call | flops 12884901888 | bytes 20971520 | tf_op jit(solution)/shard_map/experts_forward/pallas_call | solution.py:159
  106.7 0.0 copy-start.5
  106.7 1.2 copy-done.5
  107.9 8.1 %all-to-all-done = bf16[64,8,2048]{2,1,0:T(8,128)(2,1)S(1)} async-done(((bf16[64,8,2048]{2,1,0:T(8,128)(2,1)}), bf16[64,8,2048]{2,1,0:T(8,128)(2,1)S(1)}, u32[]{:S(2)}, u32[]{:S(2)}) %all-to-all-start) | async-done | bytes 2097184 | tf_op jit(solution)/shard_map/all_to_all | solution.py:358
  116.0 1.8 collective-permute-start.1
  117.8 3.8 %collective-permute-done.1.other_ref = bf16[512,2048]{1,0:T(8,128)(2,1)S(1)} collective-permute-done((bf16[512,2048]{1,0:T(8,128)(2,1)S(1)}, bf16[512,2048]{1,0:T(8,128)(2,1)S(1)}, u32[]{:S(2)}, u32[]{:S(2)}) %collective-permute-start.1) | collective-permute-done | bytes 2097184 | tf_op jit(solution)/shard_map/ppermute | solution.py:354
  121.6 11.0 %experts_forward.3 = (bf16[512,768]{1,0:T(8,128)(2,1)S(1)}, bf16[128,8,128]{2,1,0:T(8,128)(2,1)S(1)}) custom-call(s32[1]{0:T(128)} %bitcast.core_ref, bf16[512,2048]{1,0:T(8,128)(2,1)S(1)} %bitcast.14, bf16[512,2048]{1,0:T(8,128)(2,1)S(1)} %collective-permute-done.1.other_ref, bf16[1,4096,768]{2,1,0:T(8,128)(2,1)} %gx_ref.3, bf16[1,4096,768]{2,1,0:T(8,128)(2,1)} %gx_ref.3, ...), custom_call_target="tpu_custom_call" | custom-call | flops 6442450944 | bytes 16777216 | tf_op jit(solution)/shard_map/experts_forward/pallas_call | solution.py:159
  132.6 0.0 copy-start.7
  132.6 0.9 copy-done.7
  133.5 0.7 copy-done.9
  134.2 4.9 %all-to-all-start.2 = ((bf16[128,8,128]{2,1,0:T(8,128)(2,1)}), bf16[128,8,128]{2,1,0:T(8,128)(2,1)S(1)}, u32[]{:S(2)}, u32[]{:S(2)}) async-start(bf16[128,8,128]{2,1,0:T(8,128)(2,1)} %copy-done.9), calls=%async_computation.2 | async-start | bytes 524288 | tf_op jit(solution)/shard_map/all_to_all | solution.py:402
  139.1 21.4 %all-gather.2.cloned.1.call-done.adapters_ref = bf16[1024,2048]{1,0:T(8,128)(2,1)} async-done(((bf16[16,2048]{1,0:T(8,128)(2,1)}), bf16[1024,2048]{1,0:T(8,128)(2,1)}) %all-gather.2.cloned.1.call-update) | async-done | bytes 4194320 | tf_op jit(solution)/shard_map/all_gather | solution.py:384
  160.4 0.0 copy-done.4
  160.4 2.2 copy-done.1
  162.6 4.1 %project_readout.1.own_ref = f32[64,384]{1,0:T(8,128)S(1)} custom-call(s32[1]{0:T(128)} %bitcast.core_ref, s32[128,8]{1,0:T(8,128)S(1)} %copy.15.ids_ref, bf16[128,4096]{1,0:T(8,128)(2,1)S(1)} %copy-done.4, bf16[1024,2048]{1,0:T(8,128)(2,1)S(1)} %copy-done.1), custom_call_target="tpu_custom_call" | custom-call | tf_op jit(solution)/shard_map/project_readout/pallas_call | solution.py:205
  166.7 1.0 collective-permute-start.2
  167.7 0.0 copy-done.12
  167.7 0.1 copy.16.gains_ref
  167.8 0.8 collective-permute-done.2.other_ref
  168.6 0.0 all-to-all-done.2.latent_ref
  168.6 0.0 copy-done.11
  168.6 6.2 %weigh_tokens.1 = (f32[1,128]{1,0:T(1,128)}, bf16[64,16,2176]{2,1,0:T(8,128)(2,1)S(1)}) custom-call(s32[1]{0:T(128)} %bitcast.core_ref, s32[128,8]{1,0:T(8,128)S(1)} %copy.15.ids_ref, bf16[128,8]{1,0:T(8,128)(2,1)S(1)} %copy.16.gains_ref, s32[1,128]{1,0:T(1,128)S(1)} %bitcast.16, bf16[128,8,128]{2,1,0:T(8,128)(2,1)S(1)} %all-to-all-done.2.latent_ref, ...), custom_call_target="tpu_custom_call" | custom-call | tf_op jit(solution)/shard_map/weigh_tokens/pallas_call | solution.py:293
  174.8 0.0 copy-start.6
  174.8 0.0 copy-start.8
  174.8 61.0 %all_to_all.21.packed_ref = bf16[64,16,2176]{2,1,0:T(8,128)(2,1)S(1)} all-to-all(bf16[64,16,2176]{2,1,0:T(8,128)(2,1)S(1)} %get-tuple-element.22), channel_id=1, replica_groups=mesh['wide'=64,'narrow'=2] {'wide'}, dimensions={0} | all-to-all | bytes 8912896 | tf_op jit(solution)/shard_map/all_to_all | solution.py:358
  235.9 0.0 copy-done.6
  235.9 0.0 copy-done.8
  235.9 2.7 %adapter_gradients.1 = (f32[16,768]{1,0:T(8,128)}, f32[16,2048]{1,0:T(8,128)S(1)}) custom-call(bf16[64,16,2176]{2,1,0:T(8,128)(2,1)S(1)} %all_to_all.21.packed_ref, bf16[1024,768]{1,0:T(8,128)(2,1)S(1)} %copy-done.6, bf16[512,768]{1,0:T(8,128)(2,1)S(1)} %copy-done.8), custom_call_target="tpu_custom_call" | custom-call | tf_op jit(solution)/shard_map/adapter_gradients/pallas_call | solution.py:342
  238.6 1.6 collective-permute-start.3
  240.2 1.0 collective-permute-done.3
  241.2 0.7 maximum_select_fusion
  (6 shorter events, 0.0 us)
Async XLA Ops:
  7.2 0.9 copy-start
  7.2 153.3 %all-gather.2.cloned.1.call-start = ((), (), s32[]{:S(2)}) async-start(), calls=%async_computation.4 | async-start | bytes 4259840 | tf_op jit(solution)/shard_map/all_gather | solution.py:384
  9.5 1.2 copy-start.2
  13.3 65.1 %copy-start.3 = (bf16[128,4096]{1,0:T(8,128)(2,1)S(1)}, bf16[128,4096]{1,0:T(8,128)(2,1)}, u32[]{:S(2)}) copy-start(bf16[128,4096]{1,0:T(8,128)(2,1)} %rows_ref.3) | copy-start | bytes 3145732
  75.5 11.3 %copy-start.10 = (bf16[1,16,768]{2,1,0:T(8,128)(2,1)S(1)}, bf16[1,16,768]{2,1,0:T(8,128)(2,1)}, u32[]{:S(2)}) copy-start(bf16[1,16,768]{2,1,0:T(8,128)(2,1)} %a_ref.3) | copy-start | bytes 73732
  75.5 11.3 %collective-permute-start = (bf16[1024,2048]{1,0:T(8,128)(2,1)}, bf16[1024,2048]{1,0:T(8,128)(2,1)}, u32[]{:S(2)}, u32[]{:S(2)}) collective-permute-start(bf16[1024,2048]{1,0:T(8,128)(2,1)} %bitcast.6.own_ref), channel_id=1, source_target_pairs={{0,1},{1,0},{2,3},{3,2},{4,5},{5,4},{6,7},{7,6},{8,9},{9,8},{10,11... | collective-permute-start | bytes 12582920 | tf_op jit(solution)/shard_map/ppermute | solution.py:354
  81.5 34.6 %all-to-all-start = ((bf16[64,8,2048]{2,1,0:T(8,128)(2,1)}), bf16[64,8,2048]{2,1,0:T(8,128)(2,1)S(1)}, u32[]{:S(2)}, u32[]{:S(2)}) async-start(bf16[64,8,2048]{2,1,0:T(8,128)(2,1)} %bitcast.3), calls=%async_computation | async-start | bytes 4194304 | tf_op jit(solution)/shard_map/all_to_all | solution.py:358
  106.7 1.2 copy-start.5
  116.0 5.6 %collective-permute-start.1 = (bf16[512,2048]{1,0:T(8,128)(2,1)S(1)}, bf16[512,2048]{1,0:T(8,128)(2,1)S(1)}, u32[]{:S(2)}, u32[]{:S(2)}) collective-permute-start(bf16[512,2048]{1,0:T(8,128)(2,1)S(1)} %bitcast.13), channel_id=1, source_target_pairs={{0,1},{1,0},{2,3},{3,2},{4,5},{5,4},{6,7},{7,6},{8,9},{9,8},{10,11... | collective-permute-start | bytes 6291464 | tf_op jit(solution)/shard_map/ppermute | solution.py:354
  121.6 38.8 %copy-start.4 = (bf16[128,4096]{1,0:T(8,128)(2,1)S(1)}, bf16[128,4096]{1,0:T(8,128)(2,1)}, u32[]{:S(2)}) copy-start(bf16[128,4096]{1,0:T(8,128)(2,1)} %readout_ref.3) | copy-start | bytes 3145732
  132.6 0.9 copy-start.7
  133.5 0.7 copy-start.9
  134.2 33.5 %copy-start.12 = (bf16[128,8]{0,1:T(8,128)(2,1)S(1)}, bf16[128,8]{0,1:T(8,128)(2,1)}, u32[]{:S(2)}) copy-start(bf16[128,8]{0,1:T(8,128)(2,1)} %param.12) | copy-start | bytes 6148
  134.2 34.5 %copy-start.11 = (s32[128]{0:T(128)S(1)}, s32[128]{0:T(128)}, u32[]{:S(2)}) copy-start(s32[128]{0:T(128)} %param.13) | copy-start | bytes 1540
  134.2 34.4 %all-to-all-start.2 = ((bf16[128,8,128]{2,1,0:T(8,128)(2,1)}), bf16[128,8,128]{2,1,0:T(8,128)(2,1)S(1)}, u32[]{:S(2)}, u32[]{:S(2)}) async-start(bf16[128,8,128]{2,1,0:T(8,128)(2,1)} %copy-done.9), calls=%async_computation.2 | async-start | bytes 524288 | tf_op jit(solution)/shard_map/all_to_all | solution.py:402
  160.4 2.2 copy-start.1
  166.7 1.9 collective-permute-start.2
  174.8 61.1 %copy-start.6 = (bf16[1024,768]{1,0:T(8,128)(2,1)S(1)}, bf16[1024,768]{1,0:T(8,128)(2,1)}, u32[]{:S(2)}) copy-start(bf16[1024,768]{1,0:T(8,128)(2,1)} %copy-done.5) | copy-start | bytes 4718596
  174.8 61.1 %copy-start.8 = (bf16[512,768]{1,0:T(8,128)(2,1)S(1)}, bf16[512,768]{1,0:T(8,128)(2,1)}, u32[]{:S(2)}) copy-start(bf16[512,768]{1,0:T(8,128)(2,1)} %copy-done.7) | copy-start | bytes 2359300
  238.6 2.6 %collective-permute-start.3 = (f32[16,2048]{1,0:T(8,128)S(1)}, f32[16,2048]{1,0:T(8,128)S(1)}, u32[]{:S(2)}, u32[]{:S(2)}) collective-permute-start(f32[16,2048]{1,0:T(8,128)S(1)} %get-tuple-element.26), channel_id=1, source_target_pairs={{0,1},{1,0},{2,3},{3,2},{4,5},{5,4},{6,7},{7,6},{8,9},{9,8},{10,11... | collective-permute-start | bytes 393224 | tf_op jit(solution)/shard_map/ppermute | solution.py:354
Sparse Core Ops, SparseCore 0:
  78.5 81.8 all-gather.1

commit v2 on v1

--- a/solution.py
+++ b/solution.py
@@ -10,6 +10,7 @@
 F32 = jnp.float32
 BF16 = jnp.bfloat16
 ROWS = 8
+LINE = 4
 PARTS = (16, 8)
 
 
@@ -25,22 +26,21 @@
     return lax.dot_general(a, b, (dims, ((), ())), precision=precision, preferred_element_type=F32)
 
 
-def transposed(block):
-    tokens = block.shape[0]
-    eye = ones_where(iota((tokens, tokens), 0) == iota((tokens, tokens), 1))
-    return dot(block.astype(BF16), eye, ((0,), (0,)))
-
-
-def slot_of_token(ids, experts):
-    tokens, picks = ids.shape
-    ids_t = transposed(ids.astype(F32))
-    expert = iota((experts, tokens), 0).astype(F32)
-    match = jnp.zeros((experts, tokens), F32)
-    for k in range(picks):
-        match = match + jnp.where(ids_t[k : k + 1, :] == expert, 1.0, 0.0)
+def slot_of_token(ids_t, experts):
+    picks, tokens = ids_t.shape
+    match = matched(ids_t, jnp.ones((picks, tokens), F32), experts)
     before = ones_where(iota((tokens, tokens), 0) < iota((tokens, tokens), 1))
     rank = dot(match.astype(BF16), before)
-    return jnp.where(match > 0.0, rank, -1.0), ids_t
+    return jnp.where(match > 0.0, rank, -1.0)
+
+
+def matched(ids_t, values_t, experts):
+    picks, tokens = ids_t.shape
+    expert = iota((experts, tokens), 0)
+    result = jnp.zeros((experts, tokens), F32)
+    for k in range(picks):
+        result = result + jnp.where(ids_t[k : k + 1, :] == expert, values_t[k : k + 1, :], 0.0)
+    return result
 
 
 def spread(groups, slots=ROWS):
@@ -65,40 +65,49 @@
     return jnp.where(wide == wanted, 1.0, 0.0)
 
 
-def dispatch_body(experts, first, count, core_ref, ids_ref, rows_ref, out_ref, hot_ref):
+def dispatch_body(experts, core_ref, ids_ref, rows_ref, *refs):
+    out_refs, hot_refs = refs[: len(PARTS)], refs[len(PARTS) :]
+
     @pl.when(pl.program_id(0) == 0)
     def _():
-        slots, _unused = slot_of_token(ids_ref[...], experts)
-        hot_ref[...] = one_hot_slots(slots, first, count).astype(BF16)
-
-    out_ref[...] = dot(hot_ref[...], rows_ref[...]).astype(BF16)
-
-
-def dispatch(core, ids, rows, experts, first, count):
+        slots = slot_of_token(ids_ref[...], experts)
+        first = 0
+        for hot_ref, count in zip(hot_refs, PARTS):
+            hot_ref[...] = one_hot_slots(slots, first, count).astype(BF16)
+            first += count
+
+    rows = rows_ref[...]
+    for out_ref, hot_ref in zip(out_refs, hot_refs):
+        out_ref[...] = dot(hot_ref[...], rows).astype(BF16)
+
+
+def dispatch(core, ids_t, rows, experts):
     tokens, features = rows.shape
     half = features // 2
     block = min(512, half)
     steps = half // block
-    sent = experts * count
-    return pl.pallas_call(
-        functools.partial(dispatch_body, experts, first, count),
+    sizes = [experts * count for count in PARTS]
+    return pl.pallas_call(
+        functools.partial(dispatch_body, experts),
         grid_spec=pltpu.PrefetchScalarGridSpec(
             num_scalar_prefetch=1,
             grid=(steps,),
             in_specs=[
-                pl.BlockSpec(ids.shape, lambda n, c: (0, 0)),
+                pl.BlockSpec(ids_t.shape, lambda n, c: (0, 0)),
                 pl.BlockSpec((tokens, block), lambda n, c: (0, c[0] * steps + n)),
             ],
-            out_specs=pl.BlockSpec((sent, block), lambda n, c: (0, n)),
-            scratch_shapes=[pltpu.VMEM((sent, tokens), BF16)],
-        ),
-        out_shape=jax.ShapeDtypeStruct((sent, half), BF16),
+            out_specs=[pl.BlockSpec((size, block), lambda n, c: (0, n)) for size in sizes],
+            scratch_shapes=[pltpu.VMEM((size, tokens), BF16) for size in sizes],
+        ),
+        out_shape=[jax.ShapeDtypeStruct((size, half), BF16) for size in sizes],
         cost_estimate=pl.CostEstimate(
-            flops=2 * sent * tokens * half, bytes_accessed=2 * sent * half, transcendentals=0
+            flops=2 * sum(sizes) * tokens * half,
+            bytes_accessed=2 * sum(sizes) * half,
+            transcendentals=0,
         ),
         compiler_params=pltpu.CompilerParams(vmem_limit_bytes=24 * 1024 * 1024),
         name="dispatch_rows",
-    )(core, ids, rows)
+    )(core, ids_t, rows)
 
 
 def experts_body(groups, pairs, count, steps, last, core_ref, own_ref, other_ref, go_ref, gx_ref, uo_ref, ux_ref, a_ref, *refs):
@@ -182,46 +191,77 @@
     )(core, own, other, gate, gate, up, up, adapter_a, *before)
 
 
-def project_body(experts, chunks, core_ref, ids_ref, readout_ref, adapters_ref, out_ref):
-    rank = adapters_ref.shape[0] // experts
-    rows = experts * ROWS
-    slots, _unused = slot_of_token(ids_ref[...], experts)
-    every = dot(readout_ref[...], adapters_ref[...], ((1,), (1,))).astype(BF16)
-    width = experts * rank
-    own_expert = iota((rows, width), 0) // ROWS == iota((rows, width), 1) // rank
-    fold = ones_where(iota((width, ROWS * rank), 0) % rank == iota((width, ROWS * rank), 1) % rank)
+def project_body(*refs):
+    readout_refs, adapter_refs, out_refs = refs[:LINE], refs[LINE : 2 * LINE], refs[2 * LINE :]
+    adapters = jnp.concatenate([ref[...] for ref in adapter_refs], axis=0)
+    for readout_ref, out_ref in zip(readout_refs, out_refs):
+        out_ref[...] = dot(readout_ref[...], adapters, ((1,), (1,))).astype(BF16)
+
+
+def project(readouts, adapters):
+    tokens, half = readouts[0].shape
+    width = LINE * adapters[0].shape[0]
+    return pl.pallas_call(
+        project_body,
+        out_shape=[jax.ShapeDtypeStruct((tokens, width), BF16)] * LINE,
+        cost_estimate=pl.CostEstimate(
+            flops=2 * LINE * tokens * width * half,
+            bytes_accessed=2 * half * (LINE * tokens + width),
+            transcendentals=0,
+        ),
+        compiler_params=pltpu.CompilerParams(vmem_limit_bytes=24 * 1024 * 1024),
+        name="project_readout",
+    )(*readouts, *adapters)
+
+
+def pick_body(experts, chunks, place_ref, ids_ref, *refs):
+    piece_refs, out_ref = refs[:LINE], refs[LINE]
+    slots = slot_of_token(ids_ref[...], experts)
+    part = experts // LINE
+    every = piece_refs[0].shape[1]
+    rank = every // part
+    rows, width = part * ROWS, ROWS * rank
+    own_expert = iota((rows, every), 0) // ROWS == iota((rows, every), 1) // rank
+    fold = ones_where(iota((every, width), 0) % rank == iota((every, width), 1) % rank)
     lanes = own_lanes(rows, rank)
+    shape = (rows, experts)
     for c in range(chunks):
-        hot = one_hot_slots(slots, c * ROWS).astype(BF16)
-        picked = jnp.where(own_expert, dot(hot, every), 0.0).astype(BF16)
-        placed = jnp.where(lanes, dot(picked, fold), 0.0).astype(BF16)
-        out_ref[:, c * ROWS * rank : (c + 1) * ROWS * rank] = dot(gathered(experts), placed)
-
-
-def project(core, ids, readout, adapters, experts, chunks):
-    tokens, features = readout.shape
-    half = features // 2
-    rank = adapters.shape[0] // experts
-    return pl.pallas_call(
-        functools.partial(project_body, experts, chunks),
+        total = jnp.zeros((experts, width), F32)
+        for step, piece_ref in enumerate(piece_refs):
+            back = iota(shape, 0) // ROWS
+            expert = (place_ref[0] - back // LINE) % LINE
+            expert = expert * LINE + (place_ref[1] - back % LINE) % LINE
+            expert = expert * LINE + (place_ref[2] + step) % LINE
+            pick = ones_where(expert == iota(shape, 1))
+            wide = dot(pick, slots.astype(BF16))
+            wanted = (iota(wide.shape, 0) % ROWS + c * ROWS).astype(F32)
+            picked = dot(ones_where(wide == wanted), piece_ref[...])
+            picked = jnp.where(own_expert, picked, 0.0).astype(BF16)
+            placed = jnp.where(lanes, dot(picked, fold), 0.0).astype(BF16)
+            total = total + dot(pick, placed, ((0,), (0,)))
+        out_ref[:, c * width : (c + 1) * width] = total
+
+
+def pick(place, ids_t, pieces, experts, chunks):
+    full = lambda shape: pl.BlockSpec(shape, lambda n, c: (0,) * len(shape))
+    rank = pieces[0].shape[1] * LINE // experts
+    out = (experts, chunks * ROWS * rank)
+    return pl.pallas_call(
+        functools.partial(pick_body, experts, chunks),
         grid_spec=pltpu.PrefetchScalarGridSpec(
             num_scalar_prefetch=1,
             grid=(1,),
-            in_specs=[
-                pl.BlockSpec(ids.shape, lambda n, c: (0, 0)),
-                pl.BlockSpec((tokens, half), lambda n, c: (0, c[0])),
-                pl.BlockSpec(adapters.shape, lambda n, c: (0, 0)),
-            ],
-            out_specs=pl.BlockSpec((experts, chunks * ROWS * rank), lambda n, c: (0, 0)),
-        ),
-        out_shape=jax.ShapeDtypeStruct((experts, chunks * ROWS * rank), F32),
-        compiler_params=pltpu.CompilerParams(vmem_limit_bytes=48 * 1024 * 1024),
-        name="project_readout",
-    )(core, ids, readout, adapters)
-
-
-def weigh_body(experts, pairs, chunks, core_ref, ids_ref, gains_ref, mask_ref, latent_ref, own_ref, other_ref, readout_ref, log_ref, out_ref, lift_ref):
-    tokens, picks = ids_ref.shape
+            in_specs=[full(ids_t.shape)] + [full(x.shape) for x in pieces],
+            out_specs=full(out),
+        ),
+        out_shape=jax.ShapeDtypeStruct(out, F32),
+        compiler_params=pltpu.CompilerParams(vmem_limit_bytes=24 * 1024 * 1024),
+        name="pick_projections",
+    )(place, ids_t, *pieces)
+
+
+def weigh_body(experts, pairs, chunks, ids_ref, gains_ref, mask_ref, latent_ref, own_ref, other_ref, readout_ref, log_ref, out_ref, lift_ref):
+    tokens = ids_ref.shape[1]
     width = latent_ref.shape[2]
     rank = width // ROWS
     rows = experts * ROWS
@@ -229,12 +269,8 @@
 
     @pl.when(pl.program_id(0) == 0)
     def _():
-        slots, ids_t = slot_of_token(ids_ref[...], experts)
-        gains_t = transposed(gains_ref[...])
-        expert = iota((experts, tokens), 0).astype(F32)
-        gains = jnp.zeros((experts, tokens), F32)
-        for k in range(picks):
-            gains = gains + jnp.where(ids_t[k : k + 1, :] == expert, gains_t[k : k + 1, :], 0.0)
+        slots = slot_of_token(ids_ref[...], experts)
+        gains = matched(ids_ref[...], gains_ref[...].astype(F32), experts)
         spread_rows = spread(experts)
         lanes = own_lanes(rows, rank)
         first = iota((rows, width), 1) % rank == 0
@@ -283,34 +319,23 @@
         out_ref[:, :, n * block : (n + 1) * block] = part.reshape(experts, rank, block)
 
 
-def weigh(core, ids, gains, mask, latents, own, other, readout, experts, pairs, chunks):
-    tokens = ids.shape[0]
-    half = readout.shape[1] // pairs
+def weigh(ids_t, gains_t, mask, latents, own, other, readout, experts, pairs, chunks):
+    tokens, half = readout.shape
     width = latents.shape[2]
     rank = width // ROWS
-    full = lambda shape: pl.BlockSpec(shape, lambda n, c: (0,) * len(shape))
+    full = lambda shape: pl.BlockSpec(shape, lambda n: (0,) * len(shape))
+    args = (ids_t, gains_t, mask, latents, own, other, readout)
     out = (experts, rank, half + width)
     return pl.pallas_call(
         functools.partial(weigh_body, experts, pairs, chunks),
-        grid_spec=pltpu.PrefetchScalarGridSpec(
-            num_scalar_prefetch=1,
-            grid=(1,),
-            in_specs=[
-                full(ids.shape),
-                full(gains.shape),
-                full(mask.shape),
-                full(latents.shape),
-                full(own.shape),
-                full(other.shape),
-                pl.BlockSpec((tokens, half), lambda n, c: (0, c[0])),
-            ],
-            out_specs=[full((1, tokens)), full(out)],
-            scratch_shapes=[pltpu.VMEM((experts * rank, tokens), BF16)],
-        ),
+        grid=(1,),
+        in_specs=[full(x.shape) for x in args],
+        out_specs=[full((1, tokens)), full(out)],
+        scratch_shapes=[pltpu.VMEM((experts * rank, tokens), BF16)],
         out_shape=[jax.ShapeDtypeStruct((1, tokens), F32), jax.ShapeDtypeStruct(out, BF16)],
         compiler_params=pltpu.CompilerParams(vmem_limit_bytes=40 * 1024 * 1024),
         name="weigh_tokens",
-    )(core, ids, gains, mask, latents, own, other, readout)
+    )(*args)
 
 
 def gradients_body(groups, packed_ref, *refs):
@@ -354,6 +379,16 @@
     return lax.ppermute(payload, "narrow", [(0, 1), (1, 0)])
 
 
+def moved(payload, groups, stride, step):
+    if step == 0:
+        return payload
+    moves = []
+    for i in range(groups):
+        at = i // stride % LINE
+        moves.append((i, i + ((at + step) % LINE - at) * stride))
+    return lax.ppermute(payload, "wide", moves)
+
+
 def exchange(payload):
     return lax.all_to_all(payload, "wide", split_axis=0, concat_axis=0, tiled=True)
 
@@ -379,38 +414,43 @@
     side = lax.axis_index("narrow")
     core = side.reshape(1).astype(jnp.int32)
 
+    wide = lax.axis_index("wide")
+    place = jnp.stack([wide // LINE**2, wide // LINE % LINE, wide % LINE]).astype(jnp.int32)
+
+    ids_t, gains_t = route_ids.T, route_weights.T
     own_b = lax.dynamic_slice_in_dim(adapter_b[0], side * half, half, 1)
-    own_b, route_ids = lax.optimization_barrier((own_b, route_ids))
-    adapters = lax.all_gather(own_b, "wide", axis=0, tiled=True)
-
-    own, first = [], 0
-    for count in PARTS:
-        sent = dispatch(core, route_ids, hidden_in, groups, first, count)
-        own.append(exchange(sent.reshape(groups, count, half)).reshape(groups * count, half))
-        first += count
-
-    hidden, latents = [], []
-    for part, x in enumerate(own):
-        if hidden:
-            x, hidden[-1] = lax.optimization_barrier((x, hidden[-1]))
-        acts, sums = experts_forward(
-            core, x, swap(x), gate_proj, up_proj, adapter_a, latents, groups, pairs, part == len(own) - 1
-        )
-        hidden.append(acts)
-        latents.append(sums)
-    projections = project(core, route_ids, readout, adapters, groups, chunks)
+    own_readout = lax.dynamic_slice_in_dim(readout, side * half, half, 1)
+
+    sent = dispatch(core, ids_t, hidden_in, groups)
+    x = exchange(sent[0].reshape(groups, PARTS[0], half)).reshape(groups * PARTS[0], half)
+    y = exchange(sent[1].reshape(groups, PARTS[1], half)).reshape(groups * PARTS[1], half)
+    acts, sums = experts_forward(
+        core, x, swap(x), gate_proj, up_proj, adapter_a, [], groups, pairs, False
+    )
+    adapters = [moved(own_b, groups, LINE, step) for step in range(LINE)]
+    acts, adapters = lax.optimization_barrier((acts, adapters))
+    adapters = jnp.concatenate(adapters, axis=0)
+    y, acts, adapters, own_readout = lax.optimization_barrier((y, acts, adapters, own_readout))
+    adapters = [moved(adapters, groups, LINE**2, step) for step in range(LINE)]
+    readouts = [moved(own_readout, groups, 1, step) for step in range(LINE)]
+    last_acts, latents = experts_forward(
+        core, y, swap(y), gate_proj, up_proj, adapter_a, [sums], groups, pairs, True
+    )
+    hidden = [acts, last_acts]
+    pieces = project(readouts, adapters)
+    pieces = [moved(piece, groups, 1, -step) for step, piece in enumerate(pieces)]
+    projections = pick(place, ids_t, pieces, groups, chunks)
     home_latents = lax.all_to_all(
-        latents[-1], ("wide", "narrow"), split_axis=0, concat_axis=0, tiled=True
+        latents, ("wide", "narrow"), split_axis=0, concat_axis=0, tiled=True
     )
     log_ratio, packed = weigh(
-        core,
-        route_ids,
-        route_weights,
+        ids_t,
+        gains_t,
         forget_mask.reshape(1, tokens),
         home_latents,
         projections,
         swap(projections),
-        readout,
+        own_readout,
         groups,
         pairs,
         chunks,

time: 249 us -> 232 us (0.932)
  waiting for transfers between devices: 35.1 us -> 13.4 us
  starting transfers between devices: 17.5 us -> 35.1 us
  between operations: 14.2 us -> 0.85 us
    all_gather x1 -> x0, waiting for transfers between devices: 21.4 us -> none  [on_device(): adapters = lax.all_gather(own_b, 'wide', axis=0, tiled=True)]
    ppermute x0 -> x12, starting transfers between devices: none -> 14.8 us  [moved(): return lax.ppermute(payload, 'wide', moves)]
    ppermute x0 -> x12, waiting for transfers between devices: none -> 10.9 us  [moved(): return lax.ppermute(payload, 'wide', moves)]
    all_to_all x1, waiting for transfers between devices: 8.15 us -> 0.55 us  [exchange(): lax.all_to_all(payload, 'wide', split_axis=0, concat_axis=0, tiled=True)]
    ppermute x4, waiting for transfers between devices: 5.59 us -> 1.94 us  [swap(): return lax.ppermute(payload, 'narrow', [(0, 1), (1, 0)])]
    unnamed x27 -> x32, local copies, waits for them, and re-layouts: 7.17 us -> 5.8 us
  transfers between devices with their start and end apart: 7 -> 18, of which waited for: 5 -> 8; matrix products, arithmetic and copies ran while one was open for 0% -> 0% of each run, Pallas kernels for 15% -> 16%
where the time goes in v2:
time: 232 us
  blocking collectives  125 us (54%)
  Pallas kernels  50 us (22%)
  starting transfers between devices  35.1 us (15%)
  waiting for transfers between devices  13.4 us (6%)
  local copies, waits for them, and re-layouts  6.64 us (3%)
    all_to_all x2, blocking collectives, exchange(): lax.all_to_all(payload, 'wide', split_axis=0, concat_axis=0, tiled=True)  125 us
    pallas_call x2, Pallas kernels, experts_forward(): pl.pallas_call(functools.partial(experts_body, groups, pairs, count, step...  31.4 us
    ppermute x12, starting transfers between devices, moved(): return lax.ppermute(payload, 'wide', moves)  14.8 us
    ppermute x12, waiting for transfers between devices, moved(): return lax.ppermute(payload, 'wide', moves)  10.9 us
    ppermute x4, starting transfers between devices, swap(): return lax.ppermute(payload, 'narrow', [(0, 1), (1, 0)])  8.11 us
    all_to_all x1, starting transfers between devices, on_device(): lax.all_to_all(latents, ('wide', 'narrow'), split_axis=0, concat_axis=0,...  6.95 us
    pallas_call x1, Pallas kernels, weigh(): pl.pallas_call(functools.partial(weigh_body, experts, pairs, chunks), gri...  6.19 us
    unnamed x32, local copies, waits for them, and re-layouts  5.8 us
  transfers between devices with their start and end apart: 18, of which 8 were waited for; matrix products, arithmetic and copies ran while one was open for 0% of the time, Pallas kernels for 16%

profile of v2, /device:TPU:1, one launch (start us, length us, event | category | flops | bytes accessed | tf_op | source)
XLA Modules:
  0.0 231.8 jit_solution(4191679422411761250)
XLA Ops:
  0.6 0.0 copy-start
  0.7 0.0 copy-start.10
  0.7 0.8 copy-done.10
  1.4 1.2 copy-done.14
  2.7 3.2 %dispatch_rows.1 = (bf16[1024,2048]{1,0:T(8,128)(2,1)S(1)}, bf16[512,2048]{1,0:T(8,128)(2,1)S(1)}) custom-call(s32[1]{0:T(128)} %bitcast.3.core_ref, s32[8,128]{1,0:T(8,128)S(1)} %bitcast.22, bf16[128,4096]{1,0:T(8,128)(2,1)S(1)} %copy-done.14), custom_call_target="tpu_custom_call" | custom-call | flops 805306368 | bytes 6291456 | tf_op jit(solution)/shard_map/dispatch_rows/pallas_call | solution.py:90
  5.9 62.1 %all_to_all.20 = bf16[64,16,2048]{2,1,0:T(8,128)(2,1)} all-to-all(bf16[64,16,2048]{2,1,0:T(8,128)(2,1)S(1)} %bitcast.19), channel_id=1, replica_groups=mesh['wide'=64,'narrow'=2] {'wide'}, dimensions={0} | all-to-all | bytes 8388608 | tf_op jit(solution)/shard_map/all_to_all | solution.py:393
  67.9 2.8 %collective-permute-start = (bf16[1024,2048]{1,0:T(8,128)(2,1)}, bf16[1024,2048]{1,0:T(8,128)(2,1)}, u32[]{:S(2)}, u32[]{:S(2)}) collective-permute-start(bf16[1024,2048]{1,0:T(8,128)(2,1)} %bitcast.7.own_ref), channel_id=1, source_target_pairs={{0,1},{1,0},{2,3},{3,2},{4,5},{5,4},{6,7},{7,6},{8,9},{9,8},{10,11... | collective-permute-start | bytes 12582920 | tf_op jit(solution)/shard_map/ppermute | solution.py:379
  70.8 5.3 %all-to-all-start = ((bf16[64,8,2048]{2,1,0:T(8,128)(2,1)}), bf16[64,8,2048]{2,1,0:T(8,128)(2,1)S(1)}, u32[]{:S(2)}, u32[]{:S(2)}) async-start(bf16[64,8,2048]{2,1,0:T(8,128)(2,1)} %bitcast.20), calls=%async_computation | async-start | bytes 4194304 | tf_op jit(solution)/shard_map/all_to_all | solution.py:393
  76.1 1.1 collective-permute-start.1
  77.2 2.4 %collective-permute-start.2 = (bf16[16,2048]{1,0:T(8,128)(2,1)S(1)}, bf16[16,2048]{1,0:T(8,128)(2,1)S(1)}, u32[]{:S(2)}, u32[]{:S(2)}) collective-permute-start(bf16[16,2048]{1,0:T(8,128)(2,1)S(1)} %dynamic-slice_bitcast_fusion), channel_id=1, source_target_pairs={{0,16},{2,18},{4,20},{6,22},{8,24},{10,26},{12,28},{14,30},{16,0},... | collective-permute-start | bytes 196616 | tf_op jit(solution)/shard_map/ppermute | solution.py:389
  79.6 1.2 collective-permute-start.3
  80.8 0.8 constant_dynamic-slice_fusion.refs_0_.readout_ref
  81.6 0.0 collective-permute-done.other_ref
  81.6 19.8 %experts_forward.2 = (bf16[1024,768]{1,0:T(8,128)(2,1)S(1)}, bf16[128,256]{1,0:T(8,128)(2,1)S(1)}) custom-call(s32[1]{0:T(128)} %bitcast.3.core_ref, bf16[1024,2048]{1,0:T(8,128)(2,1)} %bitcast.7.own_ref, bf16[1024,2048]{1,0:T(8,128)(2,1)} %collective-permute-done.other_ref, bf16[1,4096,768]{2,1,0:T(8,128)(2,1)} %gx_ref.3, bf16[1,4096,768]{2,1,0:T(8,128)(2,1)} %gx_ref.3, ...), custom_call_target="tpu_custom_call" | custom-call | flops 12884901888 | bytes 20971520 | tf_op jit(solution)/shard_map/experts_forward/pallas_call | solution.py:168
  101.4 1.1 copy-done.4
  102.6 1.5 collective-permute-done.2
  104.1 0.5 all-to-all-done
  104.6 2.2 collective-permute-start.4
  106.8 1.1 collective-permute-start.5
  107.9 2.4 %collective-permute-start.6 = (bf16[128,2048]{1,0:T(8,128)(2,1)}, bf16[128,2048]{1,0:T(8,128)(2,1)}, u32[]{:S(2)}, u32[]{:S(2)}) collective-permute-start(bf16[128,2048]{1,0:T(8,128)(2,1)} %constant_dynamic-slice_fusion.refs_0_.readout_ref), channel_id=1, source_target_pairs={{0,4},{2,6},{4,0},{6,2},{8,12},{10,14},{12,8},{14,10},{16,20},{18,... | collective-permute-start | bytes 1572872 | tf_op jit(solution)/shard_map/ppermute | solution.py:389
  110.3 1.2 collective-permute-start.7
  111.5 4.6 %collective-permute-done.8.refs_5_ = bf16[64,2048]{1,0:T(8,128)(2,1)} collective-permute-done((bf16[64,2048]{1,0:T(8,128)(2,1)S(1)}, bf16[64,2048]{1,0:T(8,128)(2,1)}, u32[]{:S(2)}, u32[]{:S(2)}) %collective-permute-start.8) | collective-permute-done | bytes 262176 | tf_op jit(solution)/shard_map/ppermute | solution.py:389
  116.1 0.2 collective-permute-start.9
  116.3 1.0 collective-permute-start.10
  117.3 11.6 %experts_forward.3 = (bf16[512,768]{1,0:T(8,128)(2,1)S(1)}, bf16[128,8,128]{2,1,0:T(8,128)(2,1)S(1)}) custom-call(s32[1]{0:T(128)} %bitcast.3.core_ref, bf16[512,2048]{1,0:T(8,128)(2,1)S(1)} %bitcast.18, bf16[512,2048]{1,0:T(8,128)(2,1)} %collective-permute-done.4.other_ref, bf16[1,4096,768]{2,1,0:T(8,128)(2,1)} %gx_ref.3, bf16[1,4096,768]{2,1,0:T(8,128)(2,1)} %gx_ref.3, ...), custom_call_target="tpu_custom_call" | custom-call | flops 6442450944 | bytes 16777216 | tf_op jit(solution)/shard_map/experts_forward/pallas_call | solution.py:168
  129.0 0.9 copy-done.6
  129.8 0.7 copy-done.8
  130.6 7.0 %all-to-all-start.2 = ((bf16[128,8,128]{2,1,0:T(8,128)(2,1)}), bf16[128,8,128]{2,1,0:T(8,128)(2,1)S(1)}, u32[]{:S(2)}, u32[]{:S(2)}) async-start(bf16[128,8,128]{2,1,0:T(8,128)(2,1)} %copy-done.8), calls=%async_computation.2 | async-start | bytes 524288 | tf_op jit(solution)/shard_map/all_to_all | solution.py:443
  137.5 0.0 collective-permute-done.10.refs_7_
  137.5 0.0 collective-permute-done.5.refs_1_
  137.6 1.0 copy-done.1
  138.6 3.0 %project_readout.1 = (bf16[128,256]{1,0:T(8,128)(2,1)S(1)}, bf16[128,256]{1,0:T(8,128)(2,1)S(1)}, bf16[128,256]{1,0:T(8,128)(2,1)S(1)}, bf16[128,256]{1,0:T(8,128)(2,1)S(1)}) custom-call(bf16[128,2048]{1,0:T(8,128)(2,1)S(1)} %copy-done.1, bf16[128,2048]{1,0:T(8,128)(2,1)} %collective-permute-done.5.refs_1_, ...), custom_call_target="tpu_custom_call" | custom-call | flops 536870912 | bytes 3145728 | tf_op jit(solution)/shard_map/project_readout/pallas_call | solution.py:204
  141.6 3.3 %collective-permute-start.11 = (bf16[128,256]{1,0:T(8,128)(2,1)S(1)}, bf16[128,256]{1,0:T(8,128)(2,1)S(1)}, u32[]{:S(2)}, u32[]{:S(2)}) collective-permute-start(bf16[128,256]{1,0:T(8,128)(2,1)S(1)} %get-tuple-element.40), channel_id=1, source_target_pairs={{0,6},{2,0},{4,2},{6,4},{8,14},{10,8},{12,10},{14,12},{16,22},{18,... | collective-permute-start | bytes 196616 | tf_op jit(solution)/shard_map/ppermute | solution.py:389
  145.0 0.1 collective-permute-start.12
  145.1 0.8 collective-permute-start.13
  145.8 0.1 pad_add_fusion.place_ref
  145.9 0.4 collective-permute-done.11.refs_1_
  146.3 3.3 %collective-permute-done.12.refs_2_ = bf16[128,256]{1,0:T(8,128)(2,1)S(1)} collective-permute-done((bf16[128,256]{1,0:T(8,128)(2,1)S(1)}, bf16[128,256]{1,0:T(8,128)(2,1)S(1)}, u32[]{:S(2)}, u32[]{:S(2)}) %collective-permute-start.12) | collective-permute-done | bytes 65568 | tf_op jit(solution)/shard_map/ppermute | solution.py:389
  149.6 1.1 collective-permute-done.13.refs_3_
  150.8 3.5 %pick_projections.1.own_ref = f32[64,384]{1,0:T(8,128)S(1)} custom-call(s32[3]{0:T(128)S(1)} %pad_add_fusion.place_ref, s32[8,128]{1,0:T(8,128)S(1)} %bitcast.23, bf16[128,256]{1,0:T(8,128)(2,1)S(1)} %get-tuple-element.39.refs_0_, bf16[128,256]{1,0:T(8,128)(2,1)S(1)} %collective-permute-done.11.refs_1_, ...), custom_call_target="tpu_custom_call" | custom-call | tf_op jit(solution)/shard_map/pick_projections/pallas_call | solution.py:249
  154.2 1.5 collective-permute-start.14
  155.7 0.9 collective-permute-done.14.other_ref
  156.7 6.2 %weigh_tokens.1 = (f32[1,128]{1,0:T(1,128)}, bf16[64,16,2176]{2,1,0:T(8,128)(2,1)S(1)}) custom-call(s32[8,128]{1,0:T(8,128)S(1)} %bitcast.24, bf16[8,128]{1,0:T(8,128)(2,1)S(1)} %bitcast.25, s32[1,128]{1,0:T(1,128)S(1)} %bitcast.26, bf16[128,8,128]{2,1,0:T(8,128)(2,1)S(1)} %all-to-all-done.2.latent_ref, f32[64,384]{1,0:T(8,128)S(1)} %pick_projections.1.own_ref, ...), custom_call_target="tpu_custom_call" | custom-call | tf_op jit(solution)/shard_map/weigh_tokens/pallas_call | solution.py:329
  162.9 62.9 %all_to_all.21.packed_ref = bf16[64,16,2176]{2,1,0:T(8,128)(2,1)S(1)} all-to-all(bf16[64,16,2176]{2,1,0:T(8,128)(2,1)S(1)} %get-tuple-element.44), channel_id=1, replica_groups=mesh['wide'=64,'narrow'=2] {'wide'}, dimensions={0} | all-to-all | bytes 8912896 | tf_op jit(solution)/shard_map/all_to_all | solution.py:393
  225.8 2.7 %adapter_gradients.1 = (f32[16,768]{1,0:T(8,128)}, f32[16,2048]{1,0:T(8,128)S(1)}) custom-call(bf16[64,16,2176]{2,1,0:T(8,128)(2,1)S(1)} %all_to_all.21.packed_ref, bf16[1024,768]{1,0:T(8,128)(2,1)S(1)} %copy-done.5, bf16[512,768]{1,0:T(8,128)(2,1)S(1)} %copy-done.7), custom_call_target="tpu_custom_call" | custom-call | tf_op jit(solution)/shard_map/adapter_gradients/pallas_call | solution.py:367
  228.5 1.6 collective-permute-start.15
  230.1 1.0 collective-permute-done.15
  231.1 0.7 maximum_select_fusion
  (34 shorter events, 0.1 us)
Async XLA Ops:
  0.6 80.1 %copy-start = (bf16[128,4096]{1,0:T(8,128)(2,1)S(1)}, bf16[128,4096]{1,0:T(8,128)(2,1)}, u32[]{:S(2)}) copy-start(bf16[128,4096]{1,0:T(8,128)(2,1)} %param.10) | copy-start | bytes 3145732
  0.7 0.8 copy-start.10
  1.4 1.2 copy-start.14
  5.9 62.1 %copy-start.3 = (bf16[512,2048]{1,0:T(8,128)(2,1)}, bf16[512,2048]{1,0:T(8,128)(2,1)S(1)}, u32[]{:S(2)}) copy-start(bf16[512,2048]{1,0:T(8,128)(2,1)S(1)} %get-tuple-element.26) | copy-start | bytes 6291460
  67.9 8.1 %copy-start.15 = (bf16[1,16,4096]{2,1,0:T(8,128)(2,1)S(1)}, bf16[1,16,4096]{2,1,0:T(8,128)(2,1)}, u32[]{:S(2)}) copy-start(bf16[1,16,4096]{2,1,0:T(8,128)(2,1)} %param.17) | copy-start | bytes 393220
  67.9 13.7 %copy-start.9 = (bf16[1,16,768]{2,1,0:T(8,128)(2,1)S(1)}, bf16[1,16,768]{2,1,0:T(8,128)(2,1)}, u32[]{:S(2)}) copy-start(bf16[1,16,768]{2,1,0:T(8,128)(2,1)} %a_ref.3) | copy-start | bytes 73732
  67.9 13.7 %collective-permute-start = (bf16[1024,2048]{1,0:T(8,128)(2,1)}, bf16[1024,2048]{1,0:T(8,128)(2,1)}, u32[]{:S(2)}, u32[]{:S(2)}) collective-permute-start(bf16[1024,2048]{1,0:T(8,128)(2,1)} %bitcast.7.own_ref), channel_id=1, source_target_pairs={{0,1},{1,0},{2,3},{3,2},{4,5},{5,4},{6,7},{7,6},{8,9},{9,8},{10,11... | collective-permute-start | bytes 12582920 | tf_op jit(solution)/shard_map/ppermute | solution.py:379
  70.8 33.9 %all-to-all-start = ((bf16[64,8,2048]{2,1,0:T(8,128)(2,1)}), bf16[64,8,2048]{2,1,0:T(8,128)(2,1)S(1)}, u32[]{:S(2)}, u32[]{:S(2)}) async-start(bf16[64,8,2048]{2,1,0:T(8,128)(2,1)} %bitcast.20), calls=%async_computation | async-start | bytes 4194304 | tf_op jit(solution)/shard_map/all_to_all | solution.py:393
  76.1 26.5 %collective-permute-start.1 = (bf16[16,2048]{1,0:T(8,128)(2,1)S(1)}, bf16[16,2048]{1,0:T(8,128)(2,1)S(1)}, u32[]{:S(2)}, u32[]{:S(2)}) collective-permute-start(bf16[16,2048]{1,0:T(8,128)(2,1)S(1)} %dynamic-slice_bitcast_fusion), channel_id=1, source_target_pairs={{0,8},{2,10},{4,12},{6,14},{8,16},{10,18},{12,20},{14,22},{16,24},... | collective-permute-start | bytes 196616 | tf_op jit(solution)/shard_map/ppermute | solution.py:389
  77.2 26.9 %collective-permute-start.2 = (bf16[16,2048]{1,0:T(8,128)(2,1)S(1)}, bf16[16,2048]{1,0:T(8,128)(2,1)S(1)}, u32[]{:S(2)}, u32[]{:S(2)}) collective-permute-start(bf16[16,2048]{1,0:T(8,128)(2,1)S(1)} %dynamic-slice_bitcast_fusion), channel_id=1, source_target_pairs={{0,16},{2,18},{4,20},{6,22},{8,24},{10,26},{12,28},{14,30},{16,0},... | collective-permute-start | bytes 196616 | tf_op jit(solution)/shard_map/ppermute | solution.py:389
  79.6 24.5 %collective-permute-start.3 = (bf16[16,2048]{1,0:T(8,128)(2,1)S(1)}, bf16[16,2048]{1,0:T(8,128)(2,1)S(1)}, u32[]{:S(2)}, u32[]{:S(2)}) collective-permute-start(bf16[16,2048]{1,0:T(8,128)(2,1)S(1)} %dynamic-slice_bitcast_fusion), channel_id=1, source_target_pairs={{0,24},{2,26},{4,28},{6,30},{8,0},{10,2},{12,4},{14,6},{16,8},{18,... | collective-permute-start | bytes 196616 | tf_op jit(solution)/shard_map/ppermute | solution.py:389
  101.4 1.2 copy-start.4
  104.6 11.7 %collective-permute-start.4 = (bf16[512,2048]{1,0:T(8,128)(2,1)S(1)}, bf16[512,2048]{1,0:T(8,128)(2,1)}, u32[]{:S(2)}, u32[]{:S(2)}) collective-permute-start(bf16[512,2048]{1,0:T(8,128)(2,1)S(1)} %bitcast.17), channel_id=1, source_target_pairs={{0,1},{1,0},{2,3},{3,2},{4,5},{5,4},{6,7},{7,6},{8,9},{9,8},{10,11... | collective-permute-start | bytes 6291464 | tf_op jit(solution)/shard_map/ppermute | solution.py:379
  106.8 9.3 %collective-permute-start.8 = (bf16[64,2048]{1,0:T(8,128)(2,1)S(1)}, bf16[64,2048]{1,0:T(8,128)(2,1)}, u32[]{:S(2)}, u32[]{:S(2)}) collective-permute-start(bf16[64,2048]{1,0:T(8,128)(2,1)S(1)} %pad_maximum_fusion.refs_4_), channel_id=1, source_target_pairs={{0,32},{2,34},{4,36},{6,38},{8,40},{10,42},{12,44},{14,46},{16,48}... | collective-permute-start | bytes 786440 | tf_op jit(solution)/shard_map/ppermute | solution.py:389
  106.8 30.7 %collective-permute-start.5 = (bf16[128,2048]{1,0:T(8,128)(2,1)}, bf16[128,2048]{1,0:T(8,128)(2,1)}, u32[]{:S(2)}, u32[]{:S(2)}) collective-permute-start(bf16[128,2048]{1,0:T(8,128)(2,1)} %constant_dynamic-slice_fusion.refs_0_.readout_ref), channel_id=1, source_target_pairs={{0,2},{2,4},{4,6},{6,0},{8,10},{10,12},{12,14},{14,8},{16,18},{18,... | collective-permute-start | bytes 1572872 | tf_op jit(solution)/shard_map/ppermute | solution.py:389
  107.9 29.6 %collective-permute-start.6 = (bf16[128,2048]{1,0:T(8,128)(2,1)}, bf16[128,2048]{1,0:T(8,128)(2,1)}, u32[]{:S(2)}, u32[]{:S(2)}) collective-permute-start(bf16[128,2048]{1,0:T(8,128)(2,1)} %constant_dynamic-slice_fusion.refs_0_.readout_ref), channel_id=1, source_target_pairs={{0,4},{2,6},{4,0},{6,2},{8,12},{10,14},{12,8},{14,10},{16,20},{18,... | collective-permute-start | bytes 1572872 | tf_op jit(solution)/shard_map/ppermute | solution.py:389
  110.3 27.3 %collective-permute-start.7 = (bf16[128,2048]{1,0:T(8,128)(2,1)}, bf16[128,2048]{1,0:T(8,128)(2,1)}, u32[]{:S(2)}, u32[]{:S(2)}) collective-permute-start(bf16[128,2048]{1,0:T(8,128)(2,1)} %constant_dynamic-slice_fusion.refs_0_.readout_ref), channel_id=1, source_target_pairs={{0,6},{2,0},{4,2},{6,4},{8,14},{10,8},{12,10},{14,12},{16,22},{18,... | collective-permute-start | bytes 1572872 | tf_op jit(solution)/shard_map/ppermute | solution.py:389
  116.1 21.4 %collective-permute-start.9 = (bf16[64,2048]{1,0:T(8,128)(2,1)S(1)}, bf16[64,2048]{1,0:T(8,128)(2,1)}, u32[]{:S(2)}, u32[]{:S(2)}) collective-permute-start(bf16[64,2048]{1,0:T(8,128)(2,1)S(1)} %pad_maximum_fusion.refs_4_), channel_id=1, source_target_pairs={{0,64},{2,66},{4,68},{6,70},{8,72},{10,74},{12,76},{14,78},{16,80}... | collective-permute-start | bytes 786440 | tf_op jit(solution)/shard_map/ppermute | solution.py:389
  116.3 21.2 %collective-permute-start.10 = (bf16[64,2048]{1,0:T(8,128)(2,1)S(1)}, bf16[64,2048]{1,0:T(8,128)(2,1)}, u32[]{:S(2)}, u32[]{:S(2)}) collective-permute-start(bf16[64,2048]{1,0:T(8,128)(2,1)S(1)} %pad_maximum_fusion.refs_4_), channel_id=1, source_target_pairs={{0,96},{2,98},{4,100},{6,102},{8,104},{10,106},{12,108},{14,110},{... | collective-permute-start | bytes 786440 | tf_op jit(solution)/shard_map/ppermute | solution.py:389
  117.3 33.4 %copy-start.11 = (s32[128,8]{0,1:T(8,128)S(1)}, s32[128,8]{0,1:T(8,128)}, u32[]{:S(2)}) copy-start(s32[128,8]{0,1:T(8,128)} %param.11) | copy-start | bytes 12292
  117.3 39.3 %copy-start.12 = (bf16[128,8]{0,1:T(8,128)(2,1)S(1)}, bf16[128,8]{0,1:T(8,128)(2,1)}, u32[]{:S(2)}) copy-start(bf16[128,8]{0,1:T(8,128)(2,1)} %param.12) | copy-start | bytes 6148
  117.3 39.3 %copy-start.13 = (s32[128]{0:T(128)S(1)}, s32[128]{0:T(128)}, u32[]{:S(2)}) copy-start(s32[128]{0:T(128)} %param.13) | copy-start | bytes 1540
  129.0 0.9 copy-start.6
  129.8 0.7 copy-start.8
  130.5 26.1 %copy-start.2 = (bf16[128,2048]{1,0:T(8,128)(2,1)S(1)}, bf16[128,2048]{1,0:T(8,128)(2,1)}, u32[]{:S(2)}) copy-start(bf16[128,2048]{1,0:T(8,128)(2,1)} %constant_dynamic-slice_fusion.refs_0_.readout_ref) | copy-start | bytes 1572868
  130.6 26.1 %all-to-all-start.2 = ((bf16[128,8,128]{2,1,0:T(8,128)(2,1)}), bf16[128,8,128]{2,1,0:T(8,128)(2,1)S(1)}, u32[]{:S(2)}, u32[]{:S(2)}) async-start(bf16[128,8,128]{2,1,0:T(8,128)(2,1)} %copy-done.8), calls=%async_computation.2 | async-start | bytes 524288 | tf_op jit(solution)/shard_map/all_to_all | solution.py:443
  137.6 1.0 copy-start.1
  141.6 4.7 %collective-permute-start.11 = (bf16[128,256]{1,0:T(8,128)(2,1)S(1)}, bf16[128,256]{1,0:T(8,128)(2,1)S(1)}, u32[]{:S(2)}, u32[]{:S(2)}) collective-permute-start(bf16[128,256]{1,0:T(8,128)(2,1)S(1)} %get-tuple-element.40), channel_id=1, source_target_pairs={{0,6},{2,0},{4,2},{6,4},{8,14},{10,8},{12,10},{14,12},{16,22},{18,... | collective-permute-start | bytes 196616 | tf_op jit(solution)/shard_map/ppermute | solution.py:389
  145.0 4.7 %collective-permute-start.12 = (bf16[128,256]{1,0:T(8,128)(2,1)S(1)}, bf16[128,256]{1,0:T(8,128)(2,1)S(1)}, u32[]{:S(2)}, u32[]{:S(2)}) collective-permute-start(bf16[128,256]{1,0:T(8,128)(2,1)S(1)} %get-tuple-element.41), channel_id=1, source_target_pairs={{0,4},{2,6},{4,0},{6,2},{8,12},{10,14},{12,8},{14,10},{16,20},{18,... | collective-permute-start | bytes 196616 | tf_op jit(solution)/shard_map/ppermute | solution.py:389
  145.1 5.7 %collective-permute-start.13 = (bf16[128,256]{1,0:T(8,128)(2,1)S(1)}, bf16[128,256]{1,0:T(8,128)(2,1)S(1)}, u32[]{:S(2)}, u32[]{:S(2)}) collective-permute-start(bf16[128,256]{1,0:T(8,128)(2,1)S(1)} %get-tuple-element.42), channel_id=1, source_target_pairs={{0,2},{2,4},{4,6},{6,0},{8,10},{10,12},{12,14},{14,8},{16,18},{18,... | collective-permute-start | bytes 196616 | tf_op jit(solution)/shard_map/ppermute | solution.py:389
  154.2 2.4 %collective-permute-start.14 = (f32[64,384]{1,0:T(8,128)S(1)}, f32[64,384]{1,0:T(8,128)S(1)}, u32[]{:S(2)}, u32[]{:S(2)}) collective-permute-start(f32[64,384]{1,0:T(8,128)S(1)} %pick_projections.1.own_ref), channel_id=1, source_target_pairs={{0,1},{1,0},{2,3},{3,2},{4,5},{5,4},{6,7},{7,6},{8,9},{9,8},{10,11... | collective-permute-start | bytes 294920 | tf_op jit(solution)/shard_map/ppermute | solution.py:379
  162.9 62.9 %copy-start.5 = (bf16[1024,768]{1,0:T(8,128)(2,1)S(1)}, bf16[1024,768]{1,0:T(8,128)(2,1)}, u32[]{:S(2)}) copy-start(bf16[1024,768]{1,0:T(8,128)(2,1)} %copy-done.4) | copy-start | bytes 4718596
  162.9 62.9 %copy-start.7 = (bf16[512,768]{1,0:T(8,128)(2,1)S(1)}, bf16[512,768]{1,0:T(8,128)(2,1)}, u32[]{:S(2)}) copy-start(bf16[512,768]{1,0:T(8,128)(2,1)} %copy-done.6) | copy-start | bytes 2359300
  228.5 2.6 %collective-permute-start.15 = (f32[16,2048]{1,0:T(8,128)S(1)}, f32[16,2048]{1,0:T(8,128)S(1)}, u32[]{:S(2)}, u32[]{:S(2)}) collective-permute-start(f32[16,2048]{1,0:T(8,128)S(1)} %get-tuple-element.48), channel_id=1, source_target_pairs={{0,1},{1,0},{2,3},{3,2},{4,5},{5,4},{6,7},{7,6},{8,9},{9,8},{10,11... | collective-permute-start | bytes 393224 | tf_op jit(solution)/shard_map/ppermute | solution.py:379

commit v3 on v2

v3 whole, which is shorter than its diff:
```python
import functools

import jax
import jax.numpy as jnp
from jax import lax
from jax.experimental import pallas as pl
from jax.experimental.pallas import tpu as pltpu
from jax.sharding import PartitionSpec as P

F32 = jnp.float32
BF16 = jnp.bfloat16
ROWS = 8
LINE = 4
PARTS = (16, 8)


def iota(shape, dim):
    return lax.broadcasted_iota(jnp.int32, shape, dim)


def ones_where(condition, dtype=BF16):
    return jnp.where(condition, 1.0, 0.0).astype(dtype)


def dot(a, b, dims=((1,), (0,)), precision=None):
    return lax.dot_general(a, b, (dims, ((), ())), precision=precision, preferred_element_type=F32)


def slot_of_token(ids_t, expert):
    tokens = ids_t.shape[1]
    match = matched(ids_t, jnp.ones(ids_t.shape, F32), expert)
    before = ones_where(iota((tokens, tokens), 0) < iota((tokens, tokens), 1))
    rank = dot(match.astype(BF16), before)
    return jnp.where(match > 0.0, rank, -1.0)


def matched(ids_t, values_t, expert):
    result = jnp.zeros(expert.shape, F32)
    for k in range(ids_t.shape[0]):
        result = result + jnp.where(ids_t[k : k + 1, :] == expert, values_t[k : k + 1, :], 0.0)
    return result


def spread(groups, slots=ROWS):
    shape = (groups * slots, groups)
    return ones_where(iota(shape, 0) // slots == iota(shape, 1))


def gathered(groups):
    shape = (groups, groups * ROWS)
    return ones_where(iota(shape, 1) // ROWS == iota(shape, 0))


def full(shape):
    return pl.BlockSpec(shape, lambda *_: (0,) * len(shape))


def own_lanes(rows, rank, slots=ROWS):
    shape = (rows, slots * rank)
    return iota(shape, 0) % slots == iota(shape, 1) // rank


def one_hot_slots(slots, first, count=ROWS):
    rows = slots.shape[0] * count
    wide = dot(spread(slots.shape[0], count), slots.astype(BF16))
    wanted = (iota((rows, slots.shape[1]), 0) % count + first).astype(F32)
    return jnp.where(wide == wanted, 1.0, 0.0)


def dispatch_body(experts, core_ref, ids_ref, rows_ref, *refs):
    out_refs, hot_refs = refs[: len(PARTS)], refs[len(PARTS) :]

    @pl.when(pl.program_id(0) == 0)
    def _():
        expert = iota((experts, ids_ref.shape[1]), 0).astype(F32)
        slots = slot_of_token(ids_ref[...].astype(F32), expert)
        first = 0
        for hot_ref, count in zip(hot_refs, PARTS):
            hot_ref[...] = one_hot_slots(slots, first, count).astype(BF16)
            first += count

    rows = rows_ref[...]
    for out_ref, hot_ref in zip(out_refs, hot_refs):
        out_ref[...] = dot(hot_ref[...], rows).astype(BF16)


def dispatch(core, ids_t, rows, experts):
    tokens, features = rows.shape
    half = features // 2
    block = min(512, half)
    steps = half // block
    sizes = [experts * count for count in PARTS]
    return pl.pallas_call(
        functools.partial(dispatch_body, experts),
        grid_spec=pltpu.PrefetchScalarGridSpec(
            num_scalar_prefetch=1,
            grid=(steps,),
            in_specs=[
                pl.BlockSpec(ids_t.shape, lambda n, c: (0, 0)),
                pl.BlockSpec((tokens, block), lambda n, c: (0, c[0] * steps + n)),
            ],
            out_specs=[pl.BlockSpec((size, block), lambda n, c: (0, n)) for size in sizes],
            scratch_shapes=[pltpu.VMEM((size, tokens), BF16) for size in sizes],
        ),
        out_shape=[jax.ShapeDtypeStruct((size, half), BF16) for size in sizes],
        cost_estimate=pl.CostEstimate(
            flops=2 * sum(sizes) * tokens * half,
            bytes_accessed=2 * sum(sizes) * half,
            transcendentals=0,
        ),
        compiler_params=pltpu.CompilerParams(vmem_limit_bytes=24 * 1024 * 1024),
        name="dispatch_rows",
    )(core, ids_t, rows)


def experts_body(groups, count, steps, last, core_ref, own_ref, other_ref, go_ref, gx_ref, uo_ref, ux_ref, a_ref, *refs):
    before_refs, (hid_ref, lat_ref, acc_ref) = refs[:-3], refs[-3:]
    n = pl.program_id(0)
    own, other = own_ref[...], other_ref[...]
    gate = dot(own, go_ref[0]) + dot(other, gx_ref[0])
    up = dot(own, uo_ref[0]) + dot(other, ux_ref[0])
    hidden = (gate / (1.0 + jnp.exp(-gate)) * up).astype(BF16)
    hid_ref[...] = hidden
    rank = a_ref.shape[1]
    tiled = jnp.concatenate([a_ref[0]] * count, axis=0)
    part = dot(hidden, tiled, ((1,), (1,)))

    @pl.when(n == 0)
    def _():
        acc_ref[...] = part

    @pl.when(n > 0)
    def _():
        acc_ref[...] = acc_ref[...] + part

    @pl.when(n == steps - 1)
    def _():
        rows = groups * count
        mine = jnp.where(own_lanes(rows, rank, count), acc_ref[...], 0.0).astype(BF16)
        width = ROWS * rank
        shape = (groups // LINE, rows)
        for step in range(LINE):
            block = lax.rem(core_ref[1] + LINE - step, LINE)
            pick = ones_where(iota(shape, 1) // count == iota(shape, 0) * LINE + block)
            now = dot(pick, mine).astype(BF16)
            if last:
                at = step * LINE
                for piece in [ref[step] for ref in before_refs] + [now]:
                    for c in range(piece.shape[1] // width):
                        lat_ref[:, at, :] = piece[:, c * width : (c + 1) * width]
                        at += 1
                for c in range(at, (step + 1) * LINE):
                    lat_ref[:, c, :] = jnp.zeros((groups // LINE, width), BF16)
            else:
                lat_ref[step] = now


def experts_forward(core, own, other, gate, up, adapter_a, before, groups, last):
    rows, half = own.shape
    count = rows // groups
    hidden_units = gate.shape[2]
    rank = adapter_a.shape[1]
    block = min(256, hidden_units)
    steps = hidden_units // block
    width = count * rank
    mine = pl.BlockSpec((1, half, block), lambda n, c: (0, c[0], n))
    theirs = pl.BlockSpec((1, half, block), lambda n, c: (0, 1 - c[0], n))
    whole = pl.BlockSpec((rows, half), lambda n, c: (0, 0))
    in_specs = [whole, whole, mine, theirs, mine, theirs, pl.BlockSpec((1, rank, block), lambda n, c: (0, 0, n))]
    in_specs += [full(x.shape) for x in before]
    lines = groups // LINE
    out = (lines, LINE * LINE, ROWS * rank) if last else (LINE, lines, width)
    return pl.pallas_call(
        functools.partial(experts_body, groups, count, steps, last),
        grid_spec=pltpu.PrefetchScalarGridSpec(
            num_scalar_prefetch=1,
            grid=(steps,),
            in_specs=in_specs,
            out_specs=[
                pl.BlockSpec((rows, block), lambda n, c: (0, n)),
                full(out),
            ],
            scratch_shapes=[pltpu.VMEM((rows, width), F32)],
        ),
        out_shape=[
            jax.ShapeDtypeStruct((rows, hidden_units), BF16),
            jax.ShapeDtypeStruct(out, BF16),
        ],
        cost_estimate=pl.CostEstimate(
            flops=8 * rows * half * hidden_units,
            bytes_accessed=8 * half * hidden_units + 4 * rows * half,
            transcendentals=rows * hidden_units,
        ),
        compiler_params=pltpu.CompilerParams(vmem_limit_bytes=48 * 1024 * 1024),
        name="experts_forward",
    )(core, own, other, gate, gate, up, up, adapter_a, *before)


def project_body(tokens, *refs):
    readout_refs, adapter_refs, out_ref = refs[:LINE], refs[LINE : 2 * LINE], refs[2 * LINE]
    adapters = jnp.concatenate([ref[...] for ref in adapter_refs], axis=0)
    for step, ref in enumerate(readout_refs):
        out_ref[step * tokens : (step + 1) * tokens, :] = dot(ref[:tokens, :], adapters, ((1,), (1,)))


def project(readouts, adapters, tokens):
    half = readouts[0].shape[1]
    width = LINE * adapters[0].shape[0]
    return pl.pallas_call(
        functools.partial(project_body, tokens),
        out_shape=jax.ShapeDtypeStruct((LINE * tokens, width), F32),
        cost_estimate=pl.CostEstimate(
            flops=2 * LINE * tokens * width * half,
            bytes_accessed=2 * half * (LINE * tokens + width),
            transcendentals=0,
        ),
        compiler_params=pltpu.CompilerParams(vmem_limit_bytes=24 * 1024 * 1024),
        name="project_readout",
    )(*readouts, *adapters)


def pick_body(tokens, chunks, place_ref, own_ref, other_ref, *refs):
    info_refs, (picked_ref, hot_ref, gain_ref) = refs[:LINE], refs[LINE:]
    every = own_ref.shape[1]
    part = LINE * LINE
    rank = every // part
    rows, width = part * ROWS, ROWS * rank
    lanes = own_lanes(rows, rank)
    shape = (rows, every)
    line = iota(shape, 0) // ROWS
    back = iota(shape, 1) // rank
    row_y, row_x = line // LINE, line % LINE
    col_y = (place_ref[2] + LINE - back // LINE) % LINE
    col_x = (place_ref[3] + LINE - back % LINE) % LINE
    own_expert = (row_y == col_y) & (row_x == col_x)
    fold = ones_where(iota((every, width), 0) % rank == iota((every, width), 1) % rank)
    expert = (iota((part, tokens), 0) * LINE + place_ref[1]).astype(F32)
    for step, info_ref in enumerate(info_refs):
        ids_t = info_ref[:, :tokens].astype(F32)
        gains_t = info_ref[:, tokens : 2 * tokens].astype(F32)
        slots = slot_of_token(ids_t, expert)
        gains = dot(spread(part), matched(ids_t, gains_t, expert).astype(BF16))
        span = slice(step * tokens, (step + 1) * tokens)
        projection = (own_ref[span, :] + other_ref[span, :]).astype(BF16)
        for c in range(chunks):
            hot = one_hot_slots(slots, c * ROWS)
            at = step * chunks + c
            hot_ref[at * rows : (at + 1) * rows, :] = hot.astype(BF16)
            gain_ref[at * rows : (at + 1) * rows, :] = (hot * gains).astype(BF16)
            picked = jnp.where(own_expert, dot(hot.astype(BF16), projection), 0.0).astype(BF16)
            placed = jnp.where(lanes, dot(picked, fold), 0.0).astype(BF16)
            picked_ref[at * part : (at + 1) * part, :] = dot(gathered(part), placed)


def pick(place, own, other, infos, tokens, chunks):
    part = LINE * LINE
    width = ROWS * (own.shape[1] // part)
    count = LINE * chunks * part
    outs = [
        jax.ShapeDtypeStruct((count, width), F32),
        jax.ShapeDtypeStruct((count * ROWS, tokens), BF16),
        jax.ShapeDtypeStruct((count * ROWS, tokens), BF16),
    ]
    info = pl.BlockSpec((ROWS, 3 * tokens), lambda n, c: (tokens // ROWS, 0))
    return pl.pallas_call(
        functools.partial(pick_body, tokens, chunks),
        grid_spec=pltpu.PrefetchScalarGridSpec(
            num_scalar_prefetch=1,
            grid=(1,),
            in_specs=[full(own.shape), full(other.shape)] + [info] * LINE,
            out_specs=[full(x.shape) for x in outs],
        ),
        out_shape=outs,
        compiler_params=pltpu.CompilerParams(vmem_limit_bytes=24 * 1024 * 1024),
        name="pick_projections",
    )(place, own, other, *infos)


def rate_body(chunks, own_ref, other_ref, picked_ref, gain_ref, log_ref, latent_ref):
    part, _, width = own_ref.shape
    rank = width // ROWS
    pieces = []
    for step in range(LINE):
        for c in range(chunks):
            row = step * LINE + c
            pieces.append(own_ref[:, row, :].astype(F32) + other_ref[:, row, :].astype(F32))
    latent = jnp.concatenate(pieces, axis=0).astype(BF16)
    latent_ref[...] = latent
    same = ones_where(iota((width, width), 0) // rank == iota((width, width), 1) // rank, F32)
    score = dot(latent.astype(F32) * picked_ref[...], same, precision=lax.Precision.HIGHEST)
    rows = part * ROWS
    lanes = own_lanes(rows, rank) & (iota((rows, width), 1) % rank == 0)
    tokens = gain_ref.shape[1]
    log_ref[...] = jnp.zeros(log_ref.shape, F32)
    for step in range(LINE):
        total = jnp.zeros((1, tokens), F32)
        for c in range(chunks):
            at = step * chunks + c
            wide = dot(spread(part), score[at * part : (at + 1) * part].astype(BF16))
            column = jnp.sum(jnp.where(lanes, wide, 0.0), axis=1, keepdims=True)
            gain = gain_ref[at * rows : (at + 1) * rows, :].astype(F32)
            total = total + jnp.sum(gain * column, axis=0, keepdims=True)
        log_ref[step : step + 1, :] = total


def rate(own, other, picked, gains, chunks):
    return pl.pallas_call(
        functools.partial(rate_body, chunks),
        out_shape=[
            jax.ShapeDtypeStruct((ROWS, gains.shape[1]), F32),
            jax.ShapeDtypeStruct(picked.shape, BF16),
        ],
        compiler_params=pltpu.CompilerParams(vmem_limit_bytes=24 * 1024 * 1024),
        name="rate_tokens",
    )(own, other, picked, gains)


def weigh_body(chunks, tokens, *refs):
    log_refs, readout_refs = refs[:LINE], refs[LINE : 2 * LINE]
    latent_ref, picked_ref, hot_ref, gain_ref, out_ref, pack_ref = refs[2 * LINE :]
    part, rank, _ = pack_ref.shape
    half = readout_refs[0].shape[1]
    width = latent_ref.shape[1]
    rows = part * ROWS
    every = part * rank
    lanes = own_lanes(rows, rank)
    spread_rows = spread(part)
    tile = ones_where(iota((width, every), 0) % rank == iota((width, every), 1) % rank)
    own_expert = iota((rows, every), 0) // ROWS == iota((rows, every), 1) // rank
    lifts = []
    pack_ref[:, :, half:] = jnp.zeros((part, rank, width), BF16)
    for step in range(LINE):
        total = log_refs[0][step : step + 1, :]
        for back in range(1, LINE):
            at = (step - back) % LINE
            total = total + log_refs[back][at : at + 1, :]
        if step == 0:
            out_ref[...] = total
        mask = readout_refs[step][tokens : tokens + 1, 2 * tokens : 3 * tokens].astype(F32)
        coefficient = 2.0 * mask / (1.0 + jnp.exp(-total))
        lift = jnp.zeros((every, tokens), F32)
        for c in range(chunks):
            at = step * chunks + c
            span = slice(at * rows, (at + 1) * rows)
            weight = (gain_ref[span, :].astype(F32) * coefficient).astype(BF16).astype(F32)
            column = jnp.sum(weight, axis=1, keepdims=True)
            placed = jnp.where(lanes, column, 0.0).astype(BF16)
            weight = dot(gathered(part), placed)
            few = slice(at * part, (at + 1) * part)
            pack_ref[:, step * LINE + c, half:] = (weight * picked_ref[few, :]).astype(BF16)
            scaled = (weight * latent_ref[few, :].astype(F32)).astype(BF16)
            scaled = jnp.where(lanes, dot(spread_rows, scaled), 0.0).astype(BF16)
            scaled = jnp.where(own_expert, dot(scaled, tile), 0.0).astype(BF16)
            lift = lift + dot(scaled, hot_ref[span, :], ((0,), (0,)))
        lifts.append(lift.astype(BF16))
    lift = jnp.concatenate(lifts, axis=1)
    block = 512
    for n in range(half // block):
        span = slice(n * block, (n + 1) * block)
        rows_in = jnp.concatenate([ref[:tokens, span] for ref in readout_refs], axis=0)
        pack_ref[:, :, span] = dot(lift, rows_in).astype(BF16).reshape(part, rank, block)


def weigh(logs, readouts, latents, picked, hots, gains, rank, tokens, chunks):
    part = LINE * LINE
    half = readouts[0].shape[1]
    return pl.pallas_call(
        functools.partial(weigh_body, chunks, tokens),
        out_shape=[
            jax.ShapeDtypeStruct((1, tokens), F32),
            jax.ShapeDtypeStruct((part, rank, half + latents.shape[1]), BF16),
        ],
        compiler_params=pltpu.CompilerParams(vmem_limit_bytes=32 * 1024 * 1024),
        name="weigh_tokens",
    )(*logs, *readouts, latents, picked, hots, gains)


def gradients_body(groups, chunks, place_ref, packed_ref, *refs):
    hid_refs, (grad_a_ref, grad_b_ref) = refs[:-2], refs[-2:]
    rank, half = grad_b_ref.shape
    part = packed_ref.shape[0]
    block = 256
    for n in range(half // block):
        span = slice(n * block, (n + 1) * block)
        grad_b_ref[:, span] = jnp.sum(packed_ref[:, :, span].astype(F32), axis=0)
    result = jnp.zeros(grad_a_ref.shape, F32)
    at = 0
    for hid_ref in hid_refs:
        rows = hid_ref.shape[0]
        count = rows // groups
        stacks = []
        for c in range(count // ROWS):
            stack = [packed_ref[:, step * LINE + at + c, half:] for step in range(LINE)]
            stacks.append(jnp.concatenate(stack, axis=0))
        at += count // ROWS
        shape = (rows, LINE * part)
        group, col = iota(shape, 0) // count, iota(shape, 1)
        block_of = (place_ref[1] + LINE - col // part) % LINE
        pick = ones_where(group == (col % part) * LINE + block_of)
        back = dot(pick, jnp.concatenate(stacks, axis=1))
        back = jnp.where(own_lanes(rows, rank, count), back, 0.0).astype(BF16)
        total = dot(back, hid_ref[...], ((0,), (0,)))
        for s in range(count):
            result = result + total[s * rank : (s + 1) * rank]
    grad_a_ref[...] = result


def gradients(place, packed, hidden, groups, chunks):
    rank = packed.shape[1]
    half = packed.shape[2] - ROWS * rank
    hidden_units = hidden[0].shape[1]
    args = (packed, *hidden)
    outs = [
        jax.ShapeDtypeStruct((rank, hidden_units), F32),
        jax.ShapeDtypeStruct((rank, half), F32),
    ]
    return pl.pallas_call(
        functools.partial(gradients_body, groups, chunks),
        grid_spec=pltpu.PrefetchScalarGridSpec(
            num_scalar_prefetch=1,
            grid=(1,),
            in_specs=[full(x.shape) for x in args],
            out_specs=[full(x.shape) for x in outs],
        ),
        out_shape=outs,
        compiler_params=pltpu.CompilerParams(vmem_limit_bytes=32 * 1024 * 1024),
        name="adapter_gradients",
    )(place, *args)


def swap(payload):
    return lax.ppermute(payload, "narrow", [(0, 1), (1, 0)])


def moved(payload, groups, stride, step):
    if step == 0:
        return payload
    moves = []
    for i in range(groups):
        at = i // stride % LINE
        moves.append((i, i + ((at + step) % LINE - at) * stride))
    return lax.ppermute(payload, "wide", moves)


def exchange(payload, among=None):
    return lax.all_to_all(
        payload, "wide", split_axis=0, concat_axis=0, tiled=True, axis_index_groups=among
    )


def on_device(
    hidden_in,
    readout,
    route_ids,
    route_weights,
    forget_mask,
    gate_proj,
    up_proj,
    adapter_a,
    adapter_b,
):
    groups = lax.axis_size("wide")
    pairs = lax.axis_size("narrow")
    tokens, picks = route_ids.shape
    features = hidden_in.shape[1]
    half = features // pairs
    rank = adapter_a.shape[1]
    chunks = sum(PARTS) // ROWS
    side = lax.axis_index("narrow")
    wide = lax.axis_index("wide")
    place = [side, wide % LINE, wide // LINE**2, wide // LINE % LINE]
    place = jnp.stack(place).astype(jnp.int32)
    planes = [list(range(z, groups, LINE)) for z in range(LINE)]

    ids_t, gains_t = route_ids.T, route_weights.T
    own_b = lax.dynamic_slice_in_dim(adapter_b[0], side * half, half, 1)
    mask = jnp.broadcast_to(forget_mask.astype(BF16), (ROWS, tokens))
    info = jnp.concatenate([ids_t.astype(BF16), gains_t, mask], axis=1)
    info = jnp.pad(info, ((0, 0), (0, half - 3 * tokens)))
    own_readout = lax.dynamic_slice_in_dim(readout, side * half, half, 1)
    own_readout = jnp.concatenate([own_readout, info], axis=0)

    sent = dispatch(place, ids_t, hidden_in, groups)
    x = exchange(sent[0].reshape(groups, PARTS[0], half)).reshape(groups * PARTS[0], half)
    y = exchange(sent[1].reshape(groups, PARTS[1], half)).reshape(groups * PARTS[1], half)
    acts, sums = experts_forward(
        place, x, swap(x), gate_proj, up_proj, adapter_a, [], groups, False
    )
    adapters = [moved(own_b, groups, LINE, step) for step in range(LINE)]
    acts, adapters = lax.optimization_barrier((acts, adapters))
    adapters = jnp.concatenate(adapters, axis=0)
    y, acts, adapters, own_readout = lax.optimization_barrier((y, acts, adapters, own_readout))
    adapters = [moved(adapters, groups, LINE**2, step) for step in range(LINE)]
    readouts = [moved(own_readout, groups, 1, step) for step in range(LINE)]
    last_acts, latents = experts_forward(
        place, y, swap(y), gate_proj, up_proj, adapter_a, [sums], groups, True
    )
    last_acts, adapters, readouts = lax.optimization_barrier((last_acts, adapters, readouts))
    hidden = [acts, last_acts]
    projections = project(readouts, adapters, tokens)
    picked, hots, gains = pick(place, projections, swap(projections), readouts, tokens, chunks)
    latents, picked = lax.optimization_barrier((exchange(latents, planes), picked))
    log_part, latents = rate(latents, swap(latents), picked, gains, chunks)
    logs = [moved(log_part, groups, 1, step) for step in range(LINE)]
    log_ratio, packed = weigh(logs, readouts, latents, picked, hots, gains, rank, tokens, chunks)
    grad_a, part_b = gradients(place, exchange(packed, planes), hidden, groups, chunks)
    other_b = swap(part_b)
    grad_b = jnp.where(
        side == 0,
        jnp.concatenate([part_b, other_b], axis=1),
        jnp.concatenate([other_b, part_b], axis=1),
    )
    return (log_ratio.reshape(tokens), grad_a[None], grad_b[None])


def solution(mesh):
    return jax.shard_map(
        on_device,
        mesh=mesh,
        in_specs=(
            P("wide", None),
            P("wide", None),
            P("wide", None),
            P("wide", None),
            P("wide"),
            P("wide", None, "narrow"),
            P("wide", None, "narrow"),
            P("wide", None, "narrow"),
            P("wide", None, None),
        ),
        out_specs=(P("wide"), P("wide", None, "narrow"), P("wide", None, None)),
        check_vma=False,
    )
```

time: 232 us -> 212 us (0.914)
  blocking collectives: 125 us -> 83.8 us
  waiting for transfers between devices: 13.4 us -> 28.4 us
  local copies, waits for them, and re-layouts: 6.64 us -> 10.4 us
    all_to_all x2, blocking collectives: 125 us -> 83.8 us  [exchange(): lax.all_to_all(payload, 'wide', split_axis=0, concat_axis=0, tiled=True,...]
    ppermute x12, waiting for transfers between devices: 10.9 us -> 21.6 us  [moved(): return lax.ppermute(payload, 'wide', moves)]
    unnamed x32 -> x42, local copies, waits for them, and re-layouts: 5.8 us -> 10.3 us
    all_to_all x2, waiting for transfers between devices: 0.55 us -> 4.94 us  [exchange(): lax.all_to_all(payload, 'wide', split_axis=0, concat_axis=0, tiled=True,...]
    ppermute x4 -> x5, starting transfers between devices: 8.11 us -> 10.8 us  [swap(): return lax.ppermute(payload, 'narrow', [(0, 1), (1, 0)])]
    pallas_call x6 -> x7, Pallas kernels: 46.8 us -> 47 us  [the longest x2 32.1 us: experts_forward(): pl.pallas_call(functools.partial(experts_body, groups, count, steps, last...]
  transfers between devices with their start and end apart: 18 -> 19, of which waited for: 8 -> 8; matrix products, arithmetic and copies ran while one was open for 0% -> 0% of each run, Pallas kernels for 16% -> 18%
where the time goes in v3:
time: 212 us; the launch traced here: 211 us
  blocking collectives  83.8 us (40%)
  Pallas kernels  51.6 us (24%)
  starting transfers between devices  35.4 us (17%)
  waiting for transfers between devices  28.4 us (13%)
  local copies, waits for them, and re-layouts  10.4 us (5%)
    all_to_all x2, blocking collectives, exchange(): lax.all_to_all(payload, 'wide', split_axis=0, concat_axis=0, tiled=True,...  83.8 us
    pallas_call x2, Pallas kernels, experts_forward(): pl.pallas_call(functools.partial(experts_body, groups, count, steps, last...  32.1 us
    ppermute x12, waiting for transfers between devices, moved(): return lax.ppermute(payload, 'wide', moves)  21.6 us
    ppermute x12, starting transfers between devices, moved(): return lax.ppermute(payload, 'wide', moves)  14.4 us
    ppermute x5, starting transfers between devices, swap(): return lax.ppermute(payload, 'narrow', [(0, 1), (1, 0)])  10.8 us
    unnamed x42, local copies, waits for them, and re-layouts  10.3 us
    all_to_all x2, starting transfers between devices, exchange(): lax.all_to_all(payload, 'wide', split_axis=0, concat_axis=0, tiled=True,...  10.1 us
    all_to_all x2, waiting for transfers between devices, exchange(): lax.all_to_all(payload, 'wide', split_axis=0, concat_axis=0, tiled=True,...  4.94 us
  transfers between devices with their start and end apart: 19, of which 8 were waited for; matrix products, arithmetic and copies ran while one was open for 0% of the time, Pallas kernels for 18%

profile of v3, /device:TPU:1, one launch (start us, length us, event | category | flops | bytes accessed | tf_op | source)
XLA Modules:
  0.0 211.4 jit_solution(6037526332539722677)
XLA Ops:
  0.8 0.8 copy-done.15
  1.5 1.2 copy-done.17
  2.7 4.6 %dispatch_rows.1 = (bf16[1024,2048]{1,0:T(8,128)(2,1)S(1)}, bf16[512,2048]{1,0:T(8,128)(2,1)}) custom-call(s32[4]{0:T(128)S(1)} %pad_add_fusion.core_ref.place_ref, s32[8,128]{1,0:T(8,128)S(1)} %bitcast.19, bf16[128,4096]{1,0:T(8,128)(2,1)S(1)} %copy-done.17), custom_call_target="tpu_custom_call" | custom-call | flops 805306368 | bytes 6291456 | tf_op jit(solution)/shard_map/dispatch_rows/pallas_call | solution.py:93
  7.4 62.2 %all_to_all.20 = bf16[64,16,2048]{2,1,0:T(8,128)(2,1)} all-to-all(bf16[64,16,2048]{2,1,0:T(8,128)(2,1)S(1)} %bitcast.17), channel_id=1, replica_groups=mesh['wide'=64,'narrow'=2] {'wide'}, dimensions={0} | all-to-all | bytes 8388608 | tf_op jit(solution)/shard_map/all_to_all | solution.py:446
  69.5 2.9 %collective-permute-start = (bf16[1024,2048]{1,0:T(8,128)(2,1)}, bf16[1024,2048]{1,0:T(8,128)(2,1)}, u32[]{:S(2)}, u32[]{:S(2)}) collective-permute-start(bf16[1024,2048]{1,0:T(8,128)(2,1)} %bitcast.8.own_ref), channel_id=1, source_target_pairs={{0,1},{1,0},{2,3},{3,2},{4,5},{5,4},{6,7},{7,6},{8,9},{9,8},{10,11... | collective-permute-start | bytes 12582920 | tf_op jit(solution)/shard_map/ppermute | solution.py:432
  72.4 0.4 collective-permute-start.1
  72.8 0.6 collective-permute-start.2
  73.4 1.9 collective-permute-start.3
  75.3 6.6 %all-to-all-start = ((bf16[64,8,2048]{2,1,0:T(8,128)(2,1)}), bf16[64,8,2048]{2,1,0:T(8,128)(2,1)}, u32[]{:S(2)}, u32[]{:S(2)}) async-start(bf16[64,8,2048]{2,1,0:T(8,128)(2,1)} %bitcast.5), calls=%async_computation | async-start | bytes 4194304 | tf_op jit(solution)/shard_map/all_to_all | solution.py:446
  82.1 0.5 copy-done.13
  82.7 20.5 %experts_forward.2 = (bf16[1024,768]{1,0:T(8,128)(2,1)S(1)}, bf16[4,16,256]{2,1,0:T(8,128)(2,1)S(1)}) custom-call(s32[4]{0:T(128)S(1)} %pad_add_fusion.core_ref.place_ref, bf16[1024,2048]{1,0:T(8,128)(2,1)} %bitcast.8.own_ref, bf16[1024,2048]{1,0:T(8,128)(2,1)} %collective-permute-done.other_ref, bf16[1,4096,768]{2,1,0:T(8,128)(2,1)} %gx_ref.3, ...), custom_call_target="tpu_custom_call" | custom-call | flops 12884901888 | bytes 20971520 | tf_op jit(solution)/shard_map/experts_forward/pallas_call | solution.py:173
  103.2 1.2 copy-done.1
  104.4 0.6 copy-done.11
  105.0 4.6 %all-to-all-done = bf16[64,8,2048]{2,1,0:T(8,128)(2,1)} async-done(((bf16[64,8,2048]{2,1,0:T(8,128)(2,1)}), bf16[64,8,2048]{2,1,0:T(8,128)(2,1)}, u32[]{:S(2)}, u32[]{:S(2)}) %all-to-all-start) | async-done | bytes 2097184 | tf_op jit(solution)/shard_map/all_to_all | solution.py:446
  109.6 2.7 %collective-permute-start.4 = (bf16[512,2048]{1,0:T(8,128)(2,1)}, bf16[512,2048]{1,0:T(8,128)(2,1)S(1)}, u32[]{:S(2)}, u32[]{:S(2)}) collective-permute-start(bf16[512,2048]{1,0:T(8,128)(2,1)} %bitcast.6.own_ref), channel_id=1, source_target_pairs={{0,1},{1,0},{2,3},{3,2},{4,5},{5,4},{6,7},{7,6},{8,9},{9,8},{10,11... | collective-permute-start | bytes 6291464 | tf_op jit(solution)/shard_map/ppermute | solution.py:432
  112.3 1.6 collective-permute-start.6
  114.0 1.0 collective-permute-start.7
  115.0 0.6 collective-permute-start.8
  115.6 11.4 %collective-permute-done.5.refs_5_ = bf16[64,2048]{1,0:T(8,128)(2,1)S(1)} collective-permute-done((bf16[64,2048]{1,0:T(8,128)(2,1)S(1)}, bf16[64,2048]{1,0:T(8,128)(2,1)S(1)}, u32[]{:S(2)}, u32[]{:S(2)}) %collective-permute-start.5) | collective-permute-done | bytes 262176 | tf_op jit(solution)/shard_map/ppermute | solution.py:442
  127.1 1.5 collective-permute-start.9
  128.6 1.5 collective-permute-start.10
  130.1 0.8 copy-done.12
  130.9 0.7 copy-done.14
  131.6 11.6 %experts_forward.3 = (bf16[512,768]{1,0:T(8,128)(2,1)S(1)}, bf16[16,16,128]{2,1,0:T(8,128)(2,1)S(1)}) custom-call(s32[4]{0:T(128)S(1)} %pad_add_fusion.core_ref.place_ref, bf16[512,2048]{1,0:T(8,128)(2,1)} %bitcast.6.own_ref, bf16[512,2048]{1,0:T(8,128)(2,1)S(1)} %collective-permute-done.4.other_ref, bf16[1,4096,768]{2,1,0:T(8,128)(2,1)} %gx_ref.3, ...), custom_call_target="tpu_custom_call" | custom-call | flops 6442450944 | bytes 16777216 | tf_op jit(solution)/shard_map/experts_forward/pallas_call | solution.py:173
  143.3 8.9 %collective-permute-done.10.refs_3_.refs_7_ = bf16[136,2048]{1,0:T(8,128)(2,1)S(1)} collective-permute-done((bf16[136,2048]{1,0:T(8,128)(2,1)S(1)}, bf16[136,2048]{1,0:T(8,128)(2,1)S(1)}, u32[]{:S(2)}, u32[]{:S(2)}) %collective-permute-start.10) | collective-permute-done | bytes 557088 | tf_op jit(solution)/shard_map/ppermute | solution.py:442
  152.3 2.2 %project_readout.1.own_ref = f32[512,256]{1,0:T(8,128)} custom-call(bf16[136,2048]{1,0:T(8,128)(2,1)S(1)} %fusion.1.refs_0_.refs_4_, bf16[136,2048]{1,0:T(8,128)(2,1)S(1)} %collective-permute-done.8.refs_1_.refs_5_, bf16[136,2048]{1,0:T(8,128)(2,1)S(1)} %collective-permute-done.9.refs_2_.refs_6_, ...), custom_call_target="tpu_custom_call" | custom-call | flops 536870912 | bytes 3145728 | tf_op jit(solution)/shard_map/project_readout/pallas_call | solution.py:209
  154.5 1.6 collective-permute-start.11
  156.1 3.5 %all-to-all-start.2 = ((bf16[16,16,128]{2,1,0:T(8,128)(2,1)}), bf16[16,16,128]{2,1,0:T(8,128)(2,1)S(1)}, u32[]{:S(2)}, u32[]{:S(2)}) async-start(bf16[16,16,128]{2,1,0:T(8,128)(2,1)} %copy-done.10), calls=%async_computation.2 | async-start | bytes 131072 | tf_op jit(solution)/shard_map/all_to_all | solution.py:446
  159.6 4.9 %pick_projections.1 = (f32[192,128]{1,0:T(8,128)S(1)}, bf16[1536,128]{1,0:T(8,128)(2,1)S(1)}, bf16[1536,128]{1,0:T(8,128)(2,1)S(1)}) custom-call(s32[4]{0:T(128)S(1)} %pad_add_fusion.core_ref.place_ref, f32[512,256]{1,0:T(8,128)} %project_readout.1.own_ref, f32[512,256]{1,0:T(8,128)} %collective-permute-done.11.other_ref, ...), custom_call_target="tpu_custom_call" | custom-call | tf_op jit(solution)/shard_map/pick_projections/pallas_call | solution.py:265
  164.5 0.8 copy-done.3
  165.3 0.7 copy-done.8
  166.0 0.3 all-to-all-done.2.own_ref
  166.4 0.9 collective-permute-start.12
  167.2 0.9 collective-permute-done.12.other_ref
  168.1 1.0 copy-done.4
  169.1 0.8 rate_tokens.1
  169.9 1.5 collective-permute-start.13
  171.4 2.1 collective-permute-start.14
  173.5 1.6 collective-permute-start.15
  175.4 0.9 collective-permute-done.15.refs_3_
  176.3 1.0 copy-done.5
  177.3 1.0 copy-done.9
  178.3 4.1 %weigh_tokens.1 = (f32[1,128]{1,0:T(1,128)}, bf16[16,16,2176]{2,1,0:T(8,128)(2,1)S(1)}) custom-call(f32[8,128]{1,0:T(8,128)S(1)} %get-tuple-element.64.refs_0_, f32[8,128]{1,0:T(8,128)S(1)} %collective-permute-done.13.refs_1_, f32[8,128]{1,0:T(8,128)S(1)} %collective-permute-done.14.refs_2_, f32[8,128]{1,0:T(8,128)S(1)} %collective-permute-done.15.refs_3_, ...), custom_call_target="tpu_custom_call" | custom-call | tf_op jit(solution)/shard_map/weigh_tokens/pallas_call | solution.py:367
  182.4 21.6 %all_to_all.21.packed_ref = bf16[16,16,2176]{2,1,0:T(8,128)(2,1)S(1)} all-to-all(bf16[16,16,2176]{2,1,0:T(8,128)(2,1)S(1)} %get-tuple-element.68), channel_id=1, replica_groups={{0,8,16,24,32,40,48,56,64,72,80,88,96,104,112,120},{2,10,18,26,34,42,50..., dimensions={0} | all-to-all | bytes 2228224 | tf_op jit(solution)/shard_map/all_to_all | solution.py:446
  204.0 2.8 %adapter_gradients.1 = (f32[16,768]{1,0:T(8,128)}, f32[16,2048]{1,0:T(8,128)S(1)}) custom-call(s32[4]{0:T(128)S(1)} %pad_add_fusion.core_ref.place_ref, bf16[16,16,2176]{2,1,0:T(8,128)(2,1)S(1)} %all_to_all.21.packed_ref, bf16[1024,768]{1,0:T(8,128)(2,1)S(1)} %copy-done.2, bf16[512,768]{1,0:T(8,128)(2,1)S(1)} %copy-done.7), custom_call_target="tpu_custom_call" | custom-call | tf_op jit(solution)/shard_map/adapter_gradients/pallas_call | solution.py:417
  206.8 2.9 %collective-permute-start.16 = (f32[16,2048]{1,0:T(8,128)S(1)}, f32[16,2048]{1,0:T(8,128)S(1)}, u32[]{:S(2)}, u32[]{:S(2)}) collective-permute-start(f32[16,2048]{1,0:T(8,128)S(1)} %get-tuple-element.72), channel_id=1, source_target_pairs={{0,1},{1,0},{2,3},{3,2},{4,5},{5,4},{6,7},{7,6},{8,9},{9,8},{10,11... | collective-permute-start | bytes 393224 | tf_op jit(solution)/shard_map/ppermute | solution.py:432
  209.7 1.0 collective-permute-done.16
  210.6 0.7 maximum_select_fusion
  (52 shorter events, 0.6 us)
Async XLA Ops:
  0.6 81.4 %copy-start = (bf16[128,4096]{1,0:T(8,128)(2,1)S(1)}, bf16[128,4096]{1,0:T(8,128)(2,1)}, u32[]{:S(2)}) copy-start(bf16[128,4096]{1,0:T(8,128)(2,1)} %param.10) | copy-start | bytes 3145732
  0.8 0.8 copy-start.15
  1.5 1.2 copy-start.17
  7.4 65.0 %copy-start.18 = (bf16[1,16,4096]{2,1,0:T(8,128)(2,1)S(1)}, bf16[1,16,4096]{2,1,0:T(8,128)(2,1)}, u32[]{:S(2)}) copy-start(bf16[1,16,4096]{2,1,0:T(8,128)(2,1)} %param.17) | copy-start | bytes 393220
  69.5 12.6 %collective-permute-start = (bf16[1024,2048]{1,0:T(8,128)(2,1)}, bf16[1024,2048]{1,0:T(8,128)(2,1)}, u32[]{:S(2)}, u32[]{:S(2)}) collective-permute-start(bf16[1024,2048]{1,0:T(8,128)(2,1)} %bitcast.8.own_ref), channel_id=1, source_target_pairs={{0,1},{1,0},{2,3},{3,2},{4,5},{5,4},{6,7},{7,6},{8,9},{9,8},{10,11... | collective-permute-start | bytes 12582920 | tf_op jit(solution)/shard_map/ppermute | solution.py:432
  72.4 32.6 %collective-permute-start.1 = (bf16[16,2048]{1,0:T(8,128)(2,1)S(1)}, bf16[16,2048]{1,0:T(8,128)(2,1)S(1)}, u32[]{:S(2)}, u32[]{:S(2)}) collective-permute-start(bf16[16,2048]{1,0:T(8,128)(2,1)S(1)} %dynamic-slice_bitcast_fusion), channel_id=1, source_target_pairs={{0,8},{2,10},{4,12},{6,14},{8,16},{10,18},{12,20},{14,22},{16,24},... | collective-permute-start | bytes 196616 | tf_op jit(solution)/shard_map/ppermute | solution.py:442
  72.8 32.2 %collective-permute-start.2 = (bf16[16,2048]{1,0:T(8,128)(2,1)S(1)}, bf16[16,2048]{1,0:T(8,128)(2,1)S(1)}, u32[]{:S(2)}, u32[]{:S(2)}) collective-permute-start(bf16[16,2048]{1,0:T(8,128)(2,1)S(1)} %dynamic-slice_bitcast_fusion), channel_id=1, source_target_pairs={{0,16},{2,18},{4,20},{6,22},{8,24},{10,26},{12,28},{14,30},{16,0},... | collective-permute-start | bytes 196616 | tf_op jit(solution)/shard_map/ppermute | solution.py:442
  73.4 31.6 %collective-permute-start.3 = (bf16[16,2048]{1,0:T(8,128)(2,1)S(1)}, bf16[16,2048]{1,0:T(8,128)(2,1)S(1)}, u32[]{:S(2)}, u32[]{:S(2)}) collective-permute-start(bf16[16,2048]{1,0:T(8,128)(2,1)S(1)} %dynamic-slice_bitcast_fusion), channel_id=1, source_target_pairs={{0,24},{2,26},{4,28},{6,30},{8,0},{10,2},{12,4},{14,6},{16,8},{18,... | collective-permute-start | bytes 196616 | tf_op jit(solution)/shard_map/ppermute | solution.py:442
  75.3 6.6 %copy-start.20 = (s32[128]{0:T(128)S(1)}, s32[128]{0:T(128)}, u32[]{:S(2)}) copy-start(s32[128]{0:T(128)} %param.13) | copy-start | bytes 1540
  75.3 6.7 %copy-start.16 = (s32[128,8]{0,1:T(8,128)S(1)}, s32[128,8]{0,1:T(8,128)}, u32[]{:S(2)}) copy-start(s32[128,8]{0,1:T(8,128)} %param.11) | copy-start | bytes 12292
  75.3 6.7 %copy-start.19 = (bf16[128,8]{0,1:T(8,128)(2,1)S(1)}, bf16[128,8]{0,1:T(8,128)(2,1)}, u32[]{:S(2)}) copy-start(bf16[128,8]{0,1:T(8,128)(2,1)} %param.12) | copy-start | bytes 6148
  75.3 34.4 %all-to-all-start = ((bf16[64,8,2048]{2,1,0:T(8,128)(2,1)}), bf16[64,8,2048]{2,1,0:T(8,128)(2,1)}, u32[]{:S(2)}, u32[]{:S(2)}) async-start(bf16[64,8,2048]{2,1,0:T(8,128)(2,1)} %bitcast.5), calls=%async_computation | async-start | bytes 4194304 | tf_op jit(solution)/shard_map/all_to_all | solution.py:446
  81.9 0.7 copy-start.13
  103.2 1.2 copy-start.1
  104.4 0.6 copy-start.11
  109.6 19.0 %collective-permute-start.4 = (bf16[512,2048]{1,0:T(8,128)(2,1)}, bf16[512,2048]{1,0:T(8,128)(2,1)S(1)}, u32[]{:S(2)}, u32[]{:S(2)}) collective-permute-start(bf16[512,2048]{1,0:T(8,128)(2,1)} %bitcast.6.own_ref), channel_id=1, source_target_pairs={{0,1},{1,0},{2,3},{3,2},{4,5},{5,4},{6,7},{7,6},{8,9},{9,8},{10,11... | collective-permute-start | bytes 6291464 | tf_op jit(solution)/shard_map/ppermute | solution.py:432
  112.3 14.8 %collective-permute-start.5 = (bf16[64,2048]{1,0:T(8,128)(2,1)S(1)}, bf16[64,2048]{1,0:T(8,128)(2,1)S(1)}, u32[]{:S(2)}, u32[]{:S(2)}) collective-permute-start(bf16[64,2048]{1,0:T(8,128)(2,1)S(1)} %pad_maximum_fusion.refs_4_), channel_id=1, source_target_pairs={{0,32},{2,34},{4,36},{6,38},{8,40},{10,42},{12,44},{14,46},{16,48}... | collective-permute-start | bytes 786440 | tf_op jit(solution)/shard_map/ppermute | solution.py:442
  112.3 31.0 %collective-permute-start.6 = (bf16[64,2048]{1,0:T(8,128)(2,1)S(1)}, bf16[64,2048]{1,0:T(8,128)(2,1)S(1)}, u32[]{:S(2)}, u32[]{:S(2)}) collective-permute-start(bf16[64,2048]{1,0:T(8,128)(2,1)S(1)} %pad_maximum_fusion.refs_4_), channel_id=1, source_target_pairs={{0,64},{2,66},{4,68},{6,70},{8,72},{10,74},{12,76},{14,78},{16,80}... | collective-permute-start | bytes 786440 | tf_op jit(solution)/shard_map/ppermute | solution.py:442
  114.0 29.3 %collective-permute-start.7 = (bf16[64,2048]{1,0:T(8,128)(2,1)S(1)}, bf16[64,2048]{1,0:T(8,128)(2,1)S(1)}, u32[]{:S(2)}, u32[]{:S(2)}) collective-permute-start(bf16[64,2048]{1,0:T(8,128)(2,1)S(1)} %pad_maximum_fusion.refs_4_), channel_id=1, source_target_pairs={{0,96},{2,98},{4,100},{6,102},{8,104},{10,106},{12,108},{14,110},{... | collective-permute-start | bytes 786440 | tf_op jit(solution)/shard_map/ppermute | solution.py:442
  115.0 28.3 %collective-permute-start.8 = (bf16[136,2048]{1,0:T(8,128)(2,1)S(1)}, bf16[136,2048]{1,0:T(8,128)(2,1)S(1)}, u32[]{:S(2)}, u32[]{:S(2)}) collective-permute-start(bf16[136,2048]{1,0:T(8,128)(2,1)S(1)} %fusion.1.refs_0_.refs_4_), channel_id=1, source_target_pairs={{0,2},{2,4},{4,6},{6,0},{8,10},{10,12},{12,14},{14,8},{16,18},{18,... | collective-permute-start | bytes 1671176 | tf_op jit(solution)/shard_map/ppermute | solution.py:442
  127.1 16.2 %collective-permute-start.9 = (bf16[136,2048]{1,0:T(8,128)(2,1)S(1)}, bf16[136,2048]{1,0:T(8,128)(2,1)S(1)}, u32[]{:S(2)}, u32[]{:S(2)}) collective-permute-start(bf16[136,2048]{1,0:T(8,128)(2,1)S(1)} %fusion.1.refs_0_.refs_4_), channel_id=1, source_target_pairs={{0,4},{2,6},{4,0},{6,2},{8,12},{10,14},{12,8},{14,10},{16,20},{18,... | collective-permute-start | bytes 1671176 | tf_op jit(solution)/shard_map/ppermute | solution.py:442
  128.6 23.7 %collective-permute-start.10 = (bf16[136,2048]{1,0:T(8,128)(2,1)S(1)}, bf16[136,2048]{1,0:T(8,128)(2,1)S(1)}, u32[]{:S(2)}, u32[]{:S(2)}) collective-permute-start(bf16[136,2048]{1,0:T(8,128)(2,1)S(1)} %fusion.1.refs_0_.refs_4_), channel_id=1, source_target_pairs={{0,6},{2,0},{4,2},{6,4},{8,14},{10,8},{12,10},{14,12},{16,22},{18,... | collective-permute-start | bytes 1671176 | tf_op jit(solution)/shard_map/ppermute | solution.py:442
  130.1 0.8 copy-start.12
  130.9 0.7 copy-start.14
  143.3 11.3 %copy-start.6 = (bf16[512,768]{1,0:T(8,128)(2,1)}, bf16[512,768]{1,0:T(8,128)(2,1)S(1)}, u32[]{:S(2)}) copy-start(bf16[512,768]{1,0:T(8,128)(2,1)S(1)} %get-tuple-element.70.refs_1_) | copy-start | bytes 2359300
  143.3 12.8 %copy-start.10 = (bf16[16,16,128]{2,1,0:T(8,128)(2,1)}, bf16[16,16,128]{2,1,0:T(8,128)(2,1)S(1)}, u32[]{:S(2)}) copy-start(bf16[16,16,128]{2,1,0:T(8,128)(2,1)S(1)} %get-tuple-element.48) | copy-start | bytes 196612
  154.5 5.1 %collective-permute-start.11 = (f32[512,256]{1,0:T(8,128)}, f32[512,256]{1,0:T(8,128)}, u32[]{:S(2)}, u32[]{:S(2)}) collective-permute-start(f32[512,256]{1,0:T(8,128)} %project_readout.1.own_ref), channel_id=1, source_target_pairs={{0,1},{1,0},{2,3},{3,2},{4,5},{5,4},{6,7},{7,6},{8,9},{9,8},{10,11... | collective-permute-start | bytes 1572872 | tf_op jit(solution)/shard_map/ppermute | solution.py:432
  156.1 10.3 %all-to-all-start.2 = ((bf16[16,16,128]{2,1,0:T(8,128)(2,1)}), bf16[16,16,128]{2,1,0:T(8,128)(2,1)S(1)}, u32[]{:S(2)}, u32[]{:S(2)}) async-start(bf16[16,16,128]{2,1,0:T(8,128)(2,1)} %copy-done.10), calls=%async_computation.2 | async-start | bytes 131072 | tf_op jit(solution)/shard_map/all_to_all | solution.py:446
  164.5 0.8 copy-start.3
  165.3 0.7 copy-start.8
  166.4 1.8 collective-permute-start.12
  168.1 1.0 copy-start.4
  169.9 5.2 %collective-permute-start.13 = (f32[8,128]{1,0:T(8,128)S(1)}, f32[8,128]{1,0:T(8,128)S(1)}, u32[]{:S(2)}, u32[]{:S(2)}) collective-permute-start(f32[8,128]{1,0:T(8,128)S(1)} %get-tuple-element.64.refs_0_), channel_id=1, source_target_pairs={{0,2},{2,4},{4,6},{6,0},{8,10},{10,12},{12,14},{14,8},{16,18},{18,... | collective-permute-start | bytes 12296 | tf_op jit(solution)/shard_map/ppermute | solution.py:442
  171.4 4.0 %collective-permute-start.14 = (f32[8,128]{1,0:T(8,128)S(1)}, f32[8,128]{1,0:T(8,128)S(1)}, u32[]{:S(2)}, u32[]{:S(2)}) collective-permute-start(f32[8,128]{1,0:T(8,128)S(1)} %get-tuple-element.64.refs_0_), channel_id=1, source_target_pairs={{0,4},{2,6},{4,0},{6,2},{8,12},{10,14},{12,8},{14,10},{16,20},{18,... | collective-permute-start | bytes 12296 | tf_op jit(solution)/shard_map/ppermute | solution.py:442
  173.5 2.8 %collective-permute-start.15 = (f32[8,128]{1,0:T(8,128)S(1)}, f32[8,128]{1,0:T(8,128)S(1)}, u32[]{:S(2)}, u32[]{:S(2)}) collective-permute-start(f32[8,128]{1,0:T(8,128)S(1)} %get-tuple-element.64.refs_0_), channel_id=1, source_target_pairs={{0,6},{2,0},{4,2},{6,4},{8,14},{10,8},{12,10},{14,12},{16,22},{18,... | collective-permute-start | bytes 12296 | tf_op jit(solution)/shard_map/ppermute | solution.py:442
  176.3 1.0 copy-start.5
  177.3 1.0 copy-start.9
  178.3 25.7 %copy-start.2 = (bf16[1024,768]{1,0:T(8,128)(2,1)S(1)}, bf16[1024,768]{1,0:T(8,128)(2,1)}, u32[]{:S(2)}) copy-start(bf16[1024,768]{1,0:T(8,128)(2,1)} %copy-done.1) | copy-start | bytes 4718596
  178.3 25.7 %copy-start.7 = (bf16[512,768]{1,0:T(8,128)(2,1)S(1)}, bf16[512,768]{1,0:T(8,128)(2,1)}, u32[]{:S(2)}) copy-start(bf16[512,768]{1,0:T(8,128)(2,1)} %copy-done.6) | copy-start | bytes 2359300
  206.8 3.9 %collective-permute-start.16 = (f32[16,2048]{1,0:T(8,128)S(1)}, f32[16,2048]{1,0:T(8,128)S(1)}, u32[]{:S(2)}, u32[]{:S(2)}) collective-permute-start(f32[16,2048]{1,0:T(8,128)S(1)} %get-tuple-element.72), channel_id=1, source_target_pairs={{0,1},{1,0},{2,3},{3,2},{4,5},{5,4},{6,7},{7,6},{8,9},{9,8},{10,11... | collective-permute-start | bytes 393224 | tf_op jit(solution)/shard_map/ppermute | solution.py:432

commit v4 on v3

--- a/solution.py
+++ b/solution.py
@@ -108,7 +108,7 @@
             bytes_accessed=2 * sum(sizes) * half,
             transcendentals=0,
         ),
-        compiler_params=pltpu.CompilerParams(vmem_limit_bytes=24 * 1024 * 1024),
+        compiler_params=pltpu.CompilerParams(vmem_limit_bytes=20 * 1024 * 1024),
         name="dispatch_rows",
     )(core, ids_t, rows)
 
@@ -214,13 +214,13 @@
             bytes_accessed=2 * half * (LINE * tokens + width),
             transcendentals=0,
         ),
-        compiler_params=pltpu.CompilerParams(vmem_limit_bytes=24 * 1024 * 1024),
+        compiler_params=pltpu.CompilerParams(vmem_limit_bytes=16 * 1024 * 1024),
         name="project_readout",
     )(*readouts, *adapters)
 
 
 def pick_body(tokens, chunks, place_ref, own_ref, other_ref, *refs):
-    info_refs, (picked_ref, hot_ref, gain_ref) = refs[:LINE], refs[LINE:]
+    info_refs, (picked_ref, gain_ref) = refs[:LINE], refs[LINE:]
     every = own_ref.shape[1]
     part = LINE * LINE
     rank = every // part
@@ -245,7 +245,6 @@
         for c in range(chunks):
             hot = one_hot_slots(slots, c * ROWS)
             at = step * chunks + c
-            hot_ref[at * rows : (at + 1) * rows, :] = hot.astype(BF16)
             gain_ref[at * rows : (at + 1) * rows, :] = (hot * gains).astype(BF16)
             picked = jnp.where(own_expert, dot(hot.astype(BF16), projection), 0.0).astype(BF16)
             placed = jnp.where(lanes, dot(picked, fold), 0.0).astype(BF16)
@@ -259,7 +258,6 @@
     outs = [
         jax.ShapeDtypeStruct((count, width), F32),
         jax.ShapeDtypeStruct((count * ROWS, tokens), BF16),
-        jax.ShapeDtypeStruct((count * ROWS, tokens), BF16),
     ]
     info = pl.BlockSpec((ROWS, 3 * tokens), lambda n, c: (tokens // ROWS, 0))
     return pl.pallas_call(
@@ -271,7 +269,7 @@
             out_specs=[full(x.shape) for x in outs],
         ),
         out_shape=outs,
-        compiler_params=pltpu.CompilerParams(vmem_limit_bytes=24 * 1024 * 1024),
+        compiler_params=pltpu.CompilerParams(vmem_limit_bytes=16 * 1024 * 1024),
         name="pick_projections",
     )(place, own, other, *infos)
 
@@ -310,14 +308,14 @@
             jax.ShapeDtypeStruct((ROWS, gains.shape[1]), F32),
             jax.ShapeDtypeStruct(picked.shape, BF16),
         ],
-        compiler_params=pltpu.CompilerParams(vmem_limit_bytes=24 * 1024 * 1024),
+        compiler_params=pltpu.CompilerParams(vmem_limit_bytes=12 * 1024 * 1024),
         name="rate_tokens",
     )(own, other, picked, gains)
 
 
 def weigh_body(chunks, tokens, *refs):
     log_refs, readout_refs = refs[:LINE], refs[LINE : 2 * LINE]
-    latent_ref, picked_ref, hot_ref, gain_ref, out_ref, pack_ref = refs[2 * LINE :]
+    latent_ref, picked_ref, gain_ref, out_ref, pack_ref = refs[2 * LINE :]
     part, rank, _ = pack_ref.shape
     half = readout_refs[0].shape[1]
     width = latent_ref.shape[1]
@@ -342,7 +340,9 @@
         for c in range(chunks):
             at = step * chunks + c
             span = slice(at * rows, (at + 1) * rows)
-            weight = (gain_ref[span, :].astype(F32) * coefficient).astype(BF16).astype(F32)
+            gain = gain_ref[span, :].astype(F32)
+            hot = ones_where(gain > 0.0)
+            weight = (gain * coefficient).astype(BF16).astype(F32)
             column = jnp.sum(weight, axis=1, keepdims=True)
             placed = jnp.where(lanes, column, 0.0).astype(BF16)
             weight = dot(gathered(part), placed)
@@ -351,7 +351,7 @@
             scaled = (weight * latent_ref[few, :].astype(F32)).astype(BF16)
             scaled = jnp.where(lanes, dot(spread_rows, scaled), 0.0).astype(BF16)
             scaled = jnp.where(own_expert, dot(scaled, tile), 0.0).astype(BF16)
-            lift = lift + dot(scaled, hot_ref[span, :], ((0,), (0,)))
+            lift = lift + dot(scaled, hot, ((0,), (0,)))
         lifts.append(lift.astype(BF16))
     lift = jnp.concatenate(lifts, axis=1)
     block = 512
@@ -361,7 +361,7 @@
         pack_ref[:, :, span] = dot(lift, rows_in).astype(BF16).reshape(part, rank, block)
 
 
-def weigh(logs, readouts, latents, picked, hots, gains, rank, tokens, chunks):
+def weigh(logs, readouts, latents, picked, gains, rank, tokens, chunks):
     part = LINE * LINE
     half = readouts[0].shape[1]
     return pl.pallas_call(
@@ -370,9 +370,9 @@
             jax.ShapeDtypeStruct((1, tokens), F32),
             jax.ShapeDtypeStruct((part, rank, half + latents.shape[1]), BF16),
         ],
-        compiler_params=pltpu.CompilerParams(vmem_limit_bytes=32 * 1024 * 1024),
+        compiler_params=pltpu.CompilerParams(vmem_limit_bytes=20 * 1024 * 1024),
         name="weigh_tokens",
-    )(*logs, *readouts, latents, picked, hots, gains)
+    )(*logs, *readouts, latents, picked, gains)
 
 
 def gradients_body(groups, chunks, place_ref, packed_ref, *refs):
@@ -423,7 +423,7 @@
             out_specs=[full(x.shape) for x in outs],
         ),
         out_shape=outs,
-        compiler_params=pltpu.CompilerParams(vmem_limit_bytes=32 * 1024 * 1024),
+        compiler_params=pltpu.CompilerParams(vmem_limit_bytes=20 * 1024 * 1024),
         name="adapter_gradients",
     )(place, *args)
 
@@ -480,17 +480,17 @@
     own_readout = lax.dynamic_slice_in_dim(readout, side * half, half, 1)
     own_readout = jnp.concatenate([own_readout, info], axis=0)
 
-    sent = dispatch(place, ids_t, hidden_in, groups)
+    adapters = [moved(own_b, groups, LINE, step) for step in range(LINE)]
+    adapters = jnp.concatenate(adapters, axis=0)
+    sent = list(dispatch(place, ids_t, hidden_in, groups))
+    sent[0], adapters = lax.optimization_barrier((sent[0], adapters))
     x = exchange(sent[0].reshape(groups, PARTS[0], half)).reshape(groups * PARTS[0], half)
     y = exchange(sent[1].reshape(groups, PARTS[1], half)).reshape(groups * PARTS[1], half)
     acts, sums = experts_forward(
         place, x, swap(x), gate_proj, up_proj, adapter_a, [], groups, False
     )
-    adapters = [moved(own_b, groups, LINE, step) for step in range(LINE)]
-    acts, adapters = lax.optimization_barrier((acts, adapters))
-    adapters = jnp.concatenate(adapters, axis=0)
+    adapters = [moved(adapters, groups, LINE**2, step) for step in range(LINE)]
     y, acts, adapters, own_readout = lax.optimization_barrier((y, acts, adapters, own_readout))
-    adapters = [moved(adapters, groups, LINE**2, step) for step in range(LINE)]
     readouts = [moved(own_readout, groups, 1, step) for step in range(LINE)]
     last_acts, latents = experts_forward(
         place, y, swap(y), gate_proj, up_proj, adapter_a, [sums], groups, True
@@ -498,11 +498,11 @@
     last_acts, adapters, readouts = lax.optimization_barrier((last_acts, adapters, readouts))
     hidden = [acts, last_acts]
     projections = project(readouts, adapters, tokens)
-    picked, hots, gains = pick(place, projections, swap(projections), readouts, tokens, chunks)
+    picked, gains = pick(place, projections, swap(projections), readouts, tokens, chunks)
     latents, picked = lax.optimization_barrier((exchange(latents, planes), picked))
     log_part, latents = rate(latents, swap(latents), picked, gains, chunks)
     logs = [moved(log_part, groups, 1, step) for step in range(LINE)]
-    log_ratio, packed = weigh(logs, readouts, latents, picked, hots, gains, rank, tokens, chunks)
+    log_ratio, packed = weigh(logs, readouts, latents, picked, gains, rank, tokens, chunks)
     grad_a, part_b = gradients(place, exchange(packed, planes), hidden, groups, chunks)
     other_b = swap(part_b)
     grad_b = jnp.where(

time: 212 us -> 209 us (0.986)
  blocking collectives: 83.8 us -> 80.4 us
  waiting for transfers between devices: 28.4 us -> 25.3 us
  starting transfers between devices: 35.4 us -> 37.9 us
    all_to_all x2, waiting for transfers between devices: 4.94 us -> 0.84 us  [exchange(): lax.all_to_all(payload, 'wide', split_axis=0, concat_axis=0, tiled=True,...]
    all_to_all x2, blocking collectives: 83.8 us -> 80.4 us  [exchange(): lax.all_to_all(payload, 'wide', split_axis=0, concat_axis=0, tiled=True,...]
    unnamed x42 -> x48, local copies, waits for them, and re-layouts: 10.3 us -> 10.1 us
  transfers between devices with their start and end apart: 19 -> 19, of which waited for: 8 -> 11; matrix products, arithmetic and copies ran while one was open for 0% -> 0% of each run, Pallas kernels for 18% -> 20%
where the time goes in v4:
time: 209 us; the launch traced here: 208 us
  blocking collectives  80.4 us (38%)
  Pallas kernels  51.6 us (25%)
  starting transfers between devices  37.9 us (18%)
  waiting for transfers between devices  25.3 us (12%)
  local copies, waits for them, and re-layouts  11.1 us (5%)
    all_to_all x2, blocking collectives, exchange(): lax.all_to_all(payload, 'wide', split_axis=0, concat_axis=0, tiled=True,...  80.4 us
    pallas_call x2, Pallas kernels, experts_forward(): pl.pallas_call(functools.partial(experts_body, groups, count, steps, last...  32.1 us
    ppermute x12, waiting for transfers between devices, moved(): return lax.ppermute(payload, 'wide', moves)  22.1 us
    ppermute x12, starting transfers between devices, moved(): return lax.ppermute(payload, 'wide', moves)  16.2 us
    ppermute x5, starting transfers between devices, swap(): return lax.ppermute(payload, 'narrow', [(0, 1), (1, 0)])  11.1 us
    all_to_all x2, starting transfers between devices, exchange(): lax.all_to_all(payload, 'wide', split_axis=0, concat_axis=0, tiled=True,...  10.5 us
    unnamed x48, local copies, waits for them, and re-layouts  10.1 us
    pallas_call x1, Pallas kernels, pick(): pl.pallas_call(functools.partial(pick_body, tokens, chunks), grid_spec=pl...  4.91 us
  transfers between devices with their start and end apart: 19, of which 11 were waited for; matrix products, arithmetic and copies ran while one was open for 0% of the time, Pallas kernels for 20%

profile of v4, /device:TPU:1, one launch (start us, length us, event | category | flops | bytes accessed | tf_op | source)
XLA Modules:
  0.0 208.1 jit_solution(381911950829679425)
XLA Ops:
  0.7 0.9 dynamic-slice_bitcast_fusion
  1.6 3.3 %collective-permute-start.2 = (bf16[16,2048]{1,0:T(8,128)(2,1)S(1)}, bf16[16,2048]{1,0:T(8,128)(2,1)S(1)}, u32[]{:S(2)}, u32[]{:S(2)}) collective-permute-start(bf16[16,2048]{1,0:T(8,128)(2,1)S(1)} %dynamic-slice_bitcast_fusion), channel_id=1, source_target_pairs={{0,24},{2,26},{4,28},{6,30},{8,0},{10,2},{12,4},{14,6},{16,8},{18,... | collective-permute-start | bytes 196616 | tf_op jit(solution)/shard_map/ppermute | solution.py:442
  5.4 0.6 collective-permute-start
  6.1 0.7 copy-done.19
  6.8 1.2 copy-done.21
  8.0 4.6 %dispatch_rows.1 = (bf16[1024,2048]{1,0:T(8,128)(2,1)S(1)}, bf16[512,2048]{1,0:T(8,128)(2,1)}) custom-call(s32[4]{0:T(128)S(1)} %pad_add_fusion.core_ref.place_ref, s32[8,128]{1,0:T(8,128)S(1)} %bitcast.19, bf16[128,4096]{1,0:T(8,128)(2,1)S(1)} %copy-done.21), custom_call_target="tpu_custom_call" | custom-call | flops 805306368 | bytes 6291456 | tf_op jit(solution)/shard_map/dispatch_rows/pallas_call | solution.py:93
  12.7 59.7 %all_to_all.20 = bf16[64,16,2048]{2,1,0:T(8,128)(2,1)} all-to-all(bf16[64,16,2048]{2,1,0:T(8,128)(2,1)S(1)} %bitcast.17), channel_id=1, replica_groups=mesh['wide'=64,'narrow'=2] {'wide'}, dimensions={0} | all-to-all | bytes 8388608 | tf_op jit(solution)/shard_map/all_to_all | solution.py:446
  72.3 3.7 %collective-permute-start.3 = (bf16[1024,2048]{1,0:T(8,128)(2,1)}, bf16[1024,2048]{1,0:T(8,128)(2,1)}, u32[]{:S(2)}, u32[]{:S(2)}) collective-permute-start(bf16[1024,2048]{1,0:T(8,128)(2,1)} %bitcast.9.own_ref), channel_id=1, source_target_pairs={{0,1},{1,0},{2,3},{3,2},{4,5},{5,4},{6,7},{7,6},{8,9},{9,8},{10,11... | collective-permute-start | bytes 12582920 | tf_op jit(solution)/shard_map/ppermute | solution.py:432
  76.1 5.7 %all-to-all-start = ((bf16[64,8,2048]{2,1,0:T(8,128)(2,1)}), bf16[64,8,2048]{2,1,0:T(8,128)(2,1)}, u32[]{:S(2)}, u32[]{:S(2)}) async-start(bf16[64,8,2048]{2,1,0:T(8,128)(2,1)} %bitcast.5), calls=%async_computation | async-start | bytes 4194304 | tf_op jit(solution)/shard_map/all_to_all | solution.py:446
  82.0 1.0 collective-permute-start.4
  83.0 2.6 %collective-permute-start.5 = (bf16[64,2048]{1,0:T(8,128)(2,1)S(1)}, bf16[64,2048]{1,0:T(8,128)(2,1)S(1)}, u32[]{:S(2)}, u32[]{:S(2)}) collective-permute-start(bf16[64,2048]{1,0:T(8,128)(2,1)S(1)} %pad_maximum_fusion.refs_4_), channel_id=1, source_target_pairs={{0,64},{2,66},{4,68},{6,70},{8,72},{10,74},{12,76},{14,78},{16,80}... | collective-permute-start | bytes 786440 | tf_op jit(solution)/shard_map/ppermute | solution.py:442
  85.6 1.1 collective-permute-start.6
  86.6 20.5 %experts_forward.2 = (bf16[1024,768]{1,0:T(8,128)(2,1)S(1)}, bf16[4,16,256]{2,1,0:T(8,128)(2,1)S(1)}) custom-call(s32[4]{0:T(128)S(1)} %pad_add_fusion.core_ref.place_ref, bf16[1024,2048]{1,0:T(8,128)(2,1)} %bitcast.9.own_ref, bf16[1024,2048]{1,0:T(8,128)(2,1)} %collective-permute-done.3.other_ref, bf16[1,4096,768]{2,1,0:T(8,128)(2,1)} %gx_ref.3, ...), custom_call_target="tpu_custom_call" | custom-call | flops 12884901888 | bytes 20971520 | tf_op jit(solution)/shard_map/experts_forward/pallas_call | solution.py:173
  107.2 1.2 copy-done.1
  108.3 0.6 copy-done.15
  109.0 5.3 %collective-permute-done.4.refs_5_ = bf16[64,2048]{1,0:T(8,128)(2,1)S(1)} collective-permute-done((bf16[64,2048]{1,0:T(8,128)(2,1)S(1)}, bf16[64,2048]{1,0:T(8,128)(2,1)S(1)}, u32[]{:S(2)}, u32[]{:S(2)}) %collective-permute-start.4) | collective-permute-done | bytes 262176 | tf_op jit(solution)/shard_map/ppermute | solution.py:442
  114.3 0.7 copy-done.8
  115.0 4.1 %collective-permute-done.5.refs_6_ = bf16[64,2048]{1,0:T(8,128)(2,1)S(1)} collective-permute-done((bf16[64,2048]{1,0:T(8,128)(2,1)S(1)}, bf16[64,2048]{1,0:T(8,128)(2,1)S(1)}, u32[]{:S(2)}, u32[]{:S(2)}) %collective-permute-start.5) | collective-permute-done | bytes 262176 | tf_op jit(solution)/shard_map/ppermute | solution.py:442
  119.0 0.7 copy-done.10
  119.7 0.7 copy-done.12
  120.4 1.6 collective-permute-start.7
  122.0 2.6 %collective-permute-start.9 = (bf16[136,2048]{1,0:T(8,128)(2,1)S(1)}, bf16[136,2048]{1,0:T(8,128)(2,1)S(1)}, u32[]{:S(2)}, u32[]{:S(2)}) collective-permute-start(bf16[136,2048]{1,0:T(8,128)(2,1)S(1)} %fusion.1.refs_0_.refs_4_), channel_id=1, source_target_pairs={{0,4},{2,6},{4,0},{6,2},{8,12},{10,14},{12,8},{14,10},{16,20},{18,... | collective-permute-start | bytes 1671176 | tf_op jit(solution)/shard_map/ppermute | solution.py:442
  124.6 0.9 collective-permute-start.10
  125.5 0.5 collective-permute-done.7.other_ref
  126.0 0.8 copy-done.16
  126.8 0.7 copy-done.18
  127.5 11.6 %experts_forward.3 = (bf16[512,768]{1,0:T(8,128)(2,1)S(1)}, bf16[16,16,128]{2,1,0:T(8,128)(2,1)S(1)}) custom-call(s32[4]{0:T(128)S(1)} %pad_add_fusion.core_ref.place_ref, bf16[512,2048]{1,0:T(8,128)(2,1)} %bitcast.6.own_ref, bf16[512,2048]{1,0:T(8,128)(2,1)S(1)} %collective-permute-done.7.other_ref, bf16[1,4096,768]{2,1,0:T(8,128)(2,1)} %gx_ref.3, ...), custom_call_target="tpu_custom_call" | custom-call | flops 6442450944 | bytes 16777216 | tf_op jit(solution)/shard_map/experts_forward/pallas_call | solution.py:173
  139.2 10.2 %collective-permute-done.9.refs_2_.refs_6_ = bf16[136,2048]{1,0:T(8,128)(2,1)S(1)} collective-permute-done((bf16[136,2048]{1,0:T(8,128)(2,1)S(1)}, bf16[136,2048]{1,0:T(8,128)(2,1)S(1)}, u32[]{:S(2)}, u32[]{:S(2)}) %collective-permute-start.9) | collective-permute-done | bytes 557088 | tf_op jit(solution)/shard_map/ppermute | solution.py:442
  149.7 2.3 %project_readout.1.own_ref = f32[512,256]{1,0:T(8,128)} custom-call(bf16[136,2048]{1,0:T(8,128)(2,1)S(1)} %fusion.1.refs_0_.refs_4_, bf16[136,2048]{1,0:T(8,128)(2,1)S(1)} %collective-permute-done.8.refs_1_.refs_5_, bf16[136,2048]{1,0:T(8,128)(2,1)S(1)} %collective-permute-done.9.refs_2_.refs_6_, ...), custom_call_target="tpu_custom_call" | custom-call | flops 536870912 | bytes 3145728 | tf_op jit(solution)/shard_map/project_readout/pallas_call | solution.py:209
  152.0 1.1 collective-permute-start.11
  153.1 4.8 %all-to-all-start.2 = ((bf16[16,16,128]{2,1,0:T(8,128)(2,1)}), bf16[16,16,128]{2,1,0:T(8,128)(2,1)S(1)}, u32[]{:S(2)}, u32[]{:S(2)}) async-start(bf16[16,16,128]{2,1,0:T(8,128)(2,1)} %copy-done.14), calls=%async_computation.2 | async-start | bytes 131072 | tf_op jit(solution)/shard_map/all_to_all | solution.py:446
  158.0 4.9 %pick_projections.1 = (f32[192,128]{1,0:T(8,128)S(1)}, bf16[1536,128]{1,0:T(8,128)(2,1)S(1)}) custom-call(s32[4]{0:T(128)S(1)} %pad_add_fusion.core_ref.place_ref, f32[512,256]{1,0:T(8,128)} %project_readout.1.own_ref, f32[512,256]{1,0:T(8,128)} %collective-permute-done.11.other_ref, bf16[136,2048]{1,0:T(8,128)(2,1)S(1)} %fusion.1.refs_0_.refs_4_, ...), custom_call_target="tpu_custom_call" | custom-call | tf_op jit(solution)/shard_map/pick_projections/pallas_call | solution.py:263
  162.9 0.8 copy-done.3
  163.6 0.8 all-to-all-done.2.own_ref
  164.5 1.4 collective-permute-start.12
  165.9 0.9 collective-permute-done.12.other_ref
  166.8 1.0 copy-done.4
  167.8 0.8 rate_tokens.1
  168.7 3.3 %collective-permute-start.14 = (f32[8,128]{1,0:T(8,128)S(1)}, f32[8,128]{1,0:T(8,128)S(1)}, u32[]{:S(2)}, u32[]{:S(2)}) collective-permute-start(f32[8,128]{1,0:T(8,128)S(1)} %get-tuple-element.63.refs_0_), channel_id=1, source_target_pairs={{0,4},{2,6},{4,0},{6,2},{8,12},{10,14},{12,8},{14,10},{16,20},{18,... | collective-permute-start | bytes 12296 | tf_op jit(solution)/shard_map/ppermute | solution.py:442
  172.3 0.7 collective-permute-done.14.refs_2_
  173.0 1.4 collective-permute-done.15.refs_3_
  174.5 1.0 copy-done.5
  175.4 4.1 %weigh_tokens.1 = (f32[1,128]{1,0:T(1,128)}, bf16[16,16,2176]{2,1,0:T(8,128)(2,1)S(1)}) custom-call(f32[8,128]{1,0:T(8,128)S(1)} %get-tuple-element.63.refs_0_, f32[8,128]{1,0:T(8,128)S(1)} %collective-permute-done.13.refs_1_, f32[8,128]{1,0:T(8,128)S(1)} %collective-permute-done.14.refs_2_, f32[8,128]{1,0:T(8,128)S(1)} %collective-permute-done.15.refs_3_, ...), custom_call_target="tpu_custom_call" | custom-call | tf_op jit(solution)/shard_map/weigh_tokens/pallas_call | solution.py:367
  179.5 20.8 %all_to_all.21.packed_ref = bf16[16,16,2176]{2,1,0:T(8,128)(2,1)S(1)} all-to-all(bf16[16,16,2176]{2,1,0:T(8,128)(2,1)S(1)} %get-tuple-element.66), channel_id=1, replica_groups={{0,8,16,24,32,40,48,56,64,72,80,88,96,104,112,120},{2,10,18,26,34,42,50..., dimensions={0} | all-to-all | bytes 2228224 | tf_op jit(solution)/shard_map/all_to_all | solution.py:446
  200.3 2.8 %adapter_gradients.1 = (f32[16,768]{1,0:T(8,128)}, f32[16,2048]{1,0:T(8,128)S(1)}) custom-call(s32[4]{0:T(128)S(1)} %pad_add_fusion.core_ref.place_ref, bf16[16,16,2176]{2,1,0:T(8,128)(2,1)S(1)} %all_to_all.21.packed_ref, bf16[1024,768]{1,0:T(8,128)(2,1)S(1)} %copy-done.2, bf16[512,768]{1,0:T(8,128)(2,1)S(1)} %copy-done.7), custom_call_target="tpu_custom_call" | custom-call | tf_op jit(solution)/shard_map/adapter_gradients/pallas_call | solution.py:417
  203.1 3.3 %collective-permute-start.16 = (f32[16,2048]{1,0:T(8,128)S(1)}, f32[16,2048]{1,0:T(8,128)S(1)}, u32[]{:S(2)}, u32[]{:S(2)}) collective-permute-start(f32[16,2048]{1,0:T(8,128)S(1)} %get-tuple-element.70), channel_id=1, source_target_pairs={{0,1},{1,0},{2,3},{3,2},{4,5},{5,4},{6,7},{7,6},{8,9},{9,8},{10,11... | collective-permute-start | bytes 393224 | tf_op jit(solution)/shard_map/ppermute | solution.py:432
  206.4 1.0 collective-permute-done.16
  207.3 0.7 maximum_select_fusion
  (58 shorter events, 1.6 us)
Async XLA Ops:
  0.6 81.2 %copy-start = (bf16[128,4096]{1,0:T(8,128)(2,1)S(1)}, bf16[128,4096]{1,0:T(8,128)(2,1)}, u32[]{:S(2)}) copy-start(bf16[128,4096]{1,0:T(8,128)(2,1)} %param.10) | copy-start | bytes 3145732
  1.6 11.0 %collective-permute-start.2 = (bf16[16,2048]{1,0:T(8,128)(2,1)S(1)}, bf16[16,2048]{1,0:T(8,128)(2,1)S(1)}, u32[]{:S(2)}, u32[]{:S(2)}) collective-permute-start(bf16[16,2048]{1,0:T(8,128)(2,1)S(1)} %dynamic-slice_bitcast_fusion), channel_id=1, source_target_pairs={{0,24},{2,26},{4,28},{6,30},{8,0},{10,2},{12,4},{14,6},{16,8},{18,... | collective-permute-start | bytes 196616 | tf_op jit(solution)/shard_map/ppermute | solution.py:442
  4.9 7.7 %collective-permute-start.1 = (bf16[16,2048]{1,0:T(8,128)(2,1)S(1)}, bf16[16,2048]{1,0:T(8,128)(2,1)S(1)}, u32[]{:S(2)}, u32[]{:S(2)}) collective-permute-start(bf16[16,2048]{1,0:T(8,128)(2,1)S(1)} %dynamic-slice_bitcast_fusion), channel_id=1, source_target_pairs={{0,16},{2,18},{4,20},{6,22},{8,24},{10,26},{12,28},{14,30},{16,0},... | collective-permute-start | bytes 196616 | tf_op jit(solution)/shard_map/ppermute | solution.py:442
  5.4 7.2 %collective-permute-start = (bf16[16,2048]{1,0:T(8,128)(2,1)S(1)}, bf16[16,2048]{1,0:T(8,128)(2,1)S(1)}, u32[]{:S(2)}, u32[]{:S(2)}) collective-permute-start(bf16[16,2048]{1,0:T(8,128)(2,1)S(1)} %dynamic-slice_bitcast_fusion), channel_id=1, source_target_pairs={{0,8},{2,10},{4,12},{6,14},{8,16},{10,18},{12,20},{14,22},{16,24},... | collective-permute-start | bytes 196616 | tf_op jit(solution)/shard_map/ppermute | solution.py:442
  6.1 0.7 copy-start.19
  6.8 1.2 copy-start.21
  72.3 14.3 %collective-permute-start.3 = (bf16[1024,2048]{1,0:T(8,128)(2,1)}, bf16[1024,2048]{1,0:T(8,128)(2,1)}, u32[]{:S(2)}, u32[]{:S(2)}) collective-permute-start(bf16[1024,2048]{1,0:T(8,128)(2,1)} %bitcast.9.own_ref), channel_id=1, source_target_pairs={{0,1},{1,0},{2,3},{3,2},{4,5},{5,4},{6,7},{7,6},{8,9},{9,8},{10,11... | collective-permute-start | bytes 12582920 | tf_op jit(solution)/shard_map/ppermute | solution.py:432
  76.0 5.7 %copy-start.23 = (s32[128]{0:T(128)S(1)}, s32[128]{0:T(128)}, u32[]{:S(2)}) copy-start(s32[128]{0:T(128)} %param.13) | copy-start | bytes 1540
  76.0 5.8 %copy-start.20 = (s32[128,8]{0,1:T(8,128)S(1)}, s32[128,8]{0,1:T(8,128)}, u32[]{:S(2)}) copy-start(s32[128,8]{0,1:T(8,128)} %param.11) | copy-start | bytes 12292
  76.0 5.8 %copy-start.22 = (bf16[128,8]{0,1:T(8,128)(2,1)S(1)}, bf16[128,8]{0,1:T(8,128)(2,1)}, u32[]{:S(2)}) copy-start(bf16[128,8]{0,1:T(8,128)(2,1)} %param.12) | copy-start | bytes 6148
  76.1 44.4 %all-to-all-start = ((bf16[64,8,2048]{2,1,0:T(8,128)(2,1)}), bf16[64,8,2048]{2,1,0:T(8,128)(2,1)}, u32[]{:S(2)}, u32[]{:S(2)}) async-start(bf16[64,8,2048]{2,1,0:T(8,128)(2,1)} %bitcast.5), calls=%async_computation | async-start | bytes 4194304 | tf_op jit(solution)/shard_map/all_to_all | solution.py:446
  81.8 4.9 %copy-start.17 = (bf16[1,16,768]{2,1,0:T(8,128)(2,1)S(1)}, bf16[1,16,768]{2,1,0:T(8,128)(2,1)}, u32[]{:S(2)}) copy-start(bf16[1,16,768]{2,1,0:T(8,128)(2,1)} %a_ref.3) | copy-start | bytes 73732
  82.0 32.3 %collective-permute-start.4 = (bf16[64,2048]{1,0:T(8,128)(2,1)S(1)}, bf16[64,2048]{1,0:T(8,128)(2,1)S(1)}, u32[]{:S(2)}, u32[]{:S(2)}) collective-permute-start(bf16[64,2048]{1,0:T(8,128)(2,1)S(1)} %pad_maximum_fusion.refs_4_), channel_id=1, source_target_pairs={{0,32},{2,34},{4,36},{6,38},{8,40},{10,42},{12,44},{14,46},{16,48}... | collective-permute-start | bytes 786440 | tf_op jit(solution)/shard_map/ppermute | solution.py:442
  83.0 36.1 %collective-permute-start.5 = (bf16[64,2048]{1,0:T(8,128)(2,1)S(1)}, bf16[64,2048]{1,0:T(8,128)(2,1)S(1)}, u32[]{:S(2)}, u32[]{:S(2)}) collective-permute-start(bf16[64,2048]{1,0:T(8,128)(2,1)S(1)} %pad_maximum_fusion.refs_4_), channel_id=1, source_target_pairs={{0,64},{2,66},{4,68},{6,70},{8,72},{10,74},{12,76},{14,78},{16,80}... | collective-permute-start | bytes 786440 | tf_op jit(solution)/shard_map/ppermute | solution.py:442
  85.6 34.1 %collective-permute-start.6 = (bf16[64,2048]{1,0:T(8,128)(2,1)S(1)}, bf16[64,2048]{1,0:T(8,128)(2,1)S(1)}, u32[]{:S(2)}, u32[]{:S(2)}) collective-permute-start(bf16[64,2048]{1,0:T(8,128)(2,1)S(1)} %pad_maximum_fusion.refs_4_), channel_id=1, source_target_pairs={{0,96},{2,98},{4,100},{6,102},{8,104},{10,106},{12,108},{14,110},{... | collective-permute-start | bytes 786440 | tf_op jit(solution)/shard_map/ppermute | solution.py:442
  107.2 1.2 copy-start.1
  108.3 0.6 copy-start.15
  114.3 0.7 copy-start.8
  119.0 0.7 copy-start.10
  119.7 0.7 copy-start.12
  120.4 5.6 %collective-permute-start.7 = (bf16[512,2048]{1,0:T(8,128)(2,1)}, bf16[512,2048]{1,0:T(8,128)(2,1)S(1)}, u32[]{:S(2)}, u32[]{:S(2)}) collective-permute-start(bf16[512,2048]{1,0:T(8,128)(2,1)} %bitcast.6.own_ref), channel_id=1, source_target_pairs={{0,1},{1,0},{2,3},{3,2},{4,5},{5,4},{6,7},{7,6},{8,9},{9,8},{10,11... | collective-permute-start | bytes 6291464 | tf_op jit(solution)/shard_map/ppermute | solution.py:432
  122.0 17.2 %collective-permute-start.8 = (bf16[136,2048]{1,0:T(8,128)(2,1)S(1)}, bf16[136,2048]{1,0:T(8,128)(2,1)S(1)}, u32[]{:S(2)}, u32[]{:S(2)}) collective-permute-start(bf16[136,2048]{1,0:T(8,128)(2,1)S(1)} %fusion.1.refs_0_.refs_4_), channel_id=1, source_target_pairs={{0,2},{2,4},{4,6},{6,0},{8,10},{10,12},{12,14},{14,8},{16,18},{18,... | collective-permute-start | bytes 1671176 | tf_op jit(solution)/shard_map/ppermute | solution.py:442
  122.0 27.3 %collective-permute-start.9 = (bf16[136,2048]{1,0:T(8,128)(2,1)S(1)}, bf16[136,2048]{1,0:T(8,128)(2,1)S(1)}, u32[]{:S(2)}, u32[]{:S(2)}) collective-permute-start(bf16[136,2048]{1,0:T(8,128)(2,1)S(1)} %fusion.1.refs_0_.refs_4_), channel_id=1, source_target_pairs={{0,4},{2,6},{4,0},{6,2},{8,12},{10,14},{12,8},{14,10},{16,20},{18,... | collective-permute-start | bytes 1671176 | tf_op jit(solution)/shard_map/ppermute | solution.py:442
  124.6 25.1 %collective-permute-start.10 = (bf16[136,2048]{1,0:T(8,128)(2,1)S(1)}, bf16[136,2048]{1,0:T(8,128)(2,1)S(1)}, u32[]{:S(2)}, u32[]{:S(2)}) collective-permute-start(bf16[136,2048]{1,0:T(8,128)(2,1)S(1)} %fusion.1.refs_0_.refs_4_), channel_id=1, source_target_pairs={{0,6},{2,0},{4,2},{6,4},{8,14},{10,8},{12,10},{14,12},{16,22},{18,... | collective-permute-start | bytes 1671176 | tf_op jit(solution)/shard_map/ppermute | solution.py:442
  126.0 0.8 copy-start.16
  126.8 0.7 copy-start.18
  127.5 22.2 %copy-start.9 = (bf16[64,2048]{1,0:T(8,128)(2,1)S(1)}, bf16[64,2048]{1,0:T(8,128)(2,1)}, u32[]{:S(2)}) copy-start(bf16[64,2048]{1,0:T(8,128)(2,1)} %copy-done.8) | copy-start | bytes 786436
  127.5 22.2 %copy-start.11 = (bf16[64,2048]{1,0:T(8,128)(2,1)S(1)}, bf16[64,2048]{1,0:T(8,128)(2,1)}, u32[]{:S(2)}) copy-start(bf16[64,2048]{1,0:T(8,128)(2,1)} %copy-done.10) | copy-start | bytes 786436
  127.5 22.2 %copy-start.13 = (bf16[64,2048]{1,0:T(8,128)(2,1)S(1)}, bf16[64,2048]{1,0:T(8,128)(2,1)}, u32[]{:S(2)}) copy-start(bf16[64,2048]{1,0:T(8,128)(2,1)} %copy-done.12) | copy-start | bytes 786436
  139.2 12.8 %copy-start.6 = (bf16[512,768]{1,0:T(8,128)(2,1)}, bf16[512,768]{1,0:T(8,128)(2,1)S(1)}, u32[]{:S(2)}) copy-start(bf16[512,768]{1,0:T(8,128)(2,1)S(1)} %get-tuple-element.68.refs_1_) | copy-start | bytes 2359300
  139.2 13.9 %copy-start.14 = (bf16[16,16,128]{2,1,0:T(8,128)(2,1)}, bf16[16,16,128]{2,1,0:T(8,128)(2,1)S(1)}, u32[]{:S(2)}) copy-start(bf16[16,16,128]{2,1,0:T(8,128)(2,1)S(1)} %get-tuple-element.44) | copy-start | bytes 196612
  152.0 6.0 %collective-permute-start.11 = (f32[512,256]{1,0:T(8,128)}, f32[512,256]{1,0:T(8,128)}, u32[]{:S(2)}, u32[]{:S(2)}) collective-permute-start(f32[512,256]{1,0:T(8,128)} %project_readout.1.own_ref), channel_id=1, source_target_pairs={{0,1},{1,0},{2,3},{3,2},{4,5},{5,4},{6,7},{7,6},{8,9},{9,8},{10,11... | collective-permute-start | bytes 1572872 | tf_op jit(solution)/shard_map/ppermute | solution.py:432
  153.1 11.4 %all-to-all-start.2 = ((bf16[16,16,128]{2,1,0:T(8,128)(2,1)}), bf16[16,16,128]{2,1,0:T(8,128)(2,1)S(1)}, u32[]{:S(2)}, u32[]{:S(2)}) async-start(bf16[16,16,128]{2,1,0:T(8,128)(2,1)} %copy-done.14), calls=%async_computation.2 | async-start | bytes 131072 | tf_op jit(solution)/shard_map/all_to_all | solution.py:446
  162.9 0.8 copy-start.3
  164.5 2.3 %collective-permute-start.12 = (bf16[16,16,128]{2,1,0:T(8,128)(2,1)S(1)}, bf16[16,16,128]{2,1,0:T(8,128)(2,1)S(1)}, u32[]{:S(2)}, u32[]{:S(2)}) collective-permute-start(bf16[16,16,128]{2,1,0:T(8,128)(2,1)S(1)} %all-to-all-done.2.own_ref), channel_id=1, source_target_pairs={{0,1},{1,0},{2,3},{3,2},{4,5},{5,4},{6,7},{7,6},{8,9},{9,8},{10,11... | collective-permute-start | bytes 196616 | tf_op jit(solution)/shard_map/ppermute | solution.py:432
  166.8 1.0 copy-start.4
  168.6 3.7 %collective-permute-start.13 = (f32[8,128]{1,0:T(8,128)S(1)}, f32[8,128]{1,0:T(8,128)S(1)}, u32[]{:S(2)}, u32[]{:S(2)}) collective-permute-start(f32[8,128]{1,0:T(8,128)S(1)} %get-tuple-element.63.refs_0_), channel_id=1, source_target_pairs={{0,2},{2,4},{4,6},{6,0},{8,10},{10,12},{12,14},{14,8},{16,18},{18,... | collective-permute-start | bytes 12296 | tf_op jit(solution)/shard_map/ppermute | solution.py:442
  168.7 4.3 %collective-permute-start.14 = (f32[8,128]{1,0:T(8,128)S(1)}, f32[8,128]{1,0:T(8,128)S(1)}, u32[]{:S(2)}, u32[]{:S(2)}) collective-permute-start(f32[8,128]{1,0:T(8,128)S(1)} %get-tuple-element.63.refs_0_), channel_id=1, source_target_pairs={{0,4},{2,6},{4,0},{6,2},{8,12},{10,14},{12,8},{14,10},{16,20},{18,... | collective-permute-start | bytes 12296 | tf_op jit(solution)/shard_map/ppermute | solution.py:442
  172.0 2.5 %collective-permute-start.15 = (f32[8,128]{1,0:T(8,128)S(1)}, f32[8,128]{1,0:T(8,128)S(1)}, u32[]{:S(2)}, u32[]{:S(2)}) collective-permute-start(f32[8,128]{1,0:T(8,128)S(1)} %get-tuple-element.63.refs_0_), channel_id=1, source_target_pairs={{0,6},{2,0},{4,2},{6,4},{8,14},{10,8},{12,10},{14,12},{16,22},{18,... | collective-permute-start | bytes 12296 | tf_op jit(solution)/shard_map/ppermute | solution.py:442
  174.4 1.0 copy-start.5
  175.4 24.8 %copy-start.2 = (bf16[1024,768]{1,0:T(8,128)(2,1)S(1)}, bf16[1024,768]{1,0:T(8,128)(2,1)}, u32[]{:S(2)}) copy-start(bf16[1024,768]{1,0:T(8,128)(2,1)} %copy-done.1) | copy-start | bytes 4718596
  175.4 24.8 %copy-start.7 = (bf16[512,768]{1,0:T(8,128)(2,1)S(1)}, bf16[512,768]{1,0:T(8,128)(2,1)}, u32[]{:S(2)}) copy-start(bf16[512,768]{1,0:T(8,128)(2,1)} %copy-done.6) | copy-start | bytes 2359300
  203.1 4.3 %collective-permute-start.16 = (f32[16,2048]{1,0:T(8,128)S(1)}, f32[16,2048]{1,0:T(8,128)S(1)}, u32[]{:S(2)}, u32[]{:S(2)}) collective-permute-start(f32[16,2048]{1,0:T(8,128)S(1)} %get-tuple-element.70), channel_id=1, source_target_pairs={{0,1},{1,0},{2,3},{3,2},{4,5},{5,4},{6,7},{7,6},{8,9},{9,8},{10,11... | collective-permute-start | bytes 393224 | tf_op jit(solution)/shard_map/ppermute | solution.py:432

commit v5 on v4

--- a/solution.py
+++ b/solution.py
@@ -11,7 +11,7 @@
 BF16 = jnp.bfloat16
 ROWS = 8
 LINE = 4
-PARTS = (16, 8)
+PARTS = (24,)
 
 
 def iota(shape, dim):
@@ -108,14 +108,13 @@
             bytes_accessed=2 * sum(sizes) * half,
             transcendentals=0,
         ),
-        compiler_params=pltpu.CompilerParams(vmem_limit_bytes=20 * 1024 * 1024),
+        compiler_params=pltpu.CompilerParams(vmem_limit_bytes=58 * 1024 * 1024),
         name="dispatch_rows",
     )(core, ids_t, rows)
 
 
-def experts_body(groups, count, steps, last, core_ref, own_ref, other_ref, go_ref, gx_ref, uo_ref, ux_ref, a_ref, *refs):
-    before_refs, (hid_ref, lat_ref, acc_ref) = refs[:-3], refs[-3:]
-    n = pl.program_id(0)
+def experts_body(count, steps, core_ref, own_ref, other_ref, go_ref, gx_ref, uo_ref, ux_ref, a_ref, hid_ref, lat_ref, acc_ref):
+    n = pl.program_id(1)
     own, other = own_ref[...], other_ref[...]
     gate = dot(own, go_ref[0]) + dot(other, gx_ref[0])
     up = dot(own, uo_ref[0]) + dot(other, ux_ref[0])
@@ -135,65 +134,60 @@
 
     @pl.when(n == steps - 1)
     def _():
-        rows = groups * count
+        rows = acc_ref.shape[0]
         mine = jnp.where(own_lanes(rows, rank, count), acc_ref[...], 0.0).astype(BF16)
         width = ROWS * rank
-        shape = (groups // LINE, rows)
+        lines = lat_ref.shape[0]
+        shape = (lines, rows)
         for step in range(LINE):
             block = lax.rem(core_ref[1] + LINE - step, LINE)
             pick = ones_where(iota(shape, 1) // count == iota(shape, 0) * LINE + block)
             now = dot(pick, mine).astype(BF16)
-            if last:
-                at = step * LINE
-                for piece in [ref[step] for ref in before_refs] + [now]:
-                    for c in range(piece.shape[1] // width):
-                        lat_ref[:, at, :] = piece[:, c * width : (c + 1) * width]
-                        at += 1
-                for c in range(at, (step + 1) * LINE):
-                    lat_ref[:, c, :] = jnp.zeros((groups // LINE, width), BF16)
-            else:
-                lat_ref[step] = now
-
-
-def experts_forward(core, own, other, gate, up, adapter_a, before, groups, last):
-    rows, half = own.shape
-    count = rows // groups
+            for c in range(count // ROWS):
+                lat_ref[:, step * LINE + c, :] = now[:, c * width : (c + 1) * width]
+            for c in range(count // ROWS, LINE):
+                lat_ref[:, step * LINE + c, :] = jnp.zeros((lines, width), BF16)
+
+
+def experts_forward(core, own, other, gate, up, adapter_a, groups):
+    total, half = own.shape
+    count = total // groups
     hidden_units = gate.shape[2]
     rank = adapter_a.shape[1]
     block = min(256, hidden_units)
     steps = hidden_units // block
-    width = count * rank
-    mine = pl.BlockSpec((1, half, block), lambda n, c: (0, c[0], n))
-    theirs = pl.BlockSpec((1, half, block), lambda n, c: (0, 1 - c[0], n))
-    whole = pl.BlockSpec((rows, half), lambda n, c: (0, 0))
-    in_specs = [whole, whole, mine, theirs, mine, theirs, pl.BlockSpec((1, rank, block), lambda n, c: (0, 0, n))]
-    in_specs += [full(x.shape) for x in before]
+    passes = 2
+    rows = total // passes
     lines = groups // LINE
-    out = (lines, LINE * LINE, ROWS * rank) if last else (LINE, lines, width)
-    return pl.pallas_call(
-        functools.partial(experts_body, groups, count, steps, last),
+    mine = pl.BlockSpec((1, half, block), lambda m, n, c: (0, c[0], n))
+    theirs = pl.BlockSpec((1, half, block), lambda m, n, c: (0, 1 - c[0], n))
+    some = pl.BlockSpec((rows, half), lambda m, n, c: (m, 0))
+    lat = (LINE * LINE, ROWS * rank)
+    return pl.pallas_call(
+        functools.partial(experts_body, count, steps),
         grid_spec=pltpu.PrefetchScalarGridSpec(
             num_scalar_prefetch=1,
-            grid=(steps,),
-            in_specs=in_specs,
+            grid=(passes, steps),
+            in_specs=[some, some, mine, theirs, mine, theirs]
+            + [pl.BlockSpec((1, rank, block), lambda m, n, c: (0, 0, n))],
             out_specs=[
-                pl.BlockSpec((rows, block), lambda n, c: (0, n)),
-                full(out),
+                pl.BlockSpec((rows, block), lambda m, n, c: (m, n)),
+                pl.BlockSpec((lines // passes, *lat), lambda m, n, c: (m, 0, 0)),
             ],
-            scratch_shapes=[pltpu.VMEM((rows, width), F32)],
+            scratch_shapes=[pltpu.VMEM((rows, count * rank), F32)],
         ),
         out_shape=[
-            jax.ShapeDtypeStruct((rows, hidden_units), BF16),
-            jax.ShapeDtypeStruct(out, BF16),
+            jax.ShapeDtypeStruct((total, hidden_units), BF16),
+            jax.ShapeDtypeStruct((lines, *lat), BF16),
         ],
         cost_estimate=pl.CostEstimate(
-            flops=8 * rows * half * hidden_units,
-            bytes_accessed=8 * half * hidden_units + 4 * rows * half,
-            transcendentals=rows * hidden_units,
-        ),
-        compiler_params=pltpu.CompilerParams(vmem_limit_bytes=48 * 1024 * 1024),
+            flops=8 * total * half * hidden_units,
+            bytes_accessed=8 * passes * half * hidden_units + 4 * total * half,
+            transcendentals=total * hidden_units,
+        ),
+        compiler_params=pltpu.CompilerParams(vmem_limit_bytes=60 * 1024 * 1024),
         name="experts_forward",
-    )(core, own, other, gate, gate, up, up, adapter_a, *before)
+    )(core, own, other, gate, gate, up, up, adapter_a)
 
 
 def project_body(tokens, *refs):
@@ -485,18 +479,12 @@
     sent = list(dispatch(place, ids_t, hidden_in, groups))
     sent[0], adapters = lax.optimization_barrier((sent[0], adapters))
     x = exchange(sent[0].reshape(groups, PARTS[0], half)).reshape(groups * PARTS[0], half)
-    y = exchange(sent[1].reshape(groups, PARTS[1], half)).reshape(groups * PARTS[1], half)
-    acts, sums = experts_forward(
-        place, x, swap(x), gate_proj, up_proj, adapter_a, [], groups, False
-    )
+    x, adapters, own_readout = lax.optimization_barrier((x, adapters, own_readout))
     adapters = [moved(adapters, groups, LINE**2, step) for step in range(LINE)]
-    y, acts, adapters, own_readout = lax.optimization_barrier((y, acts, adapters, own_readout))
     readouts = [moved(own_readout, groups, 1, step) for step in range(LINE)]
-    last_acts, latents = experts_forward(
-        place, y, swap(y), gate_proj, up_proj, adapter_a, [sums], groups, True
-    )
-    last_acts, adapters, readouts = lax.optimization_barrier((last_acts, adapters, readouts))
-    hidden = [acts, last_acts]
+    acts, latents = experts_forward(place, x, swap(x), gate_proj, up_proj, adapter_a, groups)
+    acts, adapters, readouts = lax.optimization_barrier((acts, adapters, readouts))
+    hidden = [acts]
     projections = project(readouts, adapters, tokens)
     picked, gains = pick(place, projections, swap(projections), readouts, tokens, chunks)
     latents, picked = lax.optimization_barrier((exchange(latents, planes), picked))

time: 209 us -> 216 us (1.033)
  waiting for transfers between devices: 25.3 us -> 97.5 us
  blocking collectives: 80.4 us -> 20.8 us
  local copies, waits for them, and re-layouts: 11.1 us -> 3.77 us
    all_to_all x2, waiting for transfers between devices: 0.84 us -> 87.5 us  [exchange(): lax.all_to_all(payload, 'wide', split_axis=0, concat_axis=0, tiled=True,...]
    all_to_all x2 -> x1, blocking collectives: 80.4 us -> 20.8 us  [exchange(): lax.all_to_all(payload, 'wide', split_axis=0, concat_axis=0, tiled=True,...]
    ppermute x12, waiting for transfers between devices: 22.1 us -> 7.96 us  [moved(): return lax.ppermute(payload, 'wide', moves)]
    unnamed x48 -> x18, local copies, waits for them, and re-layouts: 10.1 us -> 2.78 us
    all_to_all x2, starting transfers between devices: 10.5 us -> 14.5 us  [exchange(): lax.all_to_all(payload, 'wide', split_axis=0, concat_axis=0, tiled=True,...]
    ppermute x5 -> x4, starting transfers between devices: 11.1 us -> 7.94 us  [swap(): return lax.ppermute(payload, 'narrow', [(0, 1), (1, 0)])]
    pallas_call x2 -> x1, Pallas kernels: 32.1 us -> 29.7 us  [experts_forward(): pl.pallas_call(functools.partial(experts_body, count, steps), grid_spec=p...]
  transfers between devices with their start and end apart: 19 -> 18, of which waited for: 11 -> 7; matrix products, arithmetic and copies ran while one was open for 0% -> 0% of each run, Pallas kernels for 20% -> 19%
where the time goes in v5:
time: 216 us; the launch traced here: 215 us
  waiting for transfers between devices  97.5 us (45%)
  Pallas kernels  53.2 us (25%)
  starting transfers between devices  37.5 us (17%)
  blocking collectives  20.8 us (10%)
  local copies, waits for them, and re-layouts  3.77 us (2%)
    all_to_all x2, waiting for transfers between devices, exchange(): lax.all_to_all(payload, 'wide', split_axis=0, concat_axis=0, tiled=True,...  87.5 us
    pallas_call x1, Pallas kernels, experts_forward(): pl.pallas_call(functools.partial(experts_body, count, steps), grid_spec=p...  29.7 us
    all_to_all x1, blocking collectives, exchange(): lax.all_to_all(payload, 'wide', split_axis=0, concat_axis=0, tiled=True,...  20.8 us
    ppermute x12, starting transfers between devices, moved(): return lax.ppermute(payload, 'wide', moves)  15 us
    all_to_all x2, starting transfers between devices, exchange(): lax.all_to_all(payload, 'wide', split_axis=0, concat_axis=0, tiled=True,...  14.5 us
    ppermute x12, waiting for transfers between devices, moved(): return lax.ppermute(payload, 'wide', moves)  7.96 us
    ppermute x4, starting transfers between devices, swap(): return lax.ppermute(payload, 'narrow', [(0, 1), (1, 0)])  7.94 us
    pallas_call x1, Pallas kernels, dispatch(): pl.pallas_call(functools.partial(dispatch_body, experts), grid_spec=pltpu...  6.53 us
  transfers between devices with their start and end apart: 18, of which 7 were waited for; matrix products, arithmetic and copies ran while one was open for 0% of the time, Pallas kernels for 19%

profile of v5, /device:TPU:1, one launch (start us, length us, event | category | flops | bytes accessed | tf_op | source)
XLA Modules:
  0.0 215.0 jit_solution(2237552621737909287)
XLA Ops:
  0.6 0.0 copy-start
  0.7 0.9 dynamic-slice_bitcast_fusion
  1.6 2.0 collective-permute-start
  3.6 2.5 %collective-permute-start.1 = (bf16[16,2048]{1,0:T(8,128)(2,1)S(1)}, bf16[16,2048]{1,0:T(8,128)(2,1)S(1)}, u32[]{:S(2)}, u32[]{:S(2)}) collective-permute-start(bf16[16,2048]{1,0:T(8,128)(2,1)S(1)} %dynamic-slice_bitcast_fusion), channel_id=1, source_target_pairs={{0,16},{2,18},{4,20},{6,22},{8,24},{10,26},{12,28},{14,30},{16,0},... | collective-permute-start | bytes 196616 | tf_op jit(solution)/shard_map/ppermute | solution.py:436
  6.1 1.2 collective-permute-start.2
  7.2 0.6 pad_add_fusion.core_ref.place_ref
  7.8 6.5 %dispatch_rows.1 = bf16[1536,2048]{1,0:T(8,128)(2,1)} custom-call(s32[4]{0:T(128)} %pad_add_fusion.core_ref.place_ref, s32[8,128]{1,0:T(8,128)} %bitcast.18, bf16[128,4096]{1,0:T(8,128)(2,1)} %rows_ref.1), custom_call_target="tpu_custom_call" | custom-call | flops 805306368 | bytes 6291456 | tf_op jit(solution)/shard_map/dispatch_rows/pallas_call | solution.py:93
  14.4 0.0 collective-permute-done
  14.4 0.0 collective-permute-done.1
  14.4 0.0 collective-permute-done.2
  14.4 0.0 copy-start.8
  14.4 0.0 copy-start.6
  14.4 0.0 copy-start.7
  14.4 9.1 %all-to-all-start = ((bf16[64,24,2048]{2,1,0:T(8,128)(2,1)}), bf16[64,24,2048]{2,1,0:T(8,128)(2,1)}, u32[]{:S(2)}, u32[]{:S(2)}) async-start(bf16[64,24,2048]{2,1,0:T(8,128)(2,1)} %bitcast.16), calls=%async_computation | async-start | bytes 12582912 | tf_op jit(solution)/shard_map/all_to_all | solution.py:440
  23.7 86.7 %all-to-all-done = bf16[64,24,2048]{2,1,0:T(8,128)(2,1)} async-done(((bf16[64,24,2048]{2,1,0:T(8,128)(2,1)}), bf16[64,24,2048]{2,1,0:T(8,128)(2,1)}, u32[]{:S(2)}, u32[]{:S(2)}) %all-to-all-start) | async-done | bytes 6291488 | tf_op jit(solution)/shard_map/all_to_all | solution.py:440
  110.4 2.4 %collective-permute-start.3 = (bf16[1536,2048]{1,0:T(8,128)(2,1)}, bf16[1536,2048]{1,0:T(8,128)(2,1)}, u32[]{:S(2)}, u32[]{:S(2)}) collective-permute-start(bf16[1536,2048]{1,0:T(8,128)(2,1)} %bitcast.7.own_ref), channel_id=1, source_target_pairs={{0,1},{1,0},{2,3},{3,2},{4,5},{5,4},{6,7},{7,6},{8,9},{9,8},{10,11... | collective-permute-start | bytes 18874376 | tf_op jit(solution)/shard_map/ppermute | solution.py:426
  112.8 0.0 collective-permute-start.8
  112.8 2.7 %collective-permute-start.9 = (bf16[136,2048]{1,0:T(8,128)(2,1)S(1)}, bf16[136,2048]{1,0:T(8,128)(2,1)S(1)}, u32[]{:S(2)}, u32[]{:S(2)}) collective-permute-start(bf16[136,2048]{1,0:T(8,128)(2,1)S(1)} %fusion.1.refs_0_.refs_4_), channel_id=1, source_target_pairs={{0,6},{2,0},{4,2},{6,4},{8,14},{10,8},{12,10},{14,12},{16,22},{18,... | collective-permute-start | bytes 1671176 | tf_op jit(solution)/shard_map/ppermute | solution.py:436
  115.5 6.5 %collective-permute-done.4.refs_5_ = bf16[64,2048]{1,0:T(8,128)(2,1)S(1)} collective-permute-done((bf16[64,2048]{1,0:T(8,128)(2,1)S(1)}, bf16[64,2048]{1,0:T(8,128)(2,1)S(1)}, u32[]{:S(2)}, u32[]{:S(2)}) %collective-permute-start.4) | collective-permute-done | bytes 262176 | tf_op jit(solution)/shard_map/ppermute | solution.py:436
  122.0 0.9 collective-permute-start.5
  122.8 0.1 collective-permute-done.3.other_ref
  122.9 0.4 collective-permute-start.6
  123.4 29.7 %experts_forward.1 = (bf16[1536,768]{1,0:T(8,128)(2,1)}, bf16[16,16,128]{2,1,0:T(8,128)(2,1)}) custom-call(s32[4]{0:T(128)} %pad_add_fusion.core_ref.place_ref, bf16[1536,2048]{1,0:T(8,128)(2,1)} %bitcast.7.own_ref, bf16[1536,2048]{1,0:T(8,128)(2,1)} %collective-permute-done.3.other_ref, bf16[1,4096,768]{2,1,0:T(8,128)(2,1)} %gx_ref.1, ...), custom_call_target="tpu_custom_call" | custom-call | flops 19327352832 | bytes 37748736 | tf_op jit(solution)/shard_map/experts_forward/pallas_call | solution.py:166
  153.1 0.0 collective-permute-done.5.refs_6_
  153.1 0.0 collective-permute-done.6.refs_7_
  153.1 0.0 collective-permute-done.9.refs_3_.refs_7_
  153.1 3.2 %project_readout.1.own_ref = f32[512,256]{1,0:T(8,128)} custom-call(bf16[136,2048]{1,0:T(8,128)(2,1)S(1)} %fusion.1.refs_0_.refs_4_, bf16[136,2048]{1,0:T(8,128)(2,1)S(1)} %collective-permute-done.7.refs_1_.refs_5_, bf16[136,2048]{1,0:T(8,128)(2,1)S(1)} %collective-permute-done.8.refs_2_.refs_6_, ...), custom_call_target="tpu_custom_call" | custom-call | flops 536870912 | bytes 3145728 | tf_op jit(solution)/shard_map/project_readout/pallas_call | solution.py:203
  156.3 1.1 collective-permute-start.10
  157.5 5.4 %all-to-all-start.1 = ((bf16[16,16,128]{2,1,0:T(8,128)(2,1)}), bf16[16,16,128]{2,1,0:T(8,128)(2,1)S(1)}, u32[]{:S(2)}, u32[]{:S(2)}) async-start(bf16[16,16,128]{2,1,0:T(8,128)(2,1)} %get-tuple-element.32), calls=%async_computation.1 | async-start | bytes 131072 | tf_op jit(solution)/shard_map/all_to_all | solution.py:440
  162.9 0.0 collective-permute-done.10.other_ref
  163.0 4.9 %pick_projections.1 = (f32[192,128]{1,0:T(8,128)S(1)}, bf16[1536,128]{1,0:T(8,128)(2,1)S(1)}) custom-call(s32[4]{0:T(128)S(1)} %copy-done.5, f32[512,256]{1,0:T(8,128)} %project_readout.1.own_ref, f32[512,256]{1,0:T(8,128)} %collective-permute-done.10.other_ref, bf16[136,2048]{1,0:T(8,128)(2,1)S(1)} %fusion.1.refs_0_.refs_4_, ...), custom_call_target="tpu_custom_call" | custom-call | tf_op jit(solution)/shard_map/pick_projections/pallas_call | solution.py:257
  167.9 0.8 copy-done.2
  168.6 0.8 all-to-all-done.1.own_ref
  169.5 1.4 collective-permute-start.11
  170.9 0.9 collective-permute-done.11.other_ref
  171.8 1.0 copy-done.3
  172.8 0.8 rate_tokens.1
  173.6 3.0 %collective-permute-start.12 = (f32[8,128]{1,0:T(8,128)S(1)}, f32[8,128]{1,0:T(8,128)S(1)}, u32[]{:S(2)}, u32[]{:S(2)}) collective-permute-start(f32[8,128]{1,0:T(8,128)S(1)} %get-tuple-element.48.refs_0_), channel_id=1, source_target_pairs={{0,2},{2,4},{4,6},{6,0},{8,10},{10,12},{12,14},{14,8},{16,18},{18,... | collective-permute-start | bytes 12296 | tf_op jit(solution)/shard_map/ppermute | solution.py:436
  176.6 2.5 %collective-permute-start.14 = (f32[8,128]{1,0:T(8,128)S(1)}, f32[8,128]{1,0:T(8,128)S(1)}, u32[]{:S(2)}, u32[]{:S(2)}) collective-permute-start(f32[8,128]{1,0:T(8,128)S(1)} %get-tuple-element.48.refs_0_), channel_id=1, source_target_pairs={{0,6},{2,0},{4,2},{6,4},{8,14},{10,8},{12,10},{14,12},{16,22},{18,... | collective-permute-start | bytes 12296 | tf_op jit(solution)/shard_map/ppermute | solution.py:436
  179.1 1.5 collective-permute-done.13.refs_2_
  180.5 0.0 collective-permute-done.14.refs_3_
  180.5 1.0 copy-done.4
  181.5 4.1 %weigh_tokens.1 = (f32[1,128]{1,0:T(1,128)}, bf16[16,16,2176]{2,1,0:T(8,128)(2,1)S(1)}) custom-call(f32[8,128]{1,0:T(8,128)S(1)} %get-tuple-element.48.refs_0_, f32[8,128]{1,0:T(8,128)S(1)} %collective-permute-done.12.refs_1_, f32[8,128]{1,0:T(8,128)S(1)} %collective-permute-done.13.refs_2_, f32[8,128]{1,0:T(8,128)S(1)} %collective-permute-done.14.refs_3_, ...), custom_call_target="tpu_custom_call" | custom-call | tf_op jit(solution)/shard_map/weigh_tokens/pallas_call | solution.py:361
  185.6 20.8 %all_to_all.15.packed_ref = bf16[16,16,2176]{2,1,0:T(8,128)(2,1)S(1)} all-to-all(bf16[16,16,2176]{2,1,0:T(8,128)(2,1)S(1)} %get-tuple-element.51), channel_id=1, replica_groups={{0,8,16,24,32,40,48,56,64,72,80,88,96,104,112,120},{2,10,18,26,34,42,50..., dimensions={0} | all-to-all | bytes 2228224 | tf_op jit(solution)/shard_map/all_to_all | solution.py:440
  206.4 3.9 %adapter_gradients.1 = (f32[16,768]{1,0:T(8,128)}, f32[16,2048]{1,0:T(8,128)S(1)}) custom-call(s32[4]{0:T(128)S(1)} %copy-done.5, bf16[16,16,2176]{2,1,0:T(8,128)(2,1)S(1)} %all_to_all.15.packed_ref, bf16[1536,768]{1,0:T(8,128)(2,1)S(1)} %copy-done.1), custom_call_target="tpu_custom_call" | custom-call | tf_op jit(solution)/shard_map/adapter_gradients/pallas_call | solution.py:411
  210.4 2.9 %collective-permute-start.15 = (f32[16,2048]{1,0:T(8,128)S(1)}, f32[16,2048]{1,0:T(8,128)S(1)}, u32[]{:S(2)}, u32[]{:S(2)}) collective-permute-start(f32[16,2048]{1,0:T(8,128)S(1)} %get-tuple-element.54), channel_id=1, source_target_pairs={{0,1},{1,0},{2,3},{3,2},{4,5},{5,4},{6,7},{7,6},{8,9},{9,8},{10,11... | collective-permute-start | bytes 393224 | tf_op jit(solution)/shard_map/ppermute | solution.py:426
  213.3 1.0 collective-permute-done.15
  214.3 0.7 maximum_select_fusion
  (24 shorter events, 0.2 us)
Async XLA Ops:
  0.6 23.0 %copy-start = (bf16[128,4096]{1,0:T(8,128)(2,1)S(1)}, bf16[128,4096]{1,0:T(8,128)(2,1)}, u32[]{:S(2)}) copy-start(bf16[128,4096]{1,0:T(8,128)(2,1)} %param.10) | copy-start | bytes 3145732
  1.6 12.8 %collective-permute-start = (bf16[16,2048]{1,0:T(8,128)(2,1)S(1)}, bf16[16,2048]{1,0:T(8,128)(2,1)S(1)}, u32[]{:S(2)}, u32[]{:S(2)}) collective-permute-start(bf16[16,2048]{1,0:T(8,128)(2,1)S(1)} %dynamic-slice_bitcast_fusion), channel_id=1, source_target_pairs={{0,8},{2,10},{4,12},{6,14},{8,16},{10,18},{12,20},{14,22},{16,24},... | collective-permute-start | bytes 196616 | tf_op jit(solution)/shard_map/ppermute | solution.py:436
  3.6 10.7 %collective-permute-start.1 = (bf16[16,2048]{1,0:T(8,128)(2,1)S(1)}, bf16[16,2048]{1,0:T(8,128)(2,1)S(1)}, u32[]{:S(2)}, u32[]{:S(2)}) collective-permute-start(bf16[16,2048]{1,0:T(8,128)(2,1)S(1)} %dynamic-slice_bitcast_fusion), channel_id=1, source_target_pairs={{0,16},{2,18},{4,20},{6,22},{8,24},{10,26},{12,28},{14,30},{16,0},... | collective-permute-start | bytes 196616 | tf_op jit(solution)/shard_map/ppermute | solution.py:436
  6.1 8.3 %collective-permute-start.2 = (bf16[16,2048]{1,0:T(8,128)(2,1)S(1)}, bf16[16,2048]{1,0:T(8,128)(2,1)S(1)}, u32[]{:S(2)}, u32[]{:S(2)}) collective-permute-start(bf16[16,2048]{1,0:T(8,128)(2,1)S(1)} %dynamic-slice_bitcast_fusion), channel_id=1, source_target_pairs={{0,24},{2,26},{4,28},{6,30},{8,0},{10,2},{12,4},{14,6},{16,8},{18,... | collective-permute-start | bytes 196616 | tf_op jit(solution)/shard_map/ppermute | solution.py:436
  14.4 9.1 %copy-start.8 = (s32[128]{0:T(128)S(1)}, s32[128]{0:T(128)}, u32[]{:S(2)}) copy-start(s32[128]{0:T(128)} %param.13) | copy-start | bytes 1540
  14.4 9.2 %copy-start.6 = (s32[128,8]{0,1:T(8,128)S(1)}, s32[128,8]{0,1:T(8,128)}, u32[]{:S(2)}) copy-start(s32[128,8]{0,1:T(8,128)} %param.11) | copy-start | bytes 12292
  14.4 9.2 %copy-start.7 = (bf16[128,8]{0,1:T(8,128)(2,1)S(1)}, bf16[128,8]{0,1:T(8,128)(2,1)}, u32[]{:S(2)}) copy-start(bf16[128,8]{0,1:T(8,128)(2,1)} %param.12) | copy-start | bytes 6148
  14.4 95.9 %all-to-all-start = ((bf16[64,24,2048]{2,1,0:T(8,128)(2,1)}), bf16[64,24,2048]{2,1,0:T(8,128)(2,1)}, u32[]{:S(2)}, u32[]{:S(2)}) async-start(bf16[64,24,2048]{2,1,0:T(8,128)(2,1)} %bitcast.16), calls=%async_computation | async-start | bytes 12582912 | tf_op jit(solution)/shard_map/all_to_all | solution.py:440
  110.4 12.6 %collective-permute-start.3 = (bf16[1536,2048]{1,0:T(8,128)(2,1)}, bf16[1536,2048]{1,0:T(8,128)(2,1)}, u32[]{:S(2)}, u32[]{:S(2)}) collective-permute-start(bf16[1536,2048]{1,0:T(8,128)(2,1)} %bitcast.7.own_ref), channel_id=1, source_target_pairs={{0,1},{1,0},{2,3},{3,2},{4,5},{5,4},{6,7},{7,6},{8,9},{9,8},{10,11... | collective-permute-start | bytes 18874376 | tf_op jit(solution)/shard_map/ppermute | solution.py:426
  112.8 9.1 %collective-permute-start.4 = (bf16[64,2048]{1,0:T(8,128)(2,1)S(1)}, bf16[64,2048]{1,0:T(8,128)(2,1)S(1)}, u32[]{:S(2)}, u32[]{:S(2)}) collective-permute-start(bf16[64,2048]{1,0:T(8,128)(2,1)S(1)} %pad_maximum_fusion.refs_4_), channel_id=1, source_target_pairs={{0,32},{2,34},{4,36},{6,38},{8,40},{10,42},{12,44},{14,46},{16,48}... | collective-permute-start | bytes 786440 | tf_op jit(solution)/shard_map/ppermute | solution.py:436
  112.8 40.3 %collective-permute-start.7 = (bf16[136,2048]{1,0:T(8,128)(2,1)S(1)}, bf16[136,2048]{1,0:T(8,128)(2,1)S(1)}, u32[]{:S(2)}, u32[]{:S(2)}) collective-permute-start(bf16[136,2048]{1,0:T(8,128)(2,1)S(1)} %fusion.1.refs_0_.refs_4_), channel_id=1, source_target_pairs={{0,2},{2,4},{4,6},{6,0},{8,10},{10,12},{12,14},{14,8},{16,18},{18,... | collective-permute-start | bytes 1671176 | tf_op jit(solution)/shard_map/ppermute | solution.py:436
  112.8 40.3 %collective-permute-start.8 = (bf16[136,2048]{1,0:T(8,128)(2,1)S(1)}, bf16[136,2048]{1,0:T(8,128)(2,1)S(1)}, u32[]{:S(2)}, u32[]{:S(2)}) collective-permute-start(bf16[136,2048]{1,0:T(8,128)(2,1)S(1)} %fusion.1.refs_0_.refs_4_), channel_id=1, source_target_pairs={{0,4},{2,6},{4,0},{6,2},{8,12},{10,14},{12,8},{14,10},{16,20},{18,... | collective-permute-start | bytes 1671176 | tf_op jit(solution)/shard_map/ppermute | solution.py:436
  112.8 40.3 %collective-permute-start.9 = (bf16[136,2048]{1,0:T(8,128)(2,1)S(1)}, bf16[136,2048]{1,0:T(8,128)(2,1)S(1)}, u32[]{:S(2)}, u32[]{:S(2)}) collective-permute-start(bf16[136,2048]{1,0:T(8,128)(2,1)S(1)} %fusion.1.refs_0_.refs_4_), channel_id=1, source_target_pairs={{0,6},{2,0},{4,2},{6,4},{8,14},{10,8},{12,10},{14,12},{16,22},{18,... | collective-permute-start | bytes 1671176 | tf_op jit(solution)/shard_map/ppermute | solution.py:436
  122.0 31.1 %collective-permute-start.5 = (bf16[64,2048]{1,0:T(8,128)(2,1)S(1)}, bf16[64,2048]{1,0:T(8,128)(2,1)S(1)}, u32[]{:S(2)}, u32[]{:S(2)}) collective-permute-start(bf16[64,2048]{1,0:T(8,128)(2,1)S(1)} %pad_maximum_fusion.refs_4_), channel_id=1, source_target_pairs={{0,64},{2,66},{4,68},{6,70},{8,72},{10,74},{12,76},{14,78},{16,80}... | collective-permute-start | bytes 786440 | tf_op jit(solution)/shard_map/ppermute | solution.py:436
  122.9 30.2 %collective-permute-start.6 = (bf16[64,2048]{1,0:T(8,128)(2,1)S(1)}, bf16[64,2048]{1,0:T(8,128)(2,1)}, u32[]{:S(2)}, u32[]{:S(2)}) collective-permute-start(bf16[64,2048]{1,0:T(8,128)(2,1)S(1)} %pad_maximum_fusion.refs_4_), channel_id=1, source_target_pairs={{0,96},{2,98},{4,100},{6,102},{8,104},{10,106},{12,108},{14,110},{... | collective-permute-start | bytes 786440 | tf_op jit(solution)/shard_map/ppermute | solution.py:436
  153.1 9.8 %copy-start.5 = (s32[4]{0:T(128)S(1)}, s32[4]{0:T(128)}, u32[]{:S(2)}) copy-start(s32[4]{0:T(128)} %pad_add_fusion.core_ref.place_ref) | copy-start | bytes 52
  156.3 6.6 %collective-permute-start.10 = (f32[512,256]{1,0:T(8,128)}, f32[512,256]{1,0:T(8,128)}, u32[]{:S(2)}, u32[]{:S(2)}) collective-permute-start(f32[512,256]{1,0:T(8,128)} %project_readout.1.own_ref), channel_id=1, source_target_pairs={{0,1},{1,0},{2,3},{3,2},{4,5},{5,4},{6,7},{7,6},{8,9},{9,8},{10,11... | collective-permute-start | bytes 1572872 | tf_op jit(solution)/shard_map/ppermute | solution.py:426
  157.5 12.0 %all-to-all-start.1 = ((bf16[16,16,128]{2,1,0:T(8,128)(2,1)}), bf16[16,16,128]{2,1,0:T(8,128)(2,1)S(1)}, u32[]{:S(2)}, u32[]{:S(2)}) async-start(bf16[16,16,128]{2,1,0:T(8,128)(2,1)} %get-tuple-element.32), calls=%async_computation.1 | async-start | bytes 131072 | tf_op jit(solution)/shard_map/all_to_all | solution.py:440
  167.9 0.8 copy-start.2
  169.5 2.3 %collective-permute-start.11 = (bf16[16,16,128]{2,1,0:T(8,128)(2,1)S(1)}, bf16[16,16,128]{2,1,0:T(8,128)(2,1)S(1)}, u32[]{:S(2)}, u32[]{:S(2)}) collective-permute-start(bf16[16,16,128]{2,1,0:T(8,128)(2,1)S(1)} %all-to-all-done.1.own_ref), channel_id=1, source_target_pairs={{0,1},{1,0},{2,3},{3,2},{4,5},{5,4},{6,7},{7,6},{8,9},{9,8},{10,11... | collective-permute-start | bytes 196616 | tf_op jit(solution)/shard_map/ppermute | solution.py:426
  171.8 1.0 copy-start.3
  173.6 5.5 %collective-permute-start.12 = (f32[8,128]{1,0:T(8,128)S(1)}, f32[8,128]{1,0:T(8,128)S(1)}, u32[]{:S(2)}, u32[]{:S(2)}) collective-permute-start(f32[8,128]{1,0:T(8,128)S(1)} %get-tuple-element.48.refs_0_), channel_id=1, source_target_pairs={{0,2},{2,4},{4,6},{6,0},{8,10},{10,12},{12,14},{14,8},{16,18},{18,... | collective-permute-start | bytes 12296 | tf_op jit(solution)/shard_map/ppermute | solution.py:436
  176.6 4.0 %collective-permute-start.13 = (f32[8,128]{1,0:T(8,128)S(1)}, f32[8,128]{1,0:T(8,128)S(1)}, u32[]{:S(2)}, u32[]{:S(2)}) collective-permute-start(f32[8,128]{1,0:T(8,128)S(1)} %get-tuple-element.48.refs_0_), channel_id=1, source_target_pairs={{0,4},{2,6},{4,0},{6,2},{8,12},{10,14},{12,8},{14,10},{16,20},{18,... | collective-permute-start | bytes 12296 | tf_op jit(solution)/shard_map/ppermute | solution.py:436
  176.6 4.0 %collective-permute-start.14 = (f32[8,128]{1,0:T(8,128)S(1)}, f32[8,128]{1,0:T(8,128)S(1)}, u32[]{:S(2)}, u32[]{:S(2)}) collective-permute-start(f32[8,128]{1,0:T(8,128)S(1)} %get-tuple-element.48.refs_0_), channel_id=1, source_target_pairs={{0,6},{2,0},{4,2},{6,4},{8,14},{10,8},{12,10},{14,12},{16,22},{18,... | collective-permute-start | bytes 12296 | tf_op jit(solution)/shard_map/ppermute | solution.py:436
  180.5 1.0 copy-start.4
  181.5 24.9 %copy-start.1 = (bf16[1536,768]{1,0:T(8,128)(2,1)S(1)}, bf16[1536,768]{1,0:T(8,128)(2,1)}, u32[]{:S(2)}) copy-start(bf16[1536,768]{1,0:T(8,128)(2,1)} %get-tuple-element.52.refs_0_) | copy-start | bytes 7077892
  210.4 3.9 %collective-permute-start.15 = (f32[16,2048]{1,0:T(8,128)S(1)}, f32[16,2048]{1,0:T(8,128)S(1)}, u32[]{:S(2)}, u32[]{:S(2)}) collective-permute-start(f32[16,2048]{1,0:T(8,128)S(1)} %get-tuple-element.54), channel_id=1, source_target_pairs={{0,1},{1,0},{2,3},{3,2},{4,5},{5,4},{6,7},{7,6},{8,9},{9,8},{10,11... | collective-permute-start | bytes 393224 | tf_op jit(solution)/shard_map/ppermute | solution.py:426

commit v6 on v4

--- a/solution.py
+++ b/solution.py
@@ -108,7 +108,7 @@
             bytes_accessed=2 * sum(sizes) * half,
             transcendentals=0,
         ),
-        compiler_params=pltpu.CompilerParams(vmem_limit_bytes=20 * 1024 * 1024),
+        compiler_params=pltpu.CompilerParams(vmem_limit_bytes=58 * 1024 * 1024),
         name="dispatch_rows",
     )(core, ids_t, rows)
 
@@ -490,12 +490,14 @@
         place, x, swap(x), gate_proj, up_proj, adapter_a, [], groups, False
     )
     adapters = [moved(adapters, groups, LINE**2, step) for step in range(LINE)]
-    y, acts, adapters, own_readout = lax.optimization_barrier((y, acts, adapters, own_readout))
+    y, acts, adapters[1], adapters[3], own_readout = lax.optimization_barrier(
+        (y, acts, adapters[1], adapters[3], own_readout)
+    )
     readouts = [moved(own_readout, groups, 1, step) for step in range(LINE)]
     last_acts, latents = experts_forward(
         place, y, swap(y), gate_proj, up_proj, adapter_a, [sums], groups, True
     )
-    last_acts, adapters, readouts = lax.optimization_barrier((last_acts, adapters, readouts))
+    last_acts, adapters[2], readouts = lax.optimization_barrier((last_acts, adapters[2], readouts))
     hidden = [acts, last_acts]
     projections = project(readouts, adapters, tokens)
     picked, gains = pick(place, projections, swap(projections), readouts, tokens, chunks)

time: 209 us -> 205 us (0.981)
  waiting for transfers between devices: 25.3 us -> 21.2 us
  local copies, waits for them, and re-layouts: 11.1 us -> 8.49 us
    ppermute x12, waiting for transfers between devices: 22.1 us -> 18.4 us  [moved(): return lax.ppermute(payload, 'wide', moves)]
    unnamed x48 -> x42, local copies, waits for them, and re-layouts: 10.1 us -> 7.5 us
  transfers between devices with their start and end apart: 19 -> 19, of which waited for: 11 -> 7; matrix products, arithmetic and copies ran while one was open for 0% -> 0% of each run, Pallas kernels for 20% -> 21%
where the time goes in v6:
time: 205 us; the launch traced here: 204 us
  blocking collectives  80.7 us (39%)
  Pallas kernels  53.2 us (26%)
  starting transfers between devices  38.1 us (19%)
  waiting for transfers between devices  21.2 us (10%)
  local copies, waits for them, and re-layouts  8.49 us (4%)
    all_to_all x2, blocking collectives, exchange(): lax.all_to_all(payload, 'wide', split_axis=0, concat_axis=0, tiled=True,...  80.7 us
    pallas_call x2, Pallas kernels, experts_forward(): pl.pallas_call(functools.partial(experts_body, groups, count, steps, last...  32.2 us
    ppermute x12, waiting for transfers between devices, moved(): return lax.ppermute(payload, 'wide', moves)  18.4 us
    ppermute x12, starting transfers between devices, moved(): return lax.ppermute(payload, 'wide', moves)  16.4 us
    all_to_all x2, starting transfers between devices, exchange(): lax.all_to_all(payload, 'wide', split_axis=0, concat_axis=0, tiled=True,...  12.1 us
    ppermute x5, starting transfers between devices, swap(): return lax.ppermute(payload, 'narrow', [(0, 1), (1, 0)])  9.6 us
    unnamed x42, local copies, waits for them, and re-layouts  7.5 us
    pallas_call x1, Pallas kernels, dispatch(): pl.pallas_call(functools.partial(dispatch_body, experts), grid_spec=pltpu...  6.22 us
  transfers between devices with their start and end apart: 19, of which 7 were waited for; matrix products, arithmetic and copies ran while one was open for 0% of the time, Pallas kernels for 21%

profile of v6, /device:TPU:1, one launch (start us, length us, event | category | flops | bytes accessed | tf_op | source)
XLA Modules:
  0.0 204.1 jit_solution(2502133763085865042)
XLA Ops:
  0.6 0.0 copy-start
  0.7 0.9 dynamic-slice_bitcast_fusion
  1.6 3.3 %collective-permute-start.2 = (bf16[16,2048]{1,0:T(8,128)(2,1)S(1)}, bf16[16,2048]{1,0:T(8,128)(2,1)S(1)}, u32[]{:S(2)}, u32[]{:S(2)}) collective-permute-start(bf16[16,2048]{1,0:T(8,128)(2,1)S(1)} %dynamic-slice_bitcast_fusion), channel_id=1, source_target_pairs={{0,24},{2,26},{4,28},{6,30},{8,0},{10,2},{12,4},{14,6},{16,8},{18,... | collective-permute-start | bytes 196616 | tf_op jit(solution)/shard_map/ppermute | solution.py:442
  4.9 0.5 collective-permute-start.1
  5.4 0.6 collective-permute-start
  6.0 0.6 pad_add_fusion.core_ref.place_ref
  6.7 6.2 %dispatch_rows.1 = (bf16[1024,2048]{1,0:T(8,128)(2,1)}, bf16[512,2048]{1,0:T(8,128)(2,1)}) custom-call(s32[4]{0:T(128)} %pad_add_fusion.core_ref.place_ref, s32[8,128]{1,0:T(8,128)} %bitcast.21, bf16[128,4096]{1,0:T(8,128)(2,1)} %rows_ref.1), custom_call_target="tpu_custom_call" | custom-call | flops 805306368 | bytes 6291456 | tf_op jit(solution)/shard_map/dispatch_rows/pallas_call | solution.py:93
  12.9 59.9 %all_to_all.20 = bf16[64,16,2048]{2,1,0:T(8,128)(2,1)} all-to-all(bf16[64,16,2048]{2,1,0:T(8,128)(2,1)} %bitcast.18), channel_id=1, replica_groups=mesh['wide'=64,'narrow'=2] {'wide'}, dimensions={0} | all-to-all | bytes 8388608 | tf_op jit(solution)/shard_map/all_to_all | solution.py:446
  72.8 3.7 %collective-permute-start.3 = (bf16[1024,2048]{1,0:T(8,128)(2,1)}, bf16[1024,2048]{1,0:T(8,128)(2,1)}, u32[]{:S(2)}, u32[]{:S(2)}) collective-permute-start(bf16[1024,2048]{1,0:T(8,128)(2,1)} %bitcast.9.own_ref), channel_id=1, source_target_pairs={{0,1},{1,0},{2,3},{3,2},{4,5},{5,4},{6,7},{7,6},{8,9},{9,8},{10,11... | collective-permute-start | bytes 12582920 | tf_op jit(solution)/shard_map/ppermute | solution.py:432
  76.5 5.7 %all-to-all-start = ((bf16[64,8,2048]{2,1,0:T(8,128)(2,1)}), bf16[64,8,2048]{2,1,0:T(8,128)(2,1)}, u32[]{:S(2)}, u32[]{:S(2)}) async-start(bf16[64,8,2048]{2,1,0:T(8,128)(2,1)} %bitcast.19), calls=%async_computation | async-start | bytes 4194304 | tf_op jit(solution)/shard_map/all_to_all | solution.py:446
  82.5 1.0 collective-permute-start.4
  83.5 1.7 collective-permute-start.5
  85.2 20.5 %experts_forward.2 = (bf16[1024,768]{1,0:T(8,128)(2,1)S(1)}, bf16[4,16,256]{2,1,0:T(8,128)(2,1)S(1)}) custom-call(s32[4]{0:T(128)S(1)} %copy-done.17, bf16[1024,2048]{1,0:T(8,128)(2,1)} %bitcast.9.own_ref, bf16[1024,2048]{1,0:T(8,128)(2,1)} %collective-permute-done.3.other_ref, bf16[1,4096,768]{2,1,0:T(8,128)(2,1)} %gx_ref.3, bf16[1,4096,768]{2,1,0:T(8,128)(2,1)} %gx_ref.3, ...), custom_call_target="tpu_custom_call" | custom-call | flops 12884901888 | bytes 20971520 | tf_op jit(solution)/shard_map/experts_forward/pallas_call | solution.py:173
  105.8 1.2 copy-done.1
  106.9 0.6 copy-done.13
  107.5 6.8 %collective-permute-done.4.refs_5_ = bf16[64,2048]{1,0:T(8,128)(2,1)S(1)} collective-permute-done((bf16[64,2048]{1,0:T(8,128)(2,1)S(1)}, bf16[64,2048]{1,0:T(8,128)(2,1)S(1)}, u32[]{:S(2)}, u32[]{:S(2)}) %collective-permute-start.4) | collective-permute-done | bytes 262176 | tf_op jit(solution)/shard_map/ppermute | solution.py:442
  114.4 0.7 copy-done.8
  115.1 0.7 copy-done.10
  115.8 0.4 collective-permute-start.6
  116.2 0.9 collective-permute-start.8
  117.1 2.4 %collective-permute-start.9 = (bf16[136,2048]{1,0:T(8,128)(2,1)S(1)}, bf16[136,2048]{1,0:T(8,128)(2,1)S(1)}, u32[]{:S(2)}, u32[]{:S(2)}) collective-permute-start(bf16[136,2048]{1,0:T(8,128)(2,1)S(1)} %fusion.1.refs_0_.refs_4_), channel_id=1, source_target_pairs={{0,4},{2,6},{4,0},{6,2},{8,12},{10,14},{12,8},{14,10},{16,20},{18,... | collective-permute-start | bytes 1671176 | tf_op jit(solution)/shard_map/ppermute | solution.py:442
  119.5 1.1 collective-permute-start.10
  120.7 0.8 copy-done.14
  121.4 0.7 copy-done.16
  122.2 11.6 %experts_forward.3 = (bf16[512,768]{1,0:T(8,128)(2,1)S(1)}, bf16[16,16,128]{2,1,0:T(8,128)(2,1)S(1)}) custom-call(s32[4]{0:T(128)S(1)} %copy-done.17, bf16[512,2048]{1,0:T(8,128)(2,1)} %bitcast.6.own_ref, bf16[512,2048]{1,0:T(8,128)(2,1)S(1)} %collective-permute-done.6.other_ref, bf16[1,4096,768]{2,1,0:T(8,128)(2,1)} %gx_ref.3, ...), custom_call_target="tpu_custom_call" | custom-call | flops 6442450944 | bytes 16777216 | tf_op jit(solution)/shard_map/experts_forward/pallas_call | solution.py:173
  133.9 10.1 %collective-permute-done.9.refs_2_.refs_6_ = bf16[136,2048]{1,0:T(8,128)(2,1)S(1)} collective-permute-done((bf16[136,2048]{1,0:T(8,128)(2,1)S(1)}, bf16[136,2048]{1,0:T(8,128)(2,1)S(1)}, u32[]{:S(2)}, u32[]{:S(2)}) %collective-permute-start.9) | collective-permute-done | bytes 557088 | tf_op jit(solution)/shard_map/ppermute | solution.py:442
  144.0 2.3 %project_readout.1.own_ref = f32[512,256]{1,0:T(8,128)} custom-call(bf16[136,2048]{1,0:T(8,128)(2,1)S(1)} %fusion.1.refs_0_.refs_4_, bf16[136,2048]{1,0:T(8,128)(2,1)S(1)} %collective-permute-done.8.refs_1_.refs_5_, bf16[136,2048]{1,0:T(8,128)(2,1)S(1)} %collective-permute-done.9.refs_2_.refs_6_, ...), custom_call_target="tpu_custom_call" | custom-call | flops 536870912 | bytes 3145728 | tf_op jit(solution)/shard_map/project_readout/pallas_call | solution.py:209
  146.2 1.1 collective-permute-start.11
  147.3 6.4 %all-to-all-start.2 = ((bf16[16,16,128]{2,1,0:T(8,128)(2,1)}), bf16[16,16,128]{2,1,0:T(8,128)(2,1)S(1)}, u32[]{:S(2)}, u32[]{:S(2)}) async-start(bf16[16,16,128]{2,1,0:T(8,128)(2,1)} %copy-done.12), calls=%async_computation.2 | async-start | bytes 131072 | tf_op jit(solution)/shard_map/all_to_all | solution.py:446
  153.8 4.9 %pick_projections.1 = (f32[192,128]{1,0:T(8,128)S(1)}, bf16[1536,128]{1,0:T(8,128)(2,1)S(1)}) custom-call(s32[4]{0:T(128)S(1)} %copy-done.17, f32[512,256]{1,0:T(8,128)} %project_readout.1.own_ref, f32[512,256]{1,0:T(8,128)} %collective-permute-done.11.other_ref, bf16[136,2048]{1,0:T(8,128)(2,1)S(1)} %fusion.1.refs_0_.refs_4_, ...), custom_call_target="tpu_custom_call" | custom-call | tf_op jit(solution)/shard_map/pick_projections/pallas_call | solution.py:263
  158.7 0.8 copy-done.3
  159.5 0.8 all-to-all-done.2.own_ref
  160.3 1.4 collective-permute-start.12
  161.7 0.9 collective-permute-done.12.other_ref
  162.6 1.0 copy-done.4
  163.6 0.8 rate_tokens.1
  164.4 1.3 collective-permute-start.13
  165.8 2.2 %collective-permute-start.14 = (f32[8,128]{1,0:T(8,128)S(1)}, f32[8,128]{1,0:T(8,128)S(1)}, u32[]{:S(2)}, u32[]{:S(2)}) collective-permute-start(f32[8,128]{1,0:T(8,128)S(1)} %get-tuple-element.53.refs_0_), channel_id=1, source_target_pairs={{0,4},{2,6},{4,0},{6,2},{8,12},{10,14},{12,8},{14,10},{16,20},{18,... | collective-permute-start | bytes 12296 | tf_op jit(solution)/shard_map/ppermute | solution.py:442
  168.0 1.2 collective-permute-start.15
  169.2 0.5 collective-permute-done.14.refs_2_
  169.7 1.0 collective-permute-done.15.refs_3_
  170.7 1.0 copy-done.5
  171.7 4.1 %weigh_tokens.1 = (f32[1,128]{1,0:T(1,128)}, bf16[16,16,2176]{2,1,0:T(8,128)(2,1)S(1)}) custom-call(f32[8,128]{1,0:T(8,128)S(1)} %get-tuple-element.53.refs_0_, f32[8,128]{1,0:T(8,128)S(1)} %collective-permute-done.13.refs_1_, f32[8,128]{1,0:T(8,128)S(1)} %collective-permute-done.14.refs_2_, f32[8,128]{1,0:T(8,128)S(1)} %collective-permute-done.15.refs_3_, ...), custom_call_target="tpu_custom_call" | custom-call | tf_op jit(solution)/shard_map/weigh_tokens/pallas_call | solution.py:367
  175.8 20.9 %all_to_all.21.packed_ref = bf16[16,16,2176]{2,1,0:T(8,128)(2,1)S(1)} all-to-all(bf16[16,16,2176]{2,1,0:T(8,128)(2,1)S(1)} %get-tuple-element.56), channel_id=1, replica_groups={{0,8,16,24,32,40,48,56,64,72,80,88,96,104,112,120},{2,10,18,26,34,42,50..., dimensions={0} | all-to-all | bytes 2228224 | tf_op jit(solution)/shard_map/all_to_all | solution.py:446
  196.7 2.8 %adapter_gradients.1 = (f32[16,768]{1,0:T(8,128)}, f32[16,2048]{1,0:T(8,128)S(1)}) custom-call(s32[4]{0:T(128)S(1)} %copy-done.17, bf16[16,16,2176]{2,1,0:T(8,128)(2,1)S(1)} %all_to_all.21.packed_ref, bf16[1024,768]{1,0:T(8,128)(2,1)S(1)} %copy-done.2, bf16[512,768]{1,0:T(8,128)(2,1)S(1)} %copy-done.7), custom_call_target="tpu_custom_call" | custom-call | tf_op jit(solution)/shard_map/adapter_gradients/pallas_call | solution.py:417
  199.5 2.9 %collective-permute-start.16 = (f32[16,2048]{1,0:T(8,128)S(1)}, f32[16,2048]{1,0:T(8,128)S(1)}, u32[]{:S(2)}, u32[]{:S(2)}) collective-permute-start(f32[16,2048]{1,0:T(8,128)S(1)} %get-tuple-element.60), channel_id=1, source_target_pairs={{0,1},{1,0},{2,3},{3,2},{4,5},{5,4},{6,7},{7,6},{8,9},{9,8},{10,11... | collective-permute-start | bytes 393224 | tf_op jit(solution)/shard_map/ppermute | solution.py:432
  202.4 1.0 collective-permute-done.16
  203.3 0.7 maximum_select_fusion
  (52 shorter events, 0.2 us)
Async XLA Ops:
  0.6 81.7 %copy-start = (bf16[128,4096]{1,0:T(8,128)(2,1)S(1)}, bf16[128,4096]{1,0:T(8,128)(2,1)}, u32[]{:S(2)}) copy-start(bf16[128,4096]{1,0:T(8,128)(2,1)} %param.10) | copy-start | bytes 3145732
  1.6 11.3 %collective-permute-start.2 = (bf16[16,2048]{1,0:T(8,128)(2,1)S(1)}, bf16[16,2048]{1,0:T(8,128)(2,1)S(1)}, u32[]{:S(2)}, u32[]{:S(2)}) collective-permute-start(bf16[16,2048]{1,0:T(8,128)(2,1)S(1)} %dynamic-slice_bitcast_fusion), channel_id=1, source_target_pairs={{0,24},{2,26},{4,28},{6,30},{8,0},{10,2},{12,4},{14,6},{16,8},{18,... | collective-permute-start | bytes 196616 | tf_op jit(solution)/shard_map/ppermute | solution.py:442
  4.9 8.0 %collective-permute-start.1 = (bf16[16,2048]{1,0:T(8,128)(2,1)S(1)}, bf16[16,2048]{1,0:T(8,128)(2,1)S(1)}, u32[]{:S(2)}, u32[]{:S(2)}) collective-permute-start(bf16[16,2048]{1,0:T(8,128)(2,1)S(1)} %dynamic-slice_bitcast_fusion), channel_id=1, source_target_pairs={{0,16},{2,18},{4,20},{6,22},{8,24},{10,26},{12,28},{14,30},{16,0},... | collective-permute-start | bytes 196616 | tf_op jit(solution)/shard_map/ppermute | solution.py:442
  5.4 7.5 %collective-permute-start = (bf16[16,2048]{1,0:T(8,128)(2,1)S(1)}, bf16[16,2048]{1,0:T(8,128)(2,1)S(1)}, u32[]{:S(2)}, u32[]{:S(2)}) collective-permute-start(bf16[16,2048]{1,0:T(8,128)(2,1)S(1)} %dynamic-slice_bitcast_fusion), channel_id=1, source_target_pairs={{0,8},{2,10},{4,12},{6,14},{8,16},{10,18},{12,20},{14,22},{16,24},... | collective-permute-start | bytes 196616 | tf_op jit(solution)/shard_map/ppermute | solution.py:442
  72.8 12.4 %collective-permute-start.3 = (bf16[1024,2048]{1,0:T(8,128)(2,1)}, bf16[1024,2048]{1,0:T(8,128)(2,1)}, u32[]{:S(2)}, u32[]{:S(2)}) collective-permute-start(bf16[1024,2048]{1,0:T(8,128)(2,1)} %bitcast.9.own_ref), channel_id=1, source_target_pairs={{0,1},{1,0},{2,3},{3,2},{4,5},{5,4},{6,7},{7,6},{8,9},{9,8},{10,11... | collective-permute-start | bytes 12582920 | tf_op jit(solution)/shard_map/ppermute | solution.py:432
  76.5 5.7 %copy-start.20 = (s32[128]{0:T(128)S(1)}, s32[128]{0:T(128)}, u32[]{:S(2)}) copy-start(s32[128]{0:T(128)} %param.13) | copy-start | bytes 1540
  76.5 5.8 %copy-start.18 = (s32[128,8]{0,1:T(8,128)S(1)}, s32[128,8]{0,1:T(8,128)}, u32[]{:S(2)}) copy-start(s32[128,8]{0,1:T(8,128)} %param.11) | copy-start | bytes 12292
  76.5 5.8 %copy-start.19 = (bf16[128,8]{0,1:T(8,128)(2,1)S(1)}, bf16[128,8]{0,1:T(8,128)(2,1)}, u32[]{:S(2)}) copy-start(bf16[128,8]{0,1:T(8,128)(2,1)} %param.12) | copy-start | bytes 6148
  76.5 39.2 %all-to-all-start = ((bf16[64,8,2048]{2,1,0:T(8,128)(2,1)}), bf16[64,8,2048]{2,1,0:T(8,128)(2,1)}, u32[]{:S(2)}, u32[]{:S(2)}) async-start(bf16[64,8,2048]{2,1,0:T(8,128)(2,1)} %bitcast.19), calls=%async_computation | async-start | bytes 4194304 | tf_op jit(solution)/shard_map/all_to_all | solution.py:446
  82.3 3.0 %copy-start.15 = (bf16[1,16,768]{2,1,0:T(8,128)(2,1)S(1)}, bf16[1,16,768]{2,1,0:T(8,128)(2,1)}, u32[]{:S(2)}) copy-start(bf16[1,16,768]{2,1,0:T(8,128)(2,1)} %a_ref.3) | copy-start | bytes 73732
  82.3 2.9 %copy-start.17 = (s32[4]{0:T(128)S(1)}, s32[4]{0:T(128)}, u32[]{:S(2)}) copy-start(s32[4]{0:T(128)} %pad_add_fusion.core_ref.place_ref) | copy-start | bytes 52
  82.5 31.9 %collective-permute-start.4 = (bf16[64,2048]{1,0:T(8,128)(2,1)S(1)}, bf16[64,2048]{1,0:T(8,128)(2,1)S(1)}, u32[]{:S(2)}, u32[]{:S(2)}) collective-permute-start(bf16[64,2048]{1,0:T(8,128)(2,1)S(1)} %pad_maximum_fusion.refs_4_), channel_id=1, source_target_pairs={{0,32},{2,34},{4,36},{6,38},{8,40},{10,42},{12,44},{14,46},{16,48}... | collective-permute-start | bytes 786440 | tf_op jit(solution)/shard_map/ppermute | solution.py:442
  83.5 31.6 %collective-permute-start.5 = (bf16[64,2048]{1,0:T(8,128)(2,1)S(1)}, bf16[64,2048]{1,0:T(8,128)(2,1)S(1)}, u32[]{:S(2)}, u32[]{:S(2)}) collective-permute-start(bf16[64,2048]{1,0:T(8,128)(2,1)S(1)} %pad_maximum_fusion.refs_4_), channel_id=1, source_target_pairs={{0,96},{2,98},{4,100},{6,102},{8,104},{10,106},{12,108},{14,110},{... | collective-permute-start | bytes 786440 | tf_op jit(solution)/shard_map/ppermute | solution.py:442
  105.8 1.2 copy-start.1
  106.9 0.6 copy-start.13
  114.3 0.7 copy-start.8
  115.1 0.7 copy-start.10
  115.8 4.9 %collective-permute-start.6 = (bf16[512,2048]{1,0:T(8,128)(2,1)}, bf16[512,2048]{1,0:T(8,128)(2,1)S(1)}, u32[]{:S(2)}, u32[]{:S(2)}) collective-permute-start(bf16[512,2048]{1,0:T(8,128)(2,1)} %bitcast.6.own_ref), channel_id=1, source_target_pairs={{0,1},{1,0},{2,3},{3,2},{4,5},{5,4},{6,7},{7,6},{8,9},{9,8},{10,11... | collective-permute-start | bytes 6291464 | tf_op jit(solution)/shard_map/ppermute | solution.py:432
  116.2 17.6 %collective-permute-start.7 = (bf16[64,2048]{1,0:T(8,128)(2,1)S(1)}, bf16[64,2048]{1,0:T(8,128)(2,1)S(1)}, u32[]{:S(2)}, u32[]{:S(2)}) collective-permute-start(bf16[64,2048]{1,0:T(8,128)(2,1)S(1)} %pad_maximum_fusion.refs_4_), channel_id=1, source_target_pairs={{0,64},{2,66},{4,68},{6,70},{8,72},{10,74},{12,76},{14,78},{16,80}... | collective-permute-start | bytes 786440 | tf_op jit(solution)/shard_map/ppermute | solution.py:442
  116.2 17.6 %collective-permute-start.8 = (bf16[136,2048]{1,0:T(8,128)(2,1)S(1)}, bf16[136,2048]{1,0:T(8,128)(2,1)S(1)}, u32[]{:S(2)}, u32[]{:S(2)}) collective-permute-start(bf16[136,2048]{1,0:T(8,128)(2,1)S(1)} %fusion.1.refs_0_.refs_4_), channel_id=1, source_target_pairs={{0,2},{2,4},{4,6},{6,0},{8,10},{10,12},{12,14},{14,8},{16,18},{18,... | collective-permute-start | bytes 1671176 | tf_op jit(solution)/shard_map/ppermute | solution.py:442
  117.1 26.8 %collective-permute-start.9 = (bf16[136,2048]{1,0:T(8,128)(2,1)S(1)}, bf16[136,2048]{1,0:T(8,128)(2,1)S(1)}, u32[]{:S(2)}, u32[]{:S(2)}) collective-permute-start(bf16[136,2048]{1,0:T(8,128)(2,1)S(1)} %fusion.1.refs_0_.refs_4_), channel_id=1, source_target_pairs={{0,4},{2,6},{4,0},{6,2},{8,12},{10,14},{12,8},{14,10},{16,20},{18,... | collective-permute-start | bytes 1671176 | tf_op jit(solution)/shard_map/ppermute | solution.py:442
  119.5 24.4 %collective-permute-start.10 = (bf16[136,2048]{1,0:T(8,128)(2,1)S(1)}, bf16[136,2048]{1,0:T(8,128)(2,1)S(1)}, u32[]{:S(2)}, u32[]{:S(2)}) collective-permute-start(bf16[136,2048]{1,0:T(8,128)(2,1)S(1)} %fusion.1.refs_0_.refs_4_), channel_id=1, source_target_pairs={{0,6},{2,0},{4,2},{6,4},{8,14},{10,8},{12,10},{14,12},{16,22},{18,... | collective-permute-start | bytes 1671176 | tf_op jit(solution)/shard_map/ppermute | solution.py:442
  120.7 0.8 copy-start.14
  121.4 0.7 copy-start.16
  122.2 21.8 %copy-start.9 = (bf16[64,2048]{1,0:T(8,128)(2,1)S(1)}, bf16[64,2048]{1,0:T(8,128)(2,1)}, u32[]{:S(2)}) copy-start(bf16[64,2048]{1,0:T(8,128)(2,1)} %copy-done.8) | copy-start | bytes 786436
  122.2 21.8 %copy-start.11 = (bf16[64,2048]{1,0:T(8,128)(2,1)S(1)}, bf16[64,2048]{1,0:T(8,128)(2,1)}, u32[]{:S(2)}) copy-start(bf16[64,2048]{1,0:T(8,128)(2,1)} %copy-done.10) | copy-start | bytes 786436
  133.8 12.4 %copy-start.6 = (bf16[512,768]{1,0:T(8,128)(2,1)}, bf16[512,768]{1,0:T(8,128)(2,1)S(1)}, u32[]{:S(2)}) copy-start(bf16[512,768]{1,0:T(8,128)(2,1)S(1)} %get-tuple-element.58.refs_1_) | copy-start | bytes 2359300
  133.8 13.5 %copy-start.12 = (bf16[16,16,128]{2,1,0:T(8,128)(2,1)}, bf16[16,16,128]{2,1,0:T(8,128)(2,1)S(1)}, u32[]{:S(2)}) copy-start(bf16[16,16,128]{2,1,0:T(8,128)(2,1)S(1)} %get-tuple-element.39) | copy-start | bytes 196612
  146.2 7.5 %collective-permute-start.11 = (f32[512,256]{1,0:T(8,128)}, f32[512,256]{1,0:T(8,128)}, u32[]{:S(2)}, u32[]{:S(2)}) collective-permute-start(f32[512,256]{1,0:T(8,128)} %project_readout.1.own_ref), channel_id=1, source_target_pairs={{0,1},{1,0},{2,3},{3,2},{4,5},{5,4},{6,7},{7,6},{8,9},{9,8},{10,11... | collective-permute-start | bytes 1572872 | tf_op jit(solution)/shard_map/ppermute | solution.py:432
  147.3 13.0 %all-to-all-start.2 = ((bf16[16,16,128]{2,1,0:T(8,128)(2,1)}), bf16[16,16,128]{2,1,0:T(8,128)(2,1)S(1)}, u32[]{:S(2)}, u32[]{:S(2)}) async-start(bf16[16,16,128]{2,1,0:T(8,128)(2,1)} %copy-done.12), calls=%async_computation.2 | async-start | bytes 131072 | tf_op jit(solution)/shard_map/all_to_all | solution.py:446
  158.7 0.8 copy-start.3
  160.3 2.3 %collective-permute-start.12 = (bf16[16,16,128]{2,1,0:T(8,128)(2,1)S(1)}, bf16[16,16,128]{2,1,0:T(8,128)(2,1)S(1)}, u32[]{:S(2)}, u32[]{:S(2)}) collective-permute-start(bf16[16,16,128]{2,1,0:T(8,128)(2,1)S(1)} %all-to-all-done.2.own_ref), channel_id=1, source_target_pairs={{0,1},{1,0},{2,3},{3,2},{4,5},{5,4},{6,7},{7,6},{8,9},{9,8},{10,11... | collective-permute-start | bytes 196616 | tf_op jit(solution)/shard_map/ppermute | solution.py:432
  162.6 1.0 copy-start.4
  164.4 4.8 %collective-permute-start.13 = (f32[8,128]{1,0:T(8,128)S(1)}, f32[8,128]{1,0:T(8,128)S(1)}, u32[]{:S(2)}, u32[]{:S(2)}) collective-permute-start(f32[8,128]{1,0:T(8,128)S(1)} %get-tuple-element.53.refs_0_), channel_id=1, source_target_pairs={{0,2},{2,4},{4,6},{6,0},{8,10},{10,12},{12,14},{14,8},{16,18},{18,... | collective-permute-start | bytes 12296 | tf_op jit(solution)/shard_map/ppermute | solution.py:442
  165.8 4.0 %collective-permute-start.14 = (f32[8,128]{1,0:T(8,128)S(1)}, f32[8,128]{1,0:T(8,128)S(1)}, u32[]{:S(2)}, u32[]{:S(2)}) collective-permute-start(f32[8,128]{1,0:T(8,128)S(1)} %get-tuple-element.53.refs_0_), channel_id=1, source_target_pairs={{0,4},{2,6},{4,0},{6,2},{8,12},{10,14},{12,8},{14,10},{16,20},{18,... | collective-permute-start | bytes 12296 | tf_op jit(solution)/shard_map/ppermute | solution.py:442
  168.0 2.8 %collective-permute-start.15 = (f32[8,128]{1,0:T(8,128)S(1)}, f32[8,128]{1,0:T(8,128)S(1)}, u32[]{:S(2)}, u32[]{:S(2)}) collective-permute-start(f32[8,128]{1,0:T(8,128)S(1)} %get-tuple-element.53.refs_0_), channel_id=1, source_target_pairs={{0,6},{2,0},{4,2},{6,4},{8,14},{10,8},{12,10},{14,12},{16,22},{18,... | collective-permute-start | bytes 12296 | tf_op jit(solution)/shard_map/ppermute | solution.py:442
  170.7 1.0 copy-start.5
  171.7 24.9 %copy-start.2 = (bf16[1024,768]{1,0:T(8,128)(2,1)S(1)}, bf16[1024,768]{1,0:T(8,128)(2,1)}, u32[]{:S(2)}) copy-start(bf16[1024,768]{1,0:T(8,128)(2,1)} %copy-done.1) | copy-start | bytes 4718596
  171.7 24.9 %copy-start.7 = (bf16[512,768]{1,0:T(8,128)(2,1)S(1)}, bf16[512,768]{1,0:T(8,128)(2,1)}, u32[]{:S(2)}) copy-start(bf16[512,768]{1,0:T(8,128)(2,1)} %copy-done.6) | copy-start | bytes 2359300
  199.5 3.9 %collective-permute-start.16 = (f32[16,2048]{1,0:T(8,128)S(1)}, f32[16,2048]{1,0:T(8,128)S(1)}, u32[]{:S(2)}, u32[]{:S(2)}) collective-permute-start(f32[16,2048]{1,0:T(8,128)S(1)} %get-tuple-element.60), channel_id=1, source_target_pairs={{0,1},{1,0},{2,3},{3,2},{4,5},{5,4},{6,7},{7,6},{8,9},{9,8},{10,11... | collective-permute-start | bytes 393224 | tf_op jit(solution)/shard_map/ppermute | solution.py:432

commit v7 on v6

--- a/solution.py
+++ b/solution.py
@@ -497,11 +497,12 @@
     last_acts, latents = experts_forward(
         place, y, swap(y), gate_proj, up_proj, adapter_a, [sums], groups, True
     )
-    last_acts, adapters[2], readouts = lax.optimization_barrier((last_acts, adapters[2], readouts))
+    latents, adapters[2], readouts = lax.optimization_barrier(
+        (exchange(latents, planes), adapters[2], readouts)
+    )
     hidden = [acts, last_acts]
     projections = project(readouts, adapters, tokens)
     picked, gains = pick(place, projections, swap(projections), readouts, tokens, chunks)
-    latents, picked = lax.optimization_barrier((exchange(latents, planes), picked))
     log_part, latents = rate(latents, swap(latents), picked, gains, chunks)
     logs = [moved(log_part, groups, 1, step) for step in range(LINE)]
     log_ratio, packed = weigh(logs, readouts, latents, picked, gains, rank, tokens, chunks)

time: 205 us -> 198 us (0.966)
  waiting for transfers between devices: 21.2 us -> 17.7 us
    ppermute x12, waiting for transfers between devices: 18.4 us -> 10.6 us  [moved(): return lax.ppermute(payload, 'wide', moves)]
    all_to_all x2, waiting for transfers between devices: 0.84 us -> 4.71 us  [exchange(): lax.all_to_all(payload, 'wide', split_axis=0, concat_axis=0, tiled=True,...]
    unnamed x42 -> x36, local copies, waits for them, and re-layouts: 7.5 us -> 8.14 us
  transfers between devices with their start and end apart: 19 -> 19, of which waited for: 7 -> 8; matrix products, arithmetic and copies ran while one was open for 0% -> 0% of each run, Pallas kernels for 21% -> 21%
where the time goes in v7:
time: 198 us
  blocking collectives  78.9 us (40%)
  Pallas kernels  53 us (27%)
  starting transfers between devices  36.5 us (18%)
  waiting for transfers between devices  17.7 us (9%)
  local copies, waits for them, and re-layouts  9.12 us (5%)
    all_to_all x2, blocking collectives, exchange(): lax.all_to_all(payload, 'wide', split_axis=0, concat_axis=0, tiled=True,...  78.9 us
    pallas_call x2, Pallas kernels, experts_forward(): pl.pallas_call(functools.partial(experts_body, groups, count, steps, last...  32.2 us
    ppermute x12, starting transfers between devices, moved(): return lax.ppermute(payload, 'wide', moves)  14.4 us
    all_to_all x2, starting transfers between devices, exchange(): lax.all_to_all(payload, 'wide', split_axis=0, concat_axis=0, tiled=True,...  12.4 us
    ppermute x12, waiting for transfers between devices, moved(): return lax.ppermute(payload, 'wide', moves)  10.6 us
    ppermute x5, starting transfers between devices, swap(): return lax.ppermute(payload, 'narrow', [(0, 1), (1, 0)])  9.73 us
    unnamed x36, local copies, waits for them, and re-layouts  8.14 us
    pallas_call x1, Pallas kernels, dispatch(): pl.pallas_call(functools.partial(dispatch_body, experts), grid_spec=pltpu...  6.24 us
  transfers between devices with their start and end apart: 19, of which 8 were waited for; matrix products, arithmetic and copies ran while one was open for 0% of the time, Pallas kernels for 21%

profile of v7, /device:TPU:1, one launch (start us, length us, event | category | flops | bytes accessed | tf_op | source)
XLA Modules:
  0.0 197.6 jit_solution(3476026554667755730)
XLA Ops:
  0.7 0.9 dynamic-slice_bitcast_fusion
  1.6 3.3 %collective-permute-start.2 = (bf16[16,2048]{1,0:T(8,128)(2,1)S(1)}, bf16[16,2048]{1,0:T(8,128)(2,1)S(1)}, u32[]{:S(2)}, u32[]{:S(2)}) collective-permute-start(bf16[16,2048]{1,0:T(8,128)(2,1)S(1)} %dynamic-slice_bitcast_fusion), channel_id=1, source_target_pairs={{0,24},{2,26},{4,28},{6,30},{8,0},{10,2},{12,4},{14,6},{16,8},{18,... | collective-permute-start | bytes 196616 | tf_op jit(solution)/shard_map/ppermute | solution.py:442
  4.9 0.5 collective-permute-start.1
  5.4 0.6 collective-permute-start
  6.0 0.7 pad_add_fusion.core_ref.place_ref
  6.7 6.2 %dispatch_rows.1 = (bf16[1024,2048]{1,0:T(8,128)(2,1)}, bf16[512,2048]{1,0:T(8,128)(2,1)}) custom-call(s32[4]{0:T(128)} %pad_add_fusion.core_ref.place_ref, s32[8,128]{1,0:T(8,128)} %bitcast.21, bf16[128,4096]{1,0:T(8,128)(2,1)} %rows_ref.1), custom_call_target="tpu_custom_call" | custom-call | flops 805306368 | bytes 6291456 | tf_op jit(solution)/shard_map/dispatch_rows/pallas_call | solution.py:93
  13.0 59.9 %all_to_all.20 = bf16[64,16,2048]{2,1,0:T(8,128)(2,1)} all-to-all(bf16[64,16,2048]{2,1,0:T(8,128)(2,1)} %bitcast.18), channel_id=1, replica_groups=mesh['wide'=64,'narrow'=2] {'wide'}, dimensions={0} | all-to-all | bytes 8388608 | tf_op jit(solution)/shard_map/all_to_all | solution.py:446
  72.9 3.7 %collective-permute-start.3 = (bf16[1024,2048]{1,0:T(8,128)(2,1)}, bf16[1024,2048]{1,0:T(8,128)(2,1)}, u32[]{:S(2)}, u32[]{:S(2)}) collective-permute-start(bf16[1024,2048]{1,0:T(8,128)(2,1)} %bitcast.9.own_ref), channel_id=1, source_target_pairs={{0,1},{1,0},{2,3},{3,2},{4,5},{5,4},{6,7},{7,6},{8,9},{9,8},{10,11... | collective-permute-start | bytes 12582920 | tf_op jit(solution)/shard_map/ppermute | solution.py:432
  76.6 5.7 %all-to-all-start = ((bf16[64,8,2048]{2,1,0:T(8,128)(2,1)}), bf16[64,8,2048]{2,1,0:T(8,128)(2,1)}, u32[]{:S(2)}, u32[]{:S(2)}) async-start(bf16[64,8,2048]{2,1,0:T(8,128)(2,1)} %bitcast.19), calls=%async_computation | async-start | bytes 4194304 | tf_op jit(solution)/shard_map/all_to_all | solution.py:446
  82.5 1.0 collective-permute-start.4
  83.5 1.7 collective-permute-start.5
  85.3 20.5 %experts_forward.2 = (bf16[1024,768]{1,0:T(8,128)(2,1)S(1)}, bf16[4,16,256]{2,1,0:T(8,128)(2,1)S(1)}) custom-call(s32[4]{0:T(128)S(1)} %copy-done.14, bf16[1024,2048]{1,0:T(8,128)(2,1)} %bitcast.9.own_ref, bf16[1024,2048]{1,0:T(8,128)(2,1)} %collective-permute-done.3.other_ref, bf16[1,4096,768]{2,1,0:T(8,128)(2,1)} %gx_ref.3, bf16[1,4096,768]{2,1,0:T(8,128)(2,1)} %gx_ref.3, ...), custom_call_target="tpu_custom_call" | custom-call | flops 12884901888 | bytes 20971520 | tf_op jit(solution)/shard_map/experts_forward/pallas_call | solution.py:173
  105.8 1.2 copy-done.1
  107.0 0.6 copy-done.10
  107.6 6.8 %collective-permute-done.4.refs_5_ = bf16[64,2048]{1,0:T(8,128)(2,1)S(1)} collective-permute-done((bf16[64,2048]{1,0:T(8,128)(2,1)S(1)}, bf16[64,2048]{1,0:T(8,128)(2,1)S(1)}, u32[]{:S(2)}, u32[]{:S(2)}) %collective-permute-start.4) | collective-permute-done | bytes 262176 | tf_op jit(solution)/shard_map/ppermute | solution.py:442
  114.4 0.7 copy-done.5
  115.1 0.7 copy-done.7
  115.8 0.4 collective-permute-start.6
  116.3 0.9 collective-permute-start.8
  117.2 2.4 %collective-permute-start.9 = (bf16[136,2048]{1,0:T(8,128)(2,1)S(1)}, bf16[136,2048]{1,0:T(8,128)(2,1)S(1)}, u32[]{:S(2)}, u32[]{:S(2)}) collective-permute-start(bf16[136,2048]{1,0:T(8,128)(2,1)S(1)} %fusion.1.refs_0_.refs_4_), channel_id=1, source_target_pairs={{0,4},{2,6},{4,0},{6,2},{8,12},{10,14},{12,8},{14,10},{16,20},{18,... | collective-permute-start | bytes 1671176 | tf_op jit(solution)/shard_map/ppermute | solution.py:442
  119.6 1.1 collective-permute-start.10
  120.7 0.8 copy-done.11
  121.5 0.7 copy-done.13
  122.2 11.6 %experts_forward.3 = (bf16[512,768]{1,0:T(8,128)(2,1)S(1)}, bf16[16,16,128]{2,1,0:T(8,128)(2,1)S(1)}) custom-call(s32[4]{0:T(128)S(1)} %copy-done.14, bf16[512,2048]{1,0:T(8,128)(2,1)} %bitcast.6.own_ref, bf16[512,2048]{1,0:T(8,128)(2,1)S(1)} %collective-permute-done.6.other_ref, bf16[1,4096,768]{2,1,0:T(8,128)(2,1)} %gx_ref.3, ...), custom_call_target="tpu_custom_call" | custom-call | flops 6442450944 | bytes 16777216 | tf_op jit(solution)/shard_map/experts_forward/pallas_call | solution.py:173
  133.9 0.9 copy-done.3
  134.8 0.6 copy-done.9
  135.4 6.7 %all-to-all-start.2 = ((bf16[16,16,128]{2,1,0:T(8,128)(2,1)}), bf16[16,16,128]{2,1,0:T(8,128)(2,1)}, u32[]{:S(2)}, u32[]{:S(2)}) async-start(bf16[16,16,128]{2,1,0:T(8,128)(2,1)} %copy-done.9), calls=%async_computation.2 | async-start | bytes 131072 | tf_op jit(solution)/shard_map/all_to_all | solution.py:446
  142.2 1.8 collective-permute-done.9.refs_2_.refs_6_
  144.0 4.7 %all-to-all-done.2.own_ref = bf16[16,16,128]{2,1,0:T(8,128)(2,1)} async-done(((bf16[16,16,128]{2,1,0:T(8,128)(2,1)}), bf16[16,16,128]{2,1,0:T(8,128)(2,1)}, u32[]{:S(2)}, u32[]{:S(2)}) %all-to-all-start.2) | async-done | bytes 65568 | tf_op jit(solution)/shard_map/all_to_all | solution.py:446
  148.7 0.9 copy-done.6
  149.7 0.9 copy-done.8
  150.6 2.4 %project_readout.1.own_ref = f32[512,256]{1,0:T(8,128)S(1)} custom-call(bf16[136,2048]{1,0:T(8,128)(2,1)S(1)} %fusion.1.refs_0_.refs_4_, bf16[136,2048]{1,0:T(8,128)(2,1)S(1)} %collective-permute-done.8.refs_1_.refs_5_, bf16[136,2048]{1,0:T(8,128)(2,1)S(1)} %collective-permute-done.9.refs_2_.refs_6_, ...), custom_call_target="tpu_custom_call" | custom-call | flops 536870912 | bytes 3145728 | tf_op jit(solution)/shard_map/project_readout/pallas_call | solution.py:209
  153.0 2.7 %collective-permute-start.12 = (f32[512,256]{1,0:T(8,128)S(1)}, f32[512,256]{1,0:T(8,128)S(1)}, u32[]{:S(2)}, u32[]{:S(2)}) collective-permute-start(f32[512,256]{1,0:T(8,128)S(1)} %project_readout.1.own_ref), channel_id=1, source_target_pairs={{0,1},{1,0},{2,3},{3,2},{4,5},{5,4},{6,7},{7,6},{8,9},{9,8},{10,11... | collective-permute-start | bytes 1572872 | tf_op jit(solution)/shard_map/ppermute | solution.py:432
  155.7 0.1 collective-permute-start.11
  155.8 1.4 collective-permute-done.12.other_ref
  157.3 3.7 %pick_projections.1 = (f32[192,128]{1,0:T(8,128)S(1)}, bf16[1536,128]{1,0:T(8,128)(2,1)S(1)}) custom-call(s32[4]{0:T(128)S(1)} %copy-done.14, f32[512,256]{1,0:T(8,128)S(1)} %project_readout.1.own_ref, f32[512,256]{1,0:T(8,128)S(1)} %collective-permute-done.12.other_ref, bf16[136,2048]{1,0:T(8,128)(2,1)S(1)} %fusion.1.refs_0_.refs_4_, ...), custom_call_target="tpu_custom_call" | custom-call | tf_op jit(solution)/shard_map/pick_projections/pallas_call | solution.py:263
  161.0 1.7 rate_tokens.1
  162.7 0.9 collective-permute-start.14
  163.6 1.8 collective-permute-start.15
  165.4 1.0 collective-permute-done.13.refs_1_
  166.4 0.4 collective-permute-done.14.refs_2_
  166.8 0.5 collective-permute-done.15.refs_3_
  167.3 4.1 %weigh_tokens.1 = (f32[1,128]{1,0:T(1,128)}, bf16[16,16,2176]{2,1,0:T(8,128)(2,1)S(1)}) custom-call(f32[8,128]{1,0:T(8,128)S(1)} %get-tuple-element.49.refs_0_, f32[8,128]{1,0:T(8,128)S(1)} %collective-permute-done.13.refs_1_, f32[8,128]{1,0:T(8,128)S(1)} %collective-permute-done.14.refs_2_, f32[8,128]{1,0:T(8,128)S(1)} %collective-permute-done.15.refs_3_, ...), custom_call_target="tpu_custom_call" | custom-call | tf_op jit(solution)/shard_map/weigh_tokens/pallas_call | solution.py:367
  171.4 19.0 %all_to_all.21.packed_ref = bf16[16,16,2176]{2,1,0:T(8,128)(2,1)S(1)} all-to-all(bf16[16,16,2176]{2,1,0:T(8,128)(2,1)S(1)} %get-tuple-element.52), channel_id=1, replica_groups={{0,8,16,24,32,40,48,56,64,72,80,88,96,104,112,120},{2,10,18,26,34,42,50..., dimensions={0} | all-to-all | bytes 2228224 | tf_op jit(solution)/shard_map/all_to_all | solution.py:446
  190.4 2.8 %adapter_gradients.1 = (f32[16,768]{1,0:T(8,128)}, f32[16,2048]{1,0:T(8,128)S(1)}) custom-call(s32[4]{0:T(128)S(1)} %copy-done.14, bf16[16,16,2176]{2,1,0:T(8,128)(2,1)S(1)} %all_to_all.21.packed_ref, bf16[1024,768]{1,0:T(8,128)(2,1)S(1)} %copy-done.2, bf16[512,768]{1,0:T(8,128)(2,1)S(1)} %copy-done.4), custom_call_target="tpu_custom_call" | custom-call | tf_op jit(solution)/shard_map/adapter_gradients/pallas_call | solution.py:417
  193.1 2.8 %collective-permute-start.16 = (f32[16,2048]{1,0:T(8,128)S(1)}, f32[16,2048]{1,0:T(8,128)S(1)}, u32[]{:S(2)}, u32[]{:S(2)}) collective-permute-start(f32[16,2048]{1,0:T(8,128)S(1)} %get-tuple-element.56), channel_id=1, source_target_pairs={{0,1},{1,0},{2,3},{3,2},{4,5},{5,4},{6,7},{7,6},{8,9},{9,8},{10,11... | collective-permute-start | bytes 393224 | tf_op jit(solution)/shard_map/ppermute | solution.py:432
  195.9 1.0 collective-permute-done.16
  196.9 0.7 maximum_select_fusion
  (46 shorter events, 0.3 us)
Async XLA Ops:
  0.6 81.8 %copy-start = (bf16[128,4096]{1,0:T(8,128)(2,1)S(1)}, bf16[128,4096]{1,0:T(8,128)(2,1)}, u32[]{:S(2)}) copy-start(bf16[128,4096]{1,0:T(8,128)(2,1)} %param.10) | copy-start | bytes 3145732
  1.6 11.4 %collective-permute-start.2 = (bf16[16,2048]{1,0:T(8,128)(2,1)S(1)}, bf16[16,2048]{1,0:T(8,128)(2,1)S(1)}, u32[]{:S(2)}, u32[]{:S(2)}) collective-permute-start(bf16[16,2048]{1,0:T(8,128)(2,1)S(1)} %dynamic-slice_bitcast_fusion), channel_id=1, source_target_pairs={{0,24},{2,26},{4,28},{6,30},{8,0},{10,2},{12,4},{14,6},{16,8},{18,... | collective-permute-start | bytes 196616 | tf_op jit(solution)/shard_map/ppermute | solution.py:442
  4.9 8.0 %collective-permute-start.1 = (bf16[16,2048]{1,0:T(8,128)(2,1)S(1)}, bf16[16,2048]{1,0:T(8,128)(2,1)S(1)}, u32[]{:S(2)}, u32[]{:S(2)}) collective-permute-start(bf16[16,2048]{1,0:T(8,128)(2,1)S(1)} %dynamic-slice_bitcast_fusion), channel_id=1, source_target_pairs={{0,16},{2,18},{4,20},{6,22},{8,24},{10,26},{12,28},{14,30},{16,0},... | collective-permute-start | bytes 196616 | tf_op jit(solution)/shard_map/ppermute | solution.py:442
  5.4 7.5 %collective-permute-start = (bf16[16,2048]{1,0:T(8,128)(2,1)S(1)}, bf16[16,2048]{1,0:T(8,128)(2,1)S(1)}, u32[]{:S(2)}, u32[]{:S(2)}) collective-permute-start(bf16[16,2048]{1,0:T(8,128)(2,1)S(1)} %dynamic-slice_bitcast_fusion), channel_id=1, source_target_pairs={{0,8},{2,10},{4,12},{6,14},{8,16},{10,18},{12,20},{14,22},{16,24},... | collective-permute-start | bytes 196616 | tf_op jit(solution)/shard_map/ppermute | solution.py:442
  72.9 12.4 %collective-permute-start.3 = (bf16[1024,2048]{1,0:T(8,128)(2,1)}, bf16[1024,2048]{1,0:T(8,128)(2,1)}, u32[]{:S(2)}, u32[]{:S(2)}) collective-permute-start(bf16[1024,2048]{1,0:T(8,128)(2,1)} %bitcast.9.own_ref), channel_id=1, source_target_pairs={{0,1},{1,0},{2,3},{3,2},{4,5},{5,4},{6,7},{7,6},{8,9},{9,8},{10,11... | collective-permute-start | bytes 12582920 | tf_op jit(solution)/shard_map/ppermute | solution.py:432
  76.6 5.7 %copy-start.17 = (s32[128]{0:T(128)S(1)}, s32[128]{0:T(128)}, u32[]{:S(2)}) copy-start(s32[128]{0:T(128)} %param.13) | copy-start | bytes 1540
  76.6 5.8 %copy-start.15 = (s32[128,8]{0,1:T(8,128)S(1)}, s32[128,8]{0,1:T(8,128)}, u32[]{:S(2)}) copy-start(s32[128,8]{0,1:T(8,128)} %param.11) | copy-start | bytes 12292
  76.6 5.8 %copy-start.16 = (bf16[128,8]{0,1:T(8,128)(2,1)S(1)}, bf16[128,8]{0,1:T(8,128)(2,1)}, u32[]{:S(2)}) copy-start(bf16[128,8]{0,1:T(8,128)(2,1)} %param.12) | copy-start | bytes 6148
  76.6 39.2 %all-to-all-start = ((bf16[64,8,2048]{2,1,0:T(8,128)(2,1)}), bf16[64,8,2048]{2,1,0:T(8,128)(2,1)}, u32[]{:S(2)}, u32[]{:S(2)}) async-start(bf16[64,8,2048]{2,1,0:T(8,128)(2,1)} %bitcast.19), calls=%async_computation | async-start | bytes 4194304 | tf_op jit(solution)/shard_map/all_to_all | solution.py:446
  82.3 3.0 %copy-start.12 = (bf16[1,16,768]{2,1,0:T(8,128)(2,1)S(1)}, bf16[1,16,768]{2,1,0:T(8,128)(2,1)}, u32[]{:S(2)}) copy-start(bf16[1,16,768]{2,1,0:T(8,128)(2,1)} %a_ref.3) | copy-start | bytes 73732
  82.3 2.9 %copy-start.14 = (s32[4]{0:T(128)S(1)}, s32[4]{0:T(128)}, u32[]{:S(2)}) copy-start(s32[4]{0:T(128)} %pad_add_fusion.core_ref.place_ref) | copy-start | bytes 52
  82.5 31.9 %collective-permute-start.4 = (bf16[64,2048]{1,0:T(8,128)(2,1)S(1)}, bf16[64,2048]{1,0:T(8,128)(2,1)S(1)}, u32[]{:S(2)}, u32[]{:S(2)}) collective-permute-start(bf16[64,2048]{1,0:T(8,128)(2,1)S(1)} %pad_maximum_fusion.refs_4_), channel_id=1, source_target_pairs={{0,32},{2,34},{4,36},{6,38},{8,40},{10,42},{12,44},{14,46},{16,48}... | collective-permute-start | bytes 786440 | tf_op jit(solution)/shard_map/ppermute | solution.py:442
  83.5 31.6 %collective-permute-start.5 = (bf16[64,2048]{1,0:T(8,128)(2,1)S(1)}, bf16[64,2048]{1,0:T(8,128)(2,1)S(1)}, u32[]{:S(2)}, u32[]{:S(2)}) collective-permute-start(bf16[64,2048]{1,0:T(8,128)(2,1)S(1)} %pad_maximum_fusion.refs_4_), channel_id=1, source_target_pairs={{0,96},{2,98},{4,100},{6,102},{8,104},{10,106},{12,108},{14,110},{... | collective-permute-start | bytes 786440 | tf_op jit(solution)/shard_map/ppermute | solution.py:442
  105.8 1.2 copy-start.1
  107.0 0.6 copy-start.10
  114.4 0.7 copy-start.5
  115.1 0.7 copy-start.7
  115.8 4.9 %collective-permute-start.6 = (bf16[512,2048]{1,0:T(8,128)(2,1)}, bf16[512,2048]{1,0:T(8,128)(2,1)S(1)}, u32[]{:S(2)}, u32[]{:S(2)}) collective-permute-start(bf16[512,2048]{1,0:T(8,128)(2,1)} %bitcast.6.own_ref), channel_id=1, source_target_pairs={{0,1},{1,0},{2,3},{3,2},{4,5},{5,4},{6,7},{7,6},{8,9},{9,8},{10,11... | collective-permute-start | bytes 6291464 | tf_op jit(solution)/shard_map/ppermute | solution.py:432
  116.3 25.9 %collective-permute-start.7 = (bf16[64,2048]{1,0:T(8,128)(2,1)S(1)}, bf16[64,2048]{1,0:T(8,128)(2,1)}, u32[]{:S(2)}, u32[]{:S(2)}) collective-permute-start(bf16[64,2048]{1,0:T(8,128)(2,1)S(1)} %pad_maximum_fusion.refs_4_), channel_id=1, source_target_pairs={{0,64},{2,66},{4,68},{6,70},{8,72},{10,74},{12,76},{14,78},{16,80}... | collective-permute-start | bytes 786440 | tf_op jit(solution)/shard_map/ppermute | solution.py:442
  116.3 25.9 %collective-permute-start.8 = (bf16[136,2048]{1,0:T(8,128)(2,1)S(1)}, bf16[136,2048]{1,0:T(8,128)(2,1)S(1)}, u32[]{:S(2)}, u32[]{:S(2)}) collective-permute-start(bf16[136,2048]{1,0:T(8,128)(2,1)S(1)} %fusion.1.refs_0_.refs_4_), channel_id=1, source_target_pairs={{0,2},{2,4},{4,6},{6,0},{8,10},{10,12},{12,14},{14,8},{16,18},{18,... | collective-permute-start | bytes 1671176 | tf_op jit(solution)/shard_map/ppermute | solution.py:442
  117.2 26.8 %collective-permute-start.9 = (bf16[136,2048]{1,0:T(8,128)(2,1)S(1)}, bf16[136,2048]{1,0:T(8,128)(2,1)S(1)}, u32[]{:S(2)}, u32[]{:S(2)}) collective-permute-start(bf16[136,2048]{1,0:T(8,128)(2,1)S(1)} %fusion.1.refs_0_.refs_4_), channel_id=1, source_target_pairs={{0,4},{2,6},{4,0},{6,2},{8,12},{10,14},{12,8},{14,10},{16,20},{18,... | collective-permute-start | bytes 1671176 | tf_op jit(solution)/shard_map/ppermute | solution.py:442
  119.6 24.4 %collective-permute-start.10 = (bf16[136,2048]{1,0:T(8,128)(2,1)S(1)}, bf16[136,2048]{1,0:T(8,128)(2,1)S(1)}, u32[]{:S(2)}, u32[]{:S(2)}) collective-permute-start(bf16[136,2048]{1,0:T(8,128)(2,1)S(1)} %fusion.1.refs_0_.refs_4_), channel_id=1, source_target_pairs={{0,6},{2,0},{4,2},{6,4},{8,14},{10,8},{12,10},{14,12},{16,22},{18,... | collective-permute-start | bytes 1671176 | tf_op jit(solution)/shard_map/ppermute | solution.py:442
  120.7 0.8 copy-start.11
  121.5 0.7 copy-start.13
  133.9 0.9 copy-start.3
  134.8 0.6 copy-start.9
  135.4 13.3 %all-to-all-start.2 = ((bf16[16,16,128]{2,1,0:T(8,128)(2,1)}), bf16[16,16,128]{2,1,0:T(8,128)(2,1)}, u32[]{:S(2)}, u32[]{:S(2)}) async-start(bf16[16,16,128]{2,1,0:T(8,128)(2,1)} %copy-done.9), calls=%async_computation.2 | async-start | bytes 131072 | tf_op jit(solution)/shard_map/all_to_all | solution.py:446
  148.7 1.0 copy-start.6
  149.7 0.9 copy-start.8
  153.0 4.2 %collective-permute-start.12 = (f32[512,256]{1,0:T(8,128)S(1)}, f32[512,256]{1,0:T(8,128)S(1)}, u32[]{:S(2)}, u32[]{:S(2)}) collective-permute-start(f32[512,256]{1,0:T(8,128)S(1)} %project_readout.1.own_ref), channel_id=1, source_target_pairs={{0,1},{1,0},{2,3},{3,2},{4,5},{5,4},{6,7},{7,6},{8,9},{9,8},{10,11... | collective-permute-start | bytes 1572872 | tf_op jit(solution)/shard_map/ppermute | solution.py:432
  155.7 5.2 %collective-permute-start.11 = (bf16[16,16,128]{2,1,0:T(8,128)(2,1)}, bf16[16,16,128]{2,1,0:T(8,128)(2,1)S(1)}, u32[]{:S(2)}, u32[]{:S(2)}) collective-permute-start(bf16[16,16,128]{2,1,0:T(8,128)(2,1)} %all-to-all-done.2.own_ref), channel_id=1, source_target_pairs={{0,1},{1,0},{2,3},{3,2},{4,5},{5,4},{6,7},{7,6},{8,9},{9,8},{10,11... | collective-permute-start | bytes 196616 | tf_op jit(solution)/shard_map/ppermute | solution.py:432
  162.6 3.7 %collective-permute-start.13 = (f32[8,128]{1,0:T(8,128)S(1)}, f32[8,128]{1,0:T(8,128)S(1)}, u32[]{:S(2)}, u32[]{:S(2)}) collective-permute-start(f32[8,128]{1,0:T(8,128)S(1)} %get-tuple-element.49.refs_0_), channel_id=1, source_target_pairs={{0,2},{2,4},{4,6},{6,0},{8,10},{10,12},{12,14},{14,8},{16,18},{18,... | collective-permute-start | bytes 12296 | tf_op jit(solution)/shard_map/ppermute | solution.py:442
  162.7 4.0 %collective-permute-start.14 = (f32[8,128]{1,0:T(8,128)S(1)}, f32[8,128]{1,0:T(8,128)S(1)}, u32[]{:S(2)}, u32[]{:S(2)}) collective-permute-start(f32[8,128]{1,0:T(8,128)S(1)} %get-tuple-element.49.refs_0_), channel_id=1, source_target_pairs={{0,4},{2,6},{4,0},{6,2},{8,12},{10,14},{12,8},{14,10},{16,20},{18,... | collective-permute-start | bytes 12296 | tf_op jit(solution)/shard_map/ppermute | solution.py:442
  163.6 3.7 %collective-permute-start.15 = (f32[8,128]{1,0:T(8,128)S(1)}, f32[8,128]{1,0:T(8,128)S(1)}, u32[]{:S(2)}, u32[]{:S(2)}) collective-permute-start(f32[8,128]{1,0:T(8,128)S(1)} %get-tuple-element.49.refs_0_), channel_id=1, source_target_pairs={{0,6},{2,0},{4,2},{6,4},{8,14},{10,8},{12,10},{14,12},{16,22},{18,... | collective-permute-start | bytes 12296 | tf_op jit(solution)/shard_map/ppermute | solution.py:442
  167.3 23.1 %copy-start.2 = (bf16[1024,768]{1,0:T(8,128)(2,1)S(1)}, bf16[1024,768]{1,0:T(8,128)(2,1)}, u32[]{:S(2)}) copy-start(bf16[1024,768]{1,0:T(8,128)(2,1)} %copy-done.1) | copy-start | bytes 4718596
  167.3 23.1 %copy-start.4 = (bf16[512,768]{1,0:T(8,128)(2,1)S(1)}, bf16[512,768]{1,0:T(8,128)(2,1)}, u32[]{:S(2)}) copy-start(bf16[512,768]{1,0:T(8,128)(2,1)} %copy-done.3) | copy-start | bytes 2359300
  193.1 3.8 %collective-permute-start.16 = (f32[16,2048]{1,0:T(8,128)S(1)}, f32[16,2048]{1,0:T(8,128)S(1)}, u32[]{:S(2)}, u32[]{:S(2)}) collective-permute-start(f32[16,2048]{1,0:T(8,128)S(1)} %get-tuple-element.56), channel_id=1, source_target_pairs={{0,1},{1,0},{2,3},{3,2},{4,5},{5,4},{6,7},{7,6},{8,9},{9,8},{10,11... | collective-permute-start | bytes 393224 | tf_op jit(solution)/shard_map/ppermute | solution.py:432
